TPU v7x, 32 devices: a whole 2x2x4 slice. The times are simulated.
32 devices in a mesh: ens: 2 (over y), tile: 4 (over z), trc: 2 (over x), lev: 2 (over core).
Axes of the slice: x: 2, y: 2, z: 4, core: 2. Of those that a mesh axis runs over, the one named last changes fastest.
Arguments:
- tracers: float32 [32, 16, 64, 128], P('trc', 'lev', ('ens', 'tile')), parts along dimension 2, may hold values from -6 to 6
- cotangent: float32 [32, 16, 64, 128], P('trc', 'lev', ('ens', 'tile')), parts along dimension 2, may hold values from -3 to 3
- zonal_speed: float32 [16, 64, 128], P('lev', ('ens', 'tile')), parts along dimension 1, may hold values from -0.3 to 0.3
- meridional_speed: float32 [16, 64, 128], P('lev', ('ens', 'tile')), parts along dimension 1, may hold values from -0.3 to 0.3
- vertical_speed: float32 [16, 64, 128], P('lev', ('ens', 'tile')), parts along dimension 1, may hold values from -0.3 to 0.3
- lateral_mixing: float32 [16, 64, 128], P('lev', ('ens', 'tile')), parts along dimension 1, may hold values from 0.01 to 0.08
- vertical_mixing: float32 [16, 64, 128], P('lev', ('ens', 'tile')), parts along dimension 1, may hold values from 0.02 to 0.16
- column_depth: int32 [64, 128], P(('ens', 'tile')), parts along dimension 0, may hold values from 0 to 16
Outputs:
- start_cotangent: float32 [32, 16, 64, 128], P('trc', 'lev', ('ens', 'tile')), parts along dimension 2
- speed_cotangent: float32 [3, 16, 64, 128], P(None, ('lev', 'trc'), ('ens', 'tile')), parts along dimension 2
There are 2 independent parts, one for each index of `ens`. A program takes and returns all parts, laid end to end along the dimension named above; each array names one. Nothing has to cross between parts.
All inputs are finite; a program needn't handle non-finite values.
Results may differ from a plain program's by a relative error of at most 0.0003.
Values sent between devices are 32-bit elements; how exact they have to be, the bound alone decides.
No kernel may reach another device: no remote copies, remote signals or barrier semaphores. Data moves between devices by JAX's collectives and lax.ppermute only.
A program may use at most 64 MiB of HBM per device.

v0:
```python
import jax
import jax.numpy as jnp
from jax import lax
from jax.sharding import PartitionSpec as P

albada_floor = 0.01


def padded_2(block, sides, width):
    for axis, dim in sides:
        count = lax.axis_size(axis)
        forward = [(i, i + 1) for i in range(count - 1)]
        backward = [(target, source) for source, target in forward]
        low = lax.ppermute(
            lax.slice_in_dim(block, block.shape[dim] - width, None, axis=dim), axis, forward
        )
        high = lax.ppermute(lax.slice_in_dim(block, 0, width, axis=dim), axis, backward)
        block = jnp.concatenate([low, block, high], axis=dim)
    return block


def albada(lower_step, upper_step):
    return (
        lower_step
        * upper_step
        * (lower_step + upper_step)
        / (lower_step * lower_step + upper_step * upper_step + albada_floor)
    )


def face_flux(far_behind, behind, beyond, far_beyond, velocity, spread, opened):
    rising = behind + 0.5 * albada(behind - far_behind, beyond - behind)
    falling = beyond - 0.5 * albada(beyond - behind, far_beyond - beyond)
    carried = jnp.where(velocity >= 0.0, rising, falling)
    return opened * (velocity * carried - spread * (beyond - behind))


def shift_across(values, offset):
    if offset > 0:
        filler = jnp.zeros(values.shape[:-1] + (offset,), values.dtype)
        return jnp.concatenate([filler, values[..., :-offset]], axis=-1)
    filler = jnp.zeros(values.shape[:-1] + (-offset,), values.dtype)
    return jnp.concatenate([values[..., -offset:], filler], axis=-1)


def window(values, direction, offset):
    leading = values.ndim - 3
    pieces = [slice(None)] * leading
    for spatial in range(2):
        extent = values.shape[leading + spatial] - 4
        if spatial == direction:
            pieces.append(slice(offset, extent + 1 + offset))
        else:
            pieces.append(slice(2, extent + 2))
    pieces.append(slice(None))
    return values[tuple(pieces)]


def advance(padded, fields):
    wetness = fields[5]
    centre = padded[:, 2:-2, 2:-2, :]
    result = centre
    for direction, speed_row, spread_row in ((0, 2, 4), (1, 0, 3)):
        through = face_flux(
            window(padded, direction, 0),
            window(padded, direction, 1),
            window(padded, direction, 2),
            window(padded, direction, 3),
            window(fields[speed_row], direction, 2),
            window(fields[spread_row], direction, 2),
            window(wetness, direction, 1) * window(wetness, direction, 2),
        )
        extent = through.shape[direction + 1]
        result = (
            result
            + lax.slice_in_dim(through, 0, extent - 1, axis=direction + 1)
            - lax.slice_in_dim(through, 1, extent, axis=direction + 1)
        )
    centre_fields = fields[:, 2:-2, 2:-2, :]
    inner_wet = centre_fields[5]
    through = face_flux(
        shift_across(centre, 2),
        shift_across(centre, 1),
        centre,
        shift_across(centre, -1),
        centre_fields[1],
        centre_fields[3],
        shift_across(inner_wet, 1) * inner_wet,
    )
    return result + through - shift_across(through, -1)


def local_step(tracer_part, field_part):
    fields = jnp.pad(field_part, ((0, 0), (1, 1), (1, 1), (0, 0)))
    return advance(tracer_part, fields)


def fold_edges(gathered):
    levels = gathered.shape[1] - 4
    columns = gathered.shape[2] - 4
    beside_all = padded_2(gathered, (("tile", 2), ("lev", 1)), 2)
    owned_part = gathered[:, 2:-2, 2:-2]
    owned_part = owned_part.at[:, 0:2].add(beside_all[:, 0:2, 4 : columns + 4])
    owned_part = owned_part.at[:, levels - 2 : levels].add(
        beside_all[:, levels + 6 : levels + 8, 4 : columns + 4]
    )
    owned_part = owned_part.at[:, :, 0:2].add(beside_all[:, 4 : levels + 4, 0:2])
    owned_part = owned_part.at[:, :, columns - 2 : columns].add(
        beside_all[:, 4 : levels + 4, columns + 6 : columns + 8]
    )
    return owned_part


def fold_back(tracer_cot, speed_cot, tracer_count):
    combined = jnp.concatenate([tracer_cot, jnp.pad(speed_cot, ((0, 0), (1, 1), (1, 1), (0, 0)))])
    owned_part = fold_edges(combined)
    return (owned_part[:tracer_count], owned_part[tracer_count:])


def share_speeds(values):
    return lax.psum_scatter(values, "trc", scatter_dimension=1, tiled=True)


def body(
    tracers,
    cotangent,
    zonal_speed,
    meridional_speed,
    vertical_speed,
    lateral_mixing,
    vertical_mixing,
    column_depth,
):
    tracer_count = tracers.shape[0]
    levels = tracers.shape[1]
    first_level = lax.axis_index("lev") * levels
    wetness = (
        (first_level + jnp.arange(levels, dtype=jnp.int32))[:, None, None] < column_depth[None]
    ).astype(jnp.float32)
    fields = jnp.stack(
        [zonal_speed, meridional_speed, vertical_speed, lateral_mixing, vertical_mixing, wetness]
    )
    deep_fields = padded_2(fields, (("tile", 2), ("lev", 1)), 3)
    deep_tracers = padded_2(tracers, (("tile", 2), ("lev", 1)), 4)
    rim_fields = deep_fields[:, 2:-2, 2:-2]
    early_rims = deep_tracers[:, 2:-2, 2:-2]
    late_rims = advance(deep_tracers, jnp.pad(deep_fields, ((0, 0), (1, 1), (1, 1), (0, 0))))
    speed_rims = rim_fields[0:3]
    other_rims = rim_fields[3:6]

    def rim_stepper(tracer_part, speed_part):
        return local_step(tracer_part, jnp.concatenate([speed_part, other_rims]))

    _, pull_late = jax.vjp(rim_stepper, late_rims, speed_rims)
    late_tracer, late_speed_rims = pull_late(cotangent)
    middle_cot, late_speed = fold_back(late_tracer, late_speed_rims, tracer_count)
    _, pull_early = jax.vjp(rim_stepper, early_rims, speed_rims)
    early_tracer, early_speed_rims = pull_early(middle_cot)
    start_cotangent, early_speed = fold_back(early_tracer, early_speed_rims, tracer_count)
    speed_cotangent = share_speeds(late_speed) + share_speeds(early_speed)
    return (start_cotangent, speed_cotangent)


def solution(mesh):
    return jax.shard_map(
        body,
        mesh=mesh,
        in_specs=(
            P("trc", "lev", ("ens", "tile"), None),
            P("trc", "lev", ("ens", "tile"), None),
            P("lev", ("ens", "tile"), None),
            P("lev", ("ens", "tile"), None),
            P("lev", ("ens", "tile"), None),
            P("lev", ("ens", "tile"), None),
            P("lev", ("ens", "tile"), None),
            P(("ens", "tile"), None),
        ),
        out_specs=(
            P("trc", "lev", ("ens", "tile"), None),
            P(None, ("lev", "trc"), ("ens", "tile"), None),
        ),
        check_vma=False,
    )
```

profile of v0, /device:TPU:0, one launch (start us, length us, event | category | flops | bytes accessed | tf_op | source)
XLA Modules:
  0.0 133.3 jit_solution(10074227495728779570)
XLA Ops:
  7.3 1.4 %fusion.80 = (f32[16,8,4,128]{3,2,1,0:T(4,128)S(1)}, f32[16,8,4,128]{3,2,1,0:T(4,128)S(1)}) fusion(f32[16,8,8,128]{3,2,1,0:T(8,128)} %param.24), kind=kLoop, calls=%fused_computation.355 | loop fusion | bytes 1048576 | tf_op jit(solution)/shard_map/slice | solution.py:17
  8.9 5.0 %collective-permute-start.5 = (f32[16,8,4,128]{3,0,2,1:T(8,128)S(1)}, f32[16,8,4,128]{3,0,2,1:T(8,128)S(1)}, u32[]{:S(2)}, u32[]{:S(2)}) collective-permute-start(f32[16,8,4,128]{3,0,2,1:T(8,128)S(1)} %copy.67), channel_id=1, source_target_pairs={{0,4},{4,8},{8,12},{1,5},{5,9},{9,13},{2,6},{6,10},{10,14},{3,7},{... | collective-permute-start | bytes 786440 | tf_op jit(solution)/shard_map/ppermute | solution.py:14
  15.6 1.4 %collective-permute-start.2 = (f32[6,8,3,128]{3,2,1,0:T(4,128)S(1)}, f32[6,8,3,128]{3,2,1,0:T(4,128)S(1)}, u32[]{:S(2)}, u32[]{:S(2)}) collective-permute-start(f32[6,8,3,128]{3,2,1,0:T(4,128)S(1)} %get-tuple-element.220), channel_id=1, source_target_pairs={{4,0},{8,4},{12,8},{5,1},{9,5},{13,9},{6,2},{10,6},{14,10},{7,3},{... | collective-permute-start | bytes 221192 | tf_op jit(solution)/shard_map/ppermute | solution.py:17
  17.0 5.2 %collective-permute-start.1 = (f32[6,8,3,128]{3,2,1,0:T(4,128)S(1)}, f32[6,8,3,128]{3,2,1,0:T(4,128)S(1)}, u32[]{:S(2)}, u32[]{:S(2)}) collective-permute-start(f32[6,8,3,128]{3,2,1,0:T(4,128)S(1)} %get-tuple-element.219), channel_id=1, source_target_pairs={{0,4},{4,8},{8,12},{1,5},{5,9},{9,13},{2,6},{6,10},{10,14},{3,7},{... | collective-permute-start | bytes 221192 | tf_op jit(solution)/shard_map/ppermute | solution.py:14
  23.8 2.0 %collective-permute-done.2 = f32[6,8,3,128]{3,2,1,0:T(4,128)S(1)} collective-permute-done((f32[6,8,3,128]{3,2,1,0:T(4,128)S(1)}, f32[6,8,3,128]{3,2,1,0:T(4,128)S(1)}, u32[]{:S(2)}, u32[]{:S(2)}) %collective-permute-start.2) | collective-permute-done | bytes 73760 | tf_op jit(solution)/shard_map/ppermute | solution.py:17
  27.1 3.0 %collective-permute-start.3 = (f32[6,3,14,128]{3,2,1,0:T(8,128)S(1)}, f32[6,3,14,128]{3,2,1,0:T(8,128)S(1)}, u32[]{:S(2)}, u32[]{:S(2)}) collective-permute-start(f32[6,3,14,128]{3,2,1,0:T(8,128)S(1)} %get-tuple-element.213), channel_id=1, source_target_pairs={{0,1},{2,3},{4,5},{6,7},{8,9},{10,11},{12,13},{14,15},{16,17},{18,... | collective-permute-start | bytes 387080 | tf_op jit(solution)/shard_map/ppermute | solution.py:14
  32.7 1.3 collective-permute-start.7
  34.0 3.3 %collective-permute-start.6 = (f32[16,4,16,128]{3,0,2,1:T(8,128)S(1)}, f32[16,4,16,128]{3,0,2,1:T(8,128)S(1)}, u32[]{:S(2)}, u32[]{:S(2)}) collective-permute-start(f32[16,4,16,128]{3,0,2,1:T(8,128)S(1)} %get-tuple-element.184), channel_id=1, source_target_pairs={{0,1},{2,3},{4,5},{6,7},{8,9},{10,11},{12,13},{14,15},{16,17},{18,... | collective-permute-start | bytes 1572872 | tf_op jit(solution)/shard_map/ppermute | solution.py:14
  39.3 1.5 %subtract_multiply_fusion.4 = f32[16,12,12,128]{3,0,2,1:T(8,128)S(1)} fusion(f32[16,12,12,127]{3,0,2,1:T(8,128)S(1)} %get-tuple-element.169, f32[16,12,12,126]{3,0,2,1:T(8,128)S(1)} %slice.765, f32[16,12,12,127]{3,0,2,1:T(8,128)S(1)} %get-tuple-element.168, f32[16,16,16,128]{3,0,2,1:T(8,128)S(1)} %pad_maximum_fusion, ...), kind=kLoop, calls=%fused_computation.29 | loop fusion | flops 7962624 | bytes 6100992 | tf_op jit(solution)/shard_map/mul | solution.py:35
  41.2 1.3 subtract_multiply_fusion
  48.4 1.4 %add_add_fusion.10 = (f32[16,9,8,128]{3,0,2,1:T(8,128)S(1)}, f32[16,9,8,128]{3,0,2,1:T(8,128)S(1)}, f32[16,9,8,128]{3,0,2,1:T(8,128)S(1)}, f32[16,9,8,128]{3,0,2,1:T(8,128)S(1)}) fusion(f32[16,9,8,128]{3,0,2,1:T(8,128)S(1)} %get-tuple-element.145, f32[9,8,128]{2,1,0:T(8,128)S(1)} %slice.780, f32[9,8,128]{2,1,0:T(8,128)S(1)} %slice_multiply_fusion.9, ...), kind=kLoop, calls=%fused_computation.122 | loop fusion | flops 10469376 | bytes 6018048 | tf_op jit(solution)/shard_map/transpose(jvp())/add_any | solution.py:32
  51.6 1.4 %add_add_fusion.14 = (f32[16,8,9,128]{3,0,2,1:T(8,128)S(1)}, f32[16,8,9,128]{3,0,2,1:T(8,128)S(1)}, f32[16,8,9,128]{3,0,2,1:T(8,128)S(1)}, f32[16,8,9,128]{3,0,2,1:T(8,128)S(1)}) fusion(f32[16,8,9,128]{3,0,2,1:T(8,128)S(1)} %get-tuple-element.142, f32[8,9,128]{2,1,0:T(8,128)S(1)} %slice.772, f32[8,9,128]{2,1,0:T(8,128)S(1)} %slice_multiply_fusion.4, ...), kind=kLoop, calls=%fused_computation.130 | loop fusion | flops 10469376 | bytes 6018048 | tf_op jit(solution)/shard_map/transpose(jvp())/add_any | solution.py:32
  55.4 1.3 collective-permute-start.9
  56.7 4.6 %collective-permute-start.8 = (f32[19,12,2,128]{3,0,2,1:T(8,128)S(1)}, f32[19,12,2,128]{3,0,2,1:T(8,128)S(1)}, u32[]{:S(2)}, u32[]{:S(2)}) collective-permute-start(f32[19,12,2,128]{3,0,2,1:T(8,128)S(1)} %get-tuple-element.178), channel_id=1, source_target_pairs={{0,4},{4,8},{8,12},{1,5},{5,9},{9,13},{2,6},{6,10},{10,14},{3,7},{... | collective-permute-start | bytes 700424 | tf_op jit(solution)/shard_map/ppermute | solution.py:14
  61.3 5.3 %collective-permute-done.9 = f32[19,12,2,128]{3,0,2,1:T(8,128)S(1)} collective-permute-done((f32[19,12,2,128]{3,0,2,1:T(8,128)S(1)}, f32[19,12,2,128]{3,0,2,1:T(8,128)S(1)}, u32[]{:S(2)}, u32[]{:S(2)}) %collective-permute-start.9) | collective-permute-done | bytes 233504 | tf_op jit(solution)/shard_map/ppermute | solution.py:17
  67.8 1.3 collective-permute-start.10
  70.5 2.2 %collective-permute-done.11 = f32[19,2,16,128]{3,0,2,1:T(8,128)S(1)} collective-permute-done((f32[19,2,16,128]{3,0,2,1:T(8,128)S(1)}, f32[19,2,16,128]{3,0,2,1:T(8,128)S(1)}, u32[]{:S(2)}, u32[]{:S(2)}) %collective-permute-start.11) | collective-permute-done | bytes 311328 | tf_op jit(solution)/shard_map/ppermute | solution.py:17
  78.9 1.4 %add_add_fusion.6 = (f32[16,8,9,128]{3,0,2,1:T(8,128)S(1)}, f32[16,8,9,128]{3,0,2,1:T(8,128)S(1)}, f32[16,8,9,128]{3,0,2,1:T(8,128)S(1)}, f32[16,8,9,128]{3,0,2,1:T(8,128)S(1)}) fusion(f32[16,8,9,128]{3,0,2,1:T(8,128)S(1)} %get-tuple-element.121, f32[8,9,128]{2,1,0:T(8,128)S(1)} %slice.772, f32[8,9,128]{2,1,0:T(8,128)S(1)} %slice_multiply_fusion.4, ...), kind=kLoop, calls=%fused_computation.106 | loop fusion | flops 10469376 | bytes 6018048 | tf_op jit(solution)/shard_map/transpose(jvp())/add_any | solution.py:32
  83.9 5.0 %collective-permute-start.12 = (f32[19,12,2,128]{3,0,2,1:T(8,128)S(1)}, f32[19,12,2,128]{3,0,2,1:T(8,128)S(1)}, u32[]{:S(2)}, u32[]{:S(2)}) collective-permute-start(f32[19,12,2,128]{3,0,2,1:T(8,128)S(1)} %get-tuple-element.176), channel_id=1, source_target_pairs={{0,4},{4,8},{8,12},{1,5},{5,9},{9,13},{2,6},{6,10},{10,14},{3,7},{... | collective-permute-start | bytes 700424 | tf_op jit(solution)/shard_map/ppermute | solution.py:14
  89.0 5.4 %collective-permute-done.13 = f32[19,12,2,128]{3,0,2,1:T(8,128)S(1)} collective-permute-done((f32[19,12,2,128]{3,0,2,1:T(8,128)S(1)}, f32[19,12,2,128]{3,0,2,1:T(8,128)S(1)}, u32[]{:S(2)}, u32[]{:S(2)}) %collective-permute-start.13) | collective-permute-done | bytes 233504 | tf_op jit(solution)/shard_map/ppermute | solution.py:17
  95.6 1.3 collective-permute-start.14
  98.3 2.2 %collective-permute-done.15 = f32[19,2,16,128]{3,0,2,1:T(8,128)S(1)} collective-permute-done((f32[19,2,16,128]{3,0,2,1:T(8,128)S(1)}, f32[19,2,16,128]{3,0,2,1:T(8,128)S(1)}, u32[]{:S(2)}, u32[]{:S(2)}) %collective-permute-start.15) | collective-permute-done | bytes 311328 | tf_op jit(solution)/shard_map/ppermute | solution.py:17
  103.6 21.4 %all-reduce.89.cloned.1.call-done = f32[3,8,8,128]{3,2,1,0:T(8,128)} async-done(((f32[3,8,8,128]{3,2,1,0:T(8,128)}), f32[3,8,8,128]{3,2,1,0:T(8,128)}) %all-reduce.89.cloned.1.call-update) | async-done | bytes 98320
  125.0 1.4 %constant_dynamic-slice_fusion = f32[3,4,8,128]{3,2,1,0:T(8,128)} fusion(f32[3,8,8,128]{3,2,1,0:T(8,128)} %all-reduce.89.cloned.1.call-done, u32[]{:T(128)S(6)} %multiply.25), kind=kLoop, calls=%fused_computation.346 | loop fusion | bytes 98308
  (161 shorter events, 36.4 us)
Async XLA Ops:
  7.2 15.0 %copy-start = (f32[16,8,8,128]{3,2,1,0:T(8,128)S(1)}, f32[16,8,8,128]{3,2,1,0:T(8,128)}, u32[]{:S(2)}) copy-start(f32[16,8,8,128]{3,2,1,0:T(8,128)} %param.24) | copy-start | bytes 1572868
  7.2 8.1 %copy-start.5 = (f32[8,8,128]{2,1,0:T(8,128)S(1)}, f32[8,8,128]{2,1,0:T(8,128)}, u32[]{:S(2)}) copy-start(f32[8,8,128]{2,1,0:T(8,128)} %param.26) | copy-start | bytes 98308
  7.2 8.2 %copy-start.2 = (f32[8,8,128]{2,1,0:T(8,128)S(1)}, f32[8,8,128]{2,1,0:T(8,128)}, u32[]{:S(2)}) copy-start(f32[8,8,128]{2,1,0:T(8,128)} %param.27) | copy-start | bytes 98308
  7.2 8.2 %copy-start.6 = (f32[8,8,128]{2,1,0:T(8,128)S(1)}, f32[8,8,128]{2,1,0:T(8,128)}, u32[]{:S(2)}) copy-start(f32[8,8,128]{2,1,0:T(8,128)} %param.28) | copy-start | bytes 98308
  7.2 8.2 %copy-start.3 = (f32[8,8,128]{2,1,0:T(8,128)S(1)}, f32[8,8,128]{2,1,0:T(8,128)}, u32[]{:S(2)}) copy-start(f32[8,8,128]{2,1,0:T(8,128)} %param.29) | copy-start | bytes 98308
  7.2 8.2 %copy-start.7 = (f32[8,8,128]{2,1,0:T(8,128)S(1)}, f32[8,8,128]{2,1,0:T(8,128)}, u32[]{:S(2)}) copy-start(f32[8,8,128]{2,1,0:T(8,128)} %param.30) | copy-start | bytes 98308
  7.2 8.2 %copy-start.4 = (s32[8,128]{1,0:T(8,128)S(1)}, s32[8,128]{1,0:T(8,128)}, u32[]{:S(2)}) copy-start(s32[8,128]{1,0:T(8,128)} %param.31) | copy-start | bytes 12292
  7.2 117.8 %all-reduce.89.cloned.1.call-start = ((), (), s32[]{:S(2)}) async-start(), calls=%async_computation | async-start | bytes 196608
  8.9 22.9 %collective-permute-start.5 = (f32[16,8,4,128]{3,0,2,1:T(8,128)S(1)}, f32[16,8,4,128]{3,0,2,1:T(8,128)S(1)}, u32[]{:S(2)}, u32[]{:S(2)}) collective-permute-start(f32[16,8,4,128]{3,0,2,1:T(8,128)S(1)} %copy.67), channel_id=1, source_target_pairs={{0,4},{4,8},{8,12},{1,5},{5,9},{9,13},{2,6},{6,10},{10,14},{3,7},{... | collective-permute-start | bytes 786440 | tf_op jit(solution)/shard_map/ppermute | solution.py:14
  14.0 18.5 %collective-permute-start = (f32[16,8,4,128]{3,0,2,1:T(8,128)S(1)}, f32[16,8,4,128]{3,0,2,1:T(8,128)S(1)}, u32[]{:S(2)}, u32[]{:S(2)}) collective-permute-start(f32[16,8,4,128]{3,0,2,1:T(8,128)S(1)} %copy.68), channel_id=1, source_target_pairs={{4,0},{8,4},{12,8},{5,1},{9,5},{13,9},{6,2},{10,6},{14,10},{7,3},{... | collective-permute-start | bytes 786440 | tf_op jit(solution)/shard_map/ppermute | solution.py:17
  15.6 10.2 %collective-permute-start.2 = (f32[6,8,3,128]{3,2,1,0:T(4,128)S(1)}, f32[6,8,3,128]{3,2,1,0:T(4,128)S(1)}, u32[]{:S(2)}, u32[]{:S(2)}) collective-permute-start(f32[6,8,3,128]{3,2,1,0:T(4,128)S(1)} %get-tuple-element.220), channel_id=1, source_target_pairs={{4,0},{8,4},{12,8},{5,1},{9,5},{13,9},{6,2},{10,6},{14,10},{7,3},{... | collective-permute-start | bytes 221192 | tf_op jit(solution)/shard_map/ppermute | solution.py:17
  17.0 8.8 %collective-permute-start.1 = (f32[6,8,3,128]{3,2,1,0:T(4,128)S(1)}, f32[6,8,3,128]{3,2,1,0:T(4,128)S(1)}, u32[]{:S(2)}, u32[]{:S(2)}) collective-permute-start(f32[6,8,3,128]{3,2,1,0:T(4,128)S(1)} %get-tuple-element.219), channel_id=1, source_target_pairs={{0,4},{4,8},{8,12},{1,5},{5,9},{9,13},{2,6},{6,10},{10,14},{3,7},{... | collective-permute-start | bytes 221192 | tf_op jit(solution)/shard_map/ppermute | solution.py:14
  25.8 4.4 %collective-permute-start.4 = (f32[6,3,14,128]{3,2,1,0:T(8,128)S(1)}, f32[6,3,14,128]{3,2,1,0:T(8,128)S(1)}, u32[]{:S(2)}, u32[]{:S(2)}) collective-permute-start(f32[6,3,14,128]{3,2,1,0:T(8,128)S(1)} %get-tuple-element.214), channel_id=1, source_target_pairs={{1,0},{3,2},{5,4},{7,6},{9,8},{11,10},{13,12},{15,14},{17,16},{19,... | collective-permute-start | bytes 387080 | tf_op jit(solution)/shard_map/ppermute | solution.py:17
  27.1 4.0 %collective-permute-start.3 = (f32[6,3,14,128]{3,2,1,0:T(8,128)S(1)}, f32[6,3,14,128]{3,2,1,0:T(8,128)S(1)}, u32[]{:S(2)}, u32[]{:S(2)}) collective-permute-start(f32[6,3,14,128]{3,2,1,0:T(8,128)S(1)} %get-tuple-element.213), channel_id=1, source_target_pairs={{0,1},{2,3},{4,5},{6,7},{8,9},{10,11},{12,13},{14,15},{16,17},{18,... | collective-permute-start | bytes 387080 | tf_op jit(solution)/shard_map/ppermute | solution.py:14
  32.7 4.8 %collective-permute-start.7 = (f32[16,4,16,128]{3,0,2,1:T(8,128)S(1)}, f32[16,4,16,128]{3,0,2,1:T(8,128)S(1)}, u32[]{:S(2)}, u32[]{:S(2)}) collective-permute-start(f32[16,4,16,128]{3,0,2,1:T(8,128)S(1)} %get-tuple-element.185), channel_id=1, source_target_pairs={{1,0},{3,2},{5,4},{7,6},{9,8},{11,10},{13,12},{15,14},{17,16},{19,... | collective-permute-start | bytes 1572872 | tf_op jit(solution)/shard_map/ppermute | solution.py:17
  34.0 4.6 %collective-permute-start.6 = (f32[16,4,16,128]{3,0,2,1:T(8,128)S(1)}, f32[16,4,16,128]{3,0,2,1:T(8,128)S(1)}, u32[]{:S(2)}, u32[]{:S(2)}) collective-permute-start(f32[16,4,16,128]{3,0,2,1:T(8,128)S(1)} %get-tuple-element.184), channel_id=1, source_target_pairs={{0,1},{2,3},{4,5},{6,7},{8,9},{10,11},{12,13},{14,15},{16,17},{18,... | collective-permute-start | bytes 1572872 | tf_op jit(solution)/shard_map/ppermute | solution.py:14
  55.4 11.2 %collective-permute-start.9 = (f32[19,12,2,128]{3,0,2,1:T(8,128)S(1)}, f32[19,12,2,128]{3,0,2,1:T(8,128)S(1)}, u32[]{:S(2)}, u32[]{:S(2)}) collective-permute-start(f32[19,12,2,128]{3,0,2,1:T(8,128)S(1)} %get-tuple-element.179), channel_id=1, source_target_pairs={{4,0},{8,4},{12,8},{5,1},{9,5},{13,9},{6,2},{10,6},{14,10},{7,3},{... | collective-permute-start | bytes 700424 | tf_op jit(solution)/shard_map/ppermute | solution.py:17
  56.7 11.1 %collective-permute-start.8 = (f32[19,12,2,128]{3,0,2,1:T(8,128)S(1)}, f32[19,12,2,128]{3,0,2,1:T(8,128)S(1)}, u32[]{:S(2)}, u32[]{:S(2)}) collective-permute-start(f32[19,12,2,128]{3,0,2,1:T(8,128)S(1)} %get-tuple-element.178), channel_id=1, source_target_pairs={{0,4},{4,8},{8,12},{1,5},{5,9},{9,13},{2,6},{6,10},{10,14},{3,7},{... | collective-permute-start | bytes 700424 | tf_op jit(solution)/shard_map/ppermute | solution.py:14
  67.8 2.7 %collective-permute-start.10 = (f32[19,2,16,128]{3,0,2,1:T(8,128)S(1)}, f32[19,2,16,128]{3,0,2,1:T(8,128)S(1)}, u32[]{:S(2)}, u32[]{:S(2)}) collective-permute-start(f32[19,2,16,128]{3,0,2,1:T(8,128)S(1)} %get-tuple-element.173), channel_id=1, source_target_pairs={{0,1},{2,3},{4,5},{6,7},{8,9},{10,11},{12,13},{14,15},{16,17},{18,... | collective-permute-start | bytes 933896 | tf_op jit(solution)/shard_map/ppermute | solution.py:14
  69.1 3.6 %collective-permute-start.11 = (f32[19,2,16,128]{3,0,2,1:T(8,128)S(1)}, f32[19,2,16,128]{3,0,2,1:T(8,128)S(1)}, u32[]{:S(2)}, u32[]{:S(2)}) collective-permute-start(f32[19,2,16,128]{3,0,2,1:T(8,128)S(1)} %get-tuple-element.172), channel_id=1, source_target_pairs={{1,0},{3,2},{5,4},{7,6},{9,8},{11,10},{13,12},{15,14},{17,16},{19,... | collective-permute-start | bytes 933896 | tf_op jit(solution)/shard_map/ppermute | solution.py:17
  82.6 11.7 %collective-permute-start.13 = (f32[19,12,2,128]{3,0,2,1:T(8,128)S(1)}, f32[19,12,2,128]{3,0,2,1:T(8,128)S(1)}, u32[]{:S(2)}, u32[]{:S(2)}) collective-permute-start(f32[19,12,2,128]{3,0,2,1:T(8,128)S(1)} %get-tuple-element.177), channel_id=1, source_target_pairs={{4,0},{8,4},{12,8},{5,1},{9,5},{13,9},{6,2},{10,6},{14,10},{7,3},{... | collective-permute-start | bytes 700424 | tf_op jit(solution)/shard_map/ppermute | solution.py:17
  83.9 11.6 %collective-permute-start.12 = (f32[19,12,2,128]{3,0,2,1:T(8,128)S(1)}, f32[19,12,2,128]{3,0,2,1:T(8,128)S(1)}, u32[]{:S(2)}, u32[]{:S(2)}) collective-permute-start(f32[19,12,2,128]{3,0,2,1:T(8,128)S(1)} %get-tuple-element.176), channel_id=1, source_target_pairs={{0,4},{4,8},{8,12},{1,5},{5,9},{9,13},{2,6},{6,10},{10,14},{3,7},{... | collective-permute-start | bytes 700424 | tf_op jit(solution)/shard_map/ppermute | solution.py:14
  95.6 2.7 %collective-permute-start.14 = (f32[19,2,16,128]{3,0,2,1:T(8,128)S(1)}, f32[19,2,16,128]{3,0,2,1:T(8,128)S(1)}, u32[]{:S(2)}, u32[]{:S(2)}) collective-permute-start(f32[19,2,16,128]{3,0,2,1:T(8,128)S(1)} %get-tuple-element.171), channel_id=1, source_target_pairs={{0,1},{2,3},{4,5},{6,7},{8,9},{10,11},{12,13},{14,15},{16,17},{18,... | collective-permute-start | bytes 933896 | tf_op jit(solution)/shard_map/ppermute | solution.py:14
  96.9 3.6 %collective-permute-start.15 = (f32[19,2,16,128]{3,0,2,1:T(8,128)S(1)}, f32[19,2,16,128]{3,0,2,1:T(8,128)S(1)}, u32[]{:S(2)}, u32[]{:S(2)}) collective-permute-start(f32[19,2,16,128]{3,0,2,1:T(8,128)S(1)} %get-tuple-element.170), channel_id=1, source_target_pairs={{1,0},{3,2},{5,4},{7,6},{9,8},{11,10},{13,12},{15,14},{17,16},{19,... | collective-permute-start | bytes 933896 | tf_op jit(solution)/shard_map/ppermute | solution.py:17
  (2 other events, 10.0 us)
Sparse Core Ops, SparseCore 0:
  101.5 23.4 all-reduce.88
where the time goes:
time: 134 us; the launch traced here: 133 us
  waiting for transfers between devices  42.8 us (32%)
  starting transfers between devices  39.2 us (29%)
  other arithmetic  26.9 us (20%)
  between operations  15.8 us (12%)
  local copies, waits for them, and re-layouts  8.55 us (6%)
    ppermute x8, starting transfers between devices, padded_2(): lax.ppermute(lax.slice_in_dim(block, block.shape[dim] - width, None, axis...  28.7 us
    unnamed x2, waiting for transfers between devices  21.4 us
    ppermute x8, waiting for transfers between devices, padded_2(): lax.ppermute(lax.slice_in_dim(block, 0, width, axis=dim), axis, backward)  17 us
    ppermute x8, starting transfers between devices, padded_2(): lax.ppermute(lax.slice_in_dim(block, 0, width, axis=dim), axis, backward)  10.5 us
    add_any x7, other arithmetic, face_flux(): rising = behind + 0.5 * albada(behind - far_behind, beyond - behind)  7.63 us
    unnamed x34, local copies, waits for them, and re-layouts  4.53 us
    ppermute x8, waiting for transfers between devices, padded_2(): lax.ppermute(lax.slice_in_dim(block, block.shape[dim] - width, None, axis...  4.34 us
    mul x3, other arithmetic, face_flux(): return opened * (velocity * carried - spread * (beyond - behind))  3.73 us
  transfers between devices with their start and end apart: 17, of which 10 were waited for; matrix products, arithmetic and copies ran while one was open for 4% of the time, Pallas kernels for 0%

commit v1 on v0

v1 whole, which is shorter than its diff:
```python
import functools

import jax
import jax.numpy as jnp
from jax import lax
from jax.experimental import pallas as pl
from jax.experimental.pallas import tpu as pltpu
from jax.sharding import PartitionSpec as P

albada_floor = 0.01
H = 4
E = 2
W = 3
NF = 5
FPAD = 16


def pairings(count):
    phases = []
    for first in (0, 1):
        pairs = []
        for i in range(first, count - 1, 2):
            pairs += [(i, i + 1), (i + 1, i)]
        if pairs:
            phases.append(pairs)
    return phases


def by_parity(even, phase, act):
    @pl.when(even)
    def _():
        act(phase == 0)

    @pl.when(jnp.logical_not(even))
    def _():
        act(phase == 1)


def pack_body(dims, n_tile, n_lev, idx_ref, q_ref, l_ref, *refs):
    T, L, C, Y = dims
    f_refs, depth_ref = refs[:NF], refs[NF]
    tile_out = refs[NF + 1 : NF + 1 + n_tile]
    lev_out = refs[NF + 1 + n_tile :]
    tile_even = idx_ref[0] == 0
    lev_even = idx_ref[1] == 0

    def slab(ref, k, c):
        return ref[pl.ds(k * C + c, T, stride=L * C), :]

    for phase, out in enumerate(tile_out):

        def send_tile(high, out=out):
            q0 = C - H if high else 0
            l0 = C - E if high else 0
            f0 = C - W if high else 0

            def level(k, carry):
                for j in range(H):
                    out[k, j * T : (j + 1) * T, :] = slab(q_ref, k, q0 + j)
                for j in range(E):
                    out[k, (H + j) * T : (H + j + 1) * T, :] = slab(l_ref, k, l0 + j)
                base = (H + E) * T
                for f in range(NF):
                    out[k, base + W * f : base + W * (f + 1), :] = f_refs[f][k, f0 : f0 + W, :]
                out[k, base + W * NF : base + W * NF + 1, :] = depth_ref[f0 : f0 + 1, :].astype(jnp.float32)
                return carry

            lax.fori_loop(0, L, level, 0)
            base = (H + E) * T + W * NF
            for j in range(1, W):
                out[j, base : base + 1, :] = depth_ref[f0 + j : f0 + j + 1, :].astype(jnp.float32)

        by_parity(tile_even, phase, send_tile)

    for phase, out in enumerate(lev_out):

        def send_lev(high, out=out):
            def column(c, carry):
                for j in range(H):
                    k = (L - H if high else 0) + j
                    out[j, pl.ds(pl.multiple_of(c * T, 8), T), :] = slab(q_ref, k, c)
                for j in range(E):
                    k = (L - E if high else 0) + j
                    out[H + j, pl.ds(pl.multiple_of(c * T, 8), T), :] = slab(l_ref, k, c)
                return carry

            lax.fori_loop(0, C, column, 0)
            for j in range(W):
                k = (L - W if high else 0) + j
                for f in range(NF):
                    out[H + E, (j * NF + f) * C : (j * NF + f + 1) * C, :] = f_refs[f][k]

        by_parity(lev_even, phase, send_lev)


def limiter(x, y, xx, yy):
    s = x * y
    r = 1.0 / (xx + yy + albada_floor)
    a = s * (x + y) * r
    return s, r, a


def forward_chain(n, get_u, get_co, emit):
    u_a, u_b = get_u(-2), get_u(-1)
    d_b = u_b - u_a
    xx_b = d_b * d_b
    half_b = None
    flux_b = None
    for f in range(0, n + 2):
        u_c = get_u(f)
        d_c = u_c - u_b
        xx_c = d_c * d_c
        _, _, a = limiter(d_b, d_c, xx_b, xx_c)
        half_c = 0.5 * a
        if f >= 1:
            v, m = get_co(f - 1)
            carried = jnp.where(v >= 0.0, u_a + half_b, u_b - half_c)
            flux = v * carried - m * d_b
            if f >= 2:
                emit(f - 2, flux_b - flux)
            flux_b = flux
        u_a, u_b, d_b, xx_b, half_b = u_b, u_c, d_c, xx_c, half_c


def adjoint_chain(n, get_u, get_l, get_co, emit, emit_speed):
    u_a, u_b = get_u(-2), get_u(-1)
    l_a, l_b = get_l(-2), get_l(-1)
    d_b = u_b - u_a
    xx_b = d_b * d_b
    hh_b = 0.5 * xx_b
    g_b = l_b - l_a
    v, m = get_co(-1)
    v_b = v
    n_b = jnp.minimum(v, 0.0) * g_b
    p_b = dm_b = None
    half_b = None
    down_a = None
    dd_a = None
    n_a = None
    for f in range(0, n + 2):
        u_c, l_c = get_u(f), get_l(f)
        d_c = u_c - u_b
        xx_c = d_c * d_c
        hh_c = 0.5 * xx_c
        g_c = l_c - l_b
        v_c, m_c = get_co(f)
        p_c = jnp.maximum(v_c, 0.0) * g_c
        n_c = jnp.minimum(v_c, 0.0) * g_c
        s, r, a = limiter(d_b, d_c, xx_b, xx_c)
        half_c = 0.5 * a
        er = (p_c - n_b) * r
        if f >= 1:
            x_c = er * (hh_c + s - d_b * a)
            dd_b = x_c + down_a - dm_b
            if f >= 2:
                emit(f - 2, n_a + p_b + dd_a - dd_b)
            if f - 1 < n:
                carried = jnp.where(v_b >= 0.0, u_a + half_b, u_b - half_c)
                emit_speed(f - 1, g_b * carried)
            dd_a = dd_b
        down_a = er * (hh_b + s - d_c * a)
        n_a = n_b
        p_b, n_b, v_b = p_c, n_c, v_c
        dm_b = m_c * g_c
        g_b = g_c
        half_b = half_c
        u_a, u_b, l_b, d_b, xx_b, hh_b = u_b, u_c, l_c, d_c, xx_c, hh_c


def lanes(T, Y):
    lane = lax.broadcasted_iota(jnp.int32, (T, Y), 1)
    return lane == 0, lane == Y - 1


def along_forward(u, v, m, first, last, Y):
    before = jnp.where(first, 0.0, pltpu.roll(u, 1, 1))
    d = u - before
    nxt = jnp.where(last, -u, pltpu.roll(d, Y - 1, 1))
    _, _, a = limiter(d, nxt, d * d, nxt * nxt)
    half = 0.5 * a
    carried = jnp.where(v >= 0.0, before + pltpu.roll(half, 1, 1), u - half)
    flux = v * carried - m * d
    return flux - pltpu.roll(flux, Y - 1, 1)


def along_adjoint(u, l, v, m, first, last, Y):
    before = jnp.where(first, 0.0, pltpu.roll(u, 1, 1))
    d = u - before
    nxt = jnp.where(last, -u, pltpu.roll(d, Y - 1, 1))
    xx, yy = d * d, nxt * nxt
    s, r, a = limiter(d, nxt, xx, yy)
    half = 0.5 * a
    g = l - pltpu.roll(l, 1, 1)
    p = jnp.maximum(v, 0.0) * g
    n = jnp.minimum(v, 0.0) * g
    er = (pltpu.roll(p, Y - 1, 1) - n) * r
    z = er * (0.5 * yy + s - d * a) - m * g
    down = er * (0.5 * xx + s - nxt * a)
    carried = jnp.where(v >= 0.0, before + pltpu.roll(half, 1, 1), u - half)
    add = (
        (n + z - down)
        + jnp.where(first, 0.0, pltpu.roll(down, 1, 1))
        + jnp.where(last, 0.0, pltpu.roll(p - z, Y - 1, 1))
    )
    return add, g * carried


class Fields:
    def __init__(self, f_ref, d_ref, level0):
        self.f, self.d, self.level0 = f_ref, d_ref, level0

    def at(self, direction, k, c):
        depth = self.d[direction, W + c]
        level = (self.level0 + k).astype(jnp.float32)
        if direction == 2:
            level = jnp.where(level >= 1.0, level, 1e9)
        is_open = depth > level
        speed = self.f[(0, 1, 2)[direction], W + k, W + c]
        mix = self.f[(3, 3, 4)[direction], W + k, W + c]
        return jnp.where(is_open, speed, 0.0), jnp.where(is_open, mix, 0.0), is_open


def adjoint(dims, fields, u_ref, u_off, l_ref, acc_ref, done, speed_ref):
    T, L, C, Y = dims
    first, last = lanes(T, Y)
    uo = u_off

    def store_speed(direction, k, c, is_open, value):
        row = jnp.sum(value, axis=0, keepdims=True)
        speed_ref[direction, k, pl.ds(c, 1), :] = jnp.where(is_open, row, 0.0)

    def level(k, carry):
        for c in range(C):
            l = l_ref[E + k, E + c]
            v, m, is_open = fields.at(1, k, c)
            add, sp = along_adjoint(u_ref[uo + k, uo + c], l, v, m, first, last, Y)
            acc_ref[k, c] = l + add
            store_speed(1, k, c, is_open, sp)
        return carry

    lax.fori_loop(0, L, level, 0)

    def level_z(k, carry):
        opened = {}

        def co(c):
            v, m, opened[c] = fields.at(0, k, c)
            return v, m

        def emit(c, value):
            acc_ref[k, c] = acc_ref[k, c] + value

        adjoint_chain(
            C,
            lambda c: u_ref[uo + k, uo + c],
            lambda c: l_ref[E + k, E + c],
            co,
            emit,
            lambda c, value: store_speed(0, k, c, opened[c], value),
        )
        return carry

    lax.fori_loop(0, L, level_z, 0)

    def column_v(c, carry):
        opened = {}

        def co(k):
            v, m, opened[k] = fields.at(2, k, c)
            return v, m

        def emit(k, value):
            done(k, c, acc_ref[k, c] + value)

        adjoint_chain(
            L,
            lambda k: u_ref[uo + k, uo + c],
            lambda k: l_ref[E + k, E + c],
            co,
            emit,
            lambda k, value: store_speed(2, k, c, opened[k], value),
        )
        return carry

    lax.fori_loop(0, C, column_v, 0)


def middle_body(dims, n_tile, n_lev, idx_ref, q_ref, l_ref, *refs):
    T, L, C, Y = dims
    f_refs, depth_ref = refs[:NF], refs[NF]
    at = NF + 1
    tile_in = refs[at : at + n_tile]
    lev_in = refs[at + n_tile : at + n_tile + n_lev]
    corner_in = refs[at + n_tile + n_lev : at + n_tile + 2 * n_lev]
    at += n_tile + 2 * n_lev
    qe, fe, de, mc_ref, sp_ref = refs[at : at + 5]
    at += 5
    tile_out = refs[at : at + n_tile]
    lev_out = refs[at + n_tile : at + n_tile + n_lev]
    le, me = refs[at + n_tile + n_lev :]
    tile_even = idx_ref[0] == 0
    lev_even = idx_ref[1] == 0
    level0 = idx_ref[2]

    def own_level(k, carry):
        for c in range(C):
            qe[H + k, H + c] = q_ref[pl.ds(k * C + c, T, stride=L * C), :]
            le[E + k, E + c] = l_ref[pl.ds(k * C + c, T, stride=L * C), :]
            for f in range(NF):
                fe[f, W + k, W + c] = f_refs[f][k, c : c + 1, :]
        return carry

    lax.fori_loop(0, L, own_level, 0)
    depths = {}
    for c in range(C):
        depths[c] = depth_ref[c : c + 1, :].astype(jnp.float32)
        de[2, W + c] = depths[c]

    zero = jnp.zeros((T, Y), jnp.float32)
    zero_row = jnp.zeros((1, Y), jnp.float32)

    def place_tile(source, high):
        q0 = H + C if high else 0
        l0 = E + C if high else 0
        f0 = W + C if high else 0

        def level(k, carry):
            for j in range(H):
                qe[H + k, q0 + j] = zero if source is None else source[k, j * T : (j + 1) * T, :]
            for j in range(E):
                le[E + k, l0 + j] = zero if source is None else source[k, (H + j) * T : (H + j + 1) * T, :]
            base = (H + E) * T
            for f in range(NF):
                for j in range(W):
                    r = base + W * f + j
                    fe[f, W + k, f0 + j] = zero_row if source is None else source[k, r : r + 1, :]
            return carry

        lax.fori_loop(0, L, level, 0)
        base = (H + E) * T + W * NF
        for j in range(W):
            de[2, f0 + j] = zero_row if source is None else source[j, base : base + 1, :]

    def place_lev(source, high):
        q0 = H + L if high else 0
        l0 = E + L if high else 0
        f0 = W + L if high else 0

        def column(c, carry):
            rows = pl.ds(pl.multiple_of(c * T, 8), T)
            for j in range(H):
                qe[q0 + j, H + c] = zero if source is None else source[j, rows, :]
            for j in range(E):
                le[l0 + j, E + c] = zero if source is None else source[H + j, rows, :]
            return carry

        lax.fori_loop(0, C, column, 0)
        for j in range(W):
            for f in range(NF):
                for c in range(C):
                    r = (j * NF + f) * C + c
                    fe[f, f0 + j, W + c] = zero_row if source is None else source[H + E, r : r + 1, :]

    def place_corner(source, tile_high, lev_high):
        for j in range(E):
            q_lev = H + L + j if lev_high else H - E + j
            f_lev = W + L + j if lev_high else W - E + j
            for i in range(E):
                if source is None:
                    qe[q_lev, (H + C + i) if tile_high else (H - E + i)] = zero
                else:
                    s = i if tile_high else H - E + i
                    qe[q_lev, (H + C + i) if tile_high else (H - E + i)] = source[j, s * T : (s + 1) * T, :]
                for f in range(NF):
                    col = (W + C + i) if tile_high else (W - E + i)
                    if source is None:
                        fe[f, f_lev, col] = zero_row
                    else:
                        r = (H + E) * T + W * f + (i if tile_high else W - E + i)
                        fe[f, f_lev, col] = source[j, r : r + 1, :]

    def zero_corners(lev_high):
        for tile_high in (False, True):
            place_corner(None, tile_high, lev_high)

    for phase in range(2):
        by_parity(
            tile_even, phase, lambda high, p=phase: place_tile(tile_in[p] if p < n_tile else None, high)
        )
        by_parity(lev_even, phase, lambda high, p=phase: place_lev(lev_in[p] if p < n_lev else None, high))
        if phase >= n_lev:
            by_parity(lev_even, phase, zero_corners)
        else:
            for other in range(2):

                def corner(lev_high, p=phase, t=other):
                    source = corner_in[p].at[t] if t < n_tile else None
                    by_parity(tile_even, t, lambda tile_high: place_corner(source, tile_high, lev_high))

                by_parity(lev_even, phase, corner)

    lane0 = lax.broadcasted_iota(jnp.int32, (1, Y), 1) == 0
    de[0, 0] = zero_row
    de[1, 0] = zero_row
    for c in range(1, C + 2 * W):
        here = de[2, c]
        de[0, c] = jnp.minimum(de[2, c - 1], here)
        de[1, c] = jnp.where(lane0, 0.0, jnp.minimum(pltpu.roll(here, 1, 1), here))

    fields = Fields(fe, de, level0)
    first, last = lanes(T, Y)

    def along(k, c):
        u = qe[H + k, H + c]
        v, m, _ = fields.at(1, k, c)
        me[E + k, E + c] = u + along_forward(u, v, m, first, last, Y)

    def own_y(k, carry):
        for c in range(-E, C + E):
            along(k, c)
        return carry

    lax.fori_loop(0, L, own_y, 0)

    def zonal(k, c0, n):
        def emit(c, value):
            me[E + k, E + c0 + c] = me[E + k, E + c0 + c] + value

        forward_chain(
            n, lambda c: qe[H + k, H + c0 + c], lambda c: fields.at(0, k, c0 + c)[:2], emit
        )

    def own_z(k, carry):
        zonal(k, -E, C + 2 * E)
        return carry

    lax.fori_loop(0, L, own_z, 0)

    for phase in range(2):
        if phase < n_lev:
            high = lev_even if phase == 0 else jnp.logical_not(lev_even)
            k0 = jnp.where(high, L, -E)

            def beside(j, carry, k0=k0):
                for c in range(C):
                    along(k0 + j, c)
                zonal(k0 + j, 0, C)
                return carry

            lax.fori_loop(0, E, beside, 0)
        else:

            def blank(high):
                def column(c, carry):
                    for j in range(E):
                        me[(E + L if high else 0) + j, E + c] = zero
                    return carry

                lax.fori_loop(0, C, column, 0)

            by_parity(lev_even, phase, blank)

    def vertical(c, k0, n):
        def emit(k, value):
            me[E + k0 + k, E + c] = me[E + k0 + k, E + c] + value

        forward_chain(
            n, lambda k: qe[H + k0 + k, H + c], lambda k: fields.at(2, k0 + k, c)[:2], emit
        )

    def own_v(c, carry):
        vertical(c, -E, L + 2 * E)
        return carry

    lax.fori_loop(0, C, own_v, 0)

    def side_v(i, carry):
        vertical(jnp.where(i < E, i - E, C - E + i), 0, L)
        return carry

    lax.fori_loop(0, 2 * E, side_v, 0)

    def done(k, c, value):
        mc_ref[k, c] = value

    adjoint(dims, fields, me, E, le, mc_ref, done, sp_ref)

    for phase, out in enumerate(tile_out):

        def send_tile(high, out=out):
            def level(k, carry):
                for j in range(E):
                    out[k, j] = mc_ref[k, (C - E if high else 0) + j]
                return carry

            lax.fori_loop(0, L, level, 0)

        by_parity(tile_even, phase, send_tile)
    for phase, out in enumerate(lev_out):

        def send_lev(high, out=out):
            def column(c, carry):
                for j in range(E):
                    out[j, c] = mc_ref[(L - E if high else 0) + j, c]
                return carry

            lax.fori_loop(0, C, column, 0)

        by_parity(lev_even, phase, send_lev)


def start_body(dims, n_tile, n_lev, idx_ref, qe, fe, de, mc_ref, late_ref, *refs):
    T, L, C, Y = dims
    tile_in = refs[:n_tile]
    lev_in = refs[n_tile : n_tile + n_lev]
    out_ref, sp_ref, le, acc = refs[n_tile + n_lev :]
    tile_even = idx_ref[0] == 0
    lev_even = idx_ref[1] == 0
    zero = jnp.zeros((T, Y), jnp.float32)

    def own(k, carry):
        for c in range(C):
            le[E + k, E + c] = mc_ref[k, c]
        return carry

    lax.fori_loop(0, L, own, 0)

    def place_tile(source, high):
        def level(k, carry):
            for j in range(E):
                le[E + k, (E + C if high else 0) + j] = zero if source is None else source[k, j]
            return carry

        lax.fori_loop(0, L, level, 0)

    def place_lev(source, high):
        def column(c, carry):
            for j in range(E):
                le[(E + L if high else 0) + j, E + c] = zero if source is None else source[j, c]
            return carry

        lax.fori_loop(0, C, column, 0)

    for phase in range(2):
        by_parity(
            tile_even, phase, lambda high, p=phase: place_tile(tile_in[p] if p < n_tile else None, high)
        )
        by_parity(lev_even, phase, lambda high, p=phase: place_lev(lev_in[p] if p < n_lev else None, high))

    def done(k, c, value):
        out_ref[pl.ds(k * C + c, T, stride=L * C), :] = value

    adjoint(dims, Fields(fe, de, idx_ref[2]), qe, H, le, acc, done, sp_ref)
    sp_ref[...] = sp_ref[...] + late_ref[...]


def f32(*shape):
    return jax.ShapeDtypeStruct(shape, jnp.float32)


def call(body, name, n_in, outs, scratch, *args):
    vmem = pl.BlockSpec(memory_space=pltpu.VMEM)
    return pl.pallas_call(
        body,
        name=name,
        out_shape=outs,
        in_specs=[pl.BlockSpec(memory_space=pltpu.SMEM)] + [vmem] * (n_in - 1),
        out_specs=[vmem] * len(outs),
        scratch_shapes=scratch,
        compiler_params=pltpu.CompilerParams(vmem_limit_bytes=48 * 1024 * 1024),
    )(*args)


def share_speeds(values):
    count = lax.axis_size("trc")
    if count != 2:
        return lax.psum_scatter(values, "trc", scatter_dimension=1, tiled=True)
    half = values.shape[1] // 2
    me = lax.axis_index("trc")
    kept = lax.dynamic_slice_in_dim(values, me * half, half, axis=1)
    given = lax.dynamic_slice_in_dim(values, (1 - me) * half, half, axis=1)
    return kept + lax.ppermute(given, "trc", [(0, 1), (1, 0)])


def body(tracers, cotangent, zonal_speed, meridional_speed, vertical_speed, lateral_mixing, vertical_mixing, column_depth):
    dims = T, L, C, Y = tracers.shape
    tile_pairs = pairings(lax.axis_size("tile"))
    lev_pairs = pairings(lax.axis_size("lev"))
    n_tile, n_lev = len(tile_pairs), len(lev_pairs)
    tile, lev = lax.axis_index("tile"), lax.axis_index("lev")
    idx = jnp.stack([tile % 2, lev % 2, lev * L]).astype(jnp.int32)
    q = tracers.reshape(T * L * C, Y)
    l = cotangent.reshape(T * L * C, Y)
    inputs = (q, l, zonal_speed, meridional_speed, vertical_speed, lateral_mixing, vertical_mixing, column_depth)

    tile_rows = (H + E) * T + FPAD
    lev_rows = max(C * T, W * NF * C)
    outs = [f32(L, tile_rows, Y)] * n_tile + [f32(H + E + 1, lev_rows, Y)] * n_lev
    packed = call(functools.partial(pack_body, dims, n_tile, n_lev), "pack", 9, outs, [], idx, *inputs)
    from_tile = [lax.ppermute(x, "tile", p) for x, p in zip(packed[:n_tile], tile_pairs)]
    from_lev = [lax.ppermute(x, "lev", p) for x, p in zip(packed[n_tile:], lev_pairs)]
    corners = []
    for phase, pairs in enumerate(lev_pairs):
        k0 = jnp.where((lev + phase) % 2 == 0, L - E, 0)
        edge = jnp.stack([lax.dynamic_slice_in_dim(x, k0, E, axis=0) for x in from_tile])
        corners.append(lax.ppermute(edge, "lev", pairs))

    ext = (L + 2 * E, C + 2 * E, T, Y)
    outs = [
        f32(L + 2 * H, C + 2 * H, T, Y),
        f32(NF, L + 2 * W, C + 2 * W, 1, Y),
        f32(3, C + 2 * W, 1, Y),
        f32(L, C, T, Y),
        f32(3, L, C, Y),
    ]
    outs += [f32(L, E, T, Y)] * n_tile + [f32(E, C, T, Y)] * n_lev
    qe, fe, de, mc, late, *edges = call(
        functools.partial(middle_body, dims, n_tile, n_lev),
        "middle",
        9 + n_tile + 2 * n_lev,
        outs,
        [pltpu.VMEM(ext, jnp.float32)] * 2,
        idx,
        *inputs,
        *from_tile,
        *from_lev,
        *corners,
    )
    mc_tile = [lax.ppermute(x, "tile", p) for x, p in zip(edges[:n_tile], tile_pairs)]
    mc_lev = [lax.ppermute(x, "lev", p) for x, p in zip(edges[n_tile:], lev_pairs)]
    start, speeds = call(
        functools.partial(start_body, dims, n_tile, n_lev),
        "start",
        6 + n_tile + n_lev,
        [f32(T * L * C, Y), f32(3, L, C, Y)],
        [pltpu.VMEM(ext, jnp.float32), pltpu.VMEM((L, C, T, Y), jnp.float32)],
        idx,
        qe,
        fe,
        de,
        mc,
        late,
        *mc_tile,
        *mc_lev,
    )
    return start.reshape(T, L, C, Y), share_speeds(speeds)


def solution(mesh):
    return jax.shard_map(
        body,
        mesh=mesh,
        in_specs=(
            P("trc", "lev", ("ens", "tile"), None),
            P("trc", "lev", ("ens", "tile"), None),
            P("lev", ("ens", "tile"), None),
            P("lev", ("ens", "tile"), None),
            P("lev", ("ens", "tile"), None),
            P("lev", ("ens", "tile"), None),
            P("lev", ("ens", "tile"), None),
            P(("ens", "tile"), None),
        ),
        out_specs=(
            P("trc", "lev", ("ens", "tile"), None),
            P(None, ("lev", "trc"), ("ens", "tile"), None),
        ),
        check_vma=False,
    )
```

time: 134 us -> 65.9 us (0.49)
  the two profiles are of different devices: /device:TPU:0 before, /device:TPU:10 now
where the time goes in v1:
time: 65.9 us; the launch traced here: 65.1 us
  waiting for transfers between devices  21.8 us (33%)
  Pallas kernels  21 us (32%)
  local copies, waits for them, and re-layouts  13.8 us (21%)
  starting transfers between devices  6.92 us (11%)
  between operations  0.82 us (1%)
  other arithmetic  0.72 us (1%)
    pallas_call x3, Pallas kernels, call(): pl.pallas_call(body, name=name, out_shape=outs, in_specs=[pl.BlockSpec(me...  21 us
    ppermute x4, waiting for transfers between devices, body(): lax.ppermute(x, 'tile', p)  16.8 us
    unnamed x48, local copies, waits for them, and re-layouts  13.8 us
    ppermute x4, starting transfers between devices, body(): lax.ppermute(x, 'tile', p)  6.17 us
    ppermute x1, waiting for transfers between devices, share_speeds(): return kept + lax.ppermute(given, 'trc', [(0, 1), (1, 0)])  3.55 us
    ppermute x1, waiting for transfers between devices, body(): corners.append(lax.ppermute(edge, 'lev', pairs))  1.46 us
  transfers between devices with their start and end apart: 8, of which 6 were waited for; matrix products, arithmetic and copies ran while one was open for 0% of the time, Pallas kernels for 0%

profile of v1, /device:TPU:10, one launch (start us, length us, event | category | flops | bytes accessed | tf_op | source)
XLA Modules:
  0.0 65.1 jit_solution(1092360597051225807)
XLA Ops:
  0.8 1.0 %copy-done.1 = f32[16,8,8,128]{3,2,1,0:T(8,128)S(1)} copy-done((f32[16,8,8,128]{3,2,1,0:T(8,128)S(1)}, f32[16,8,8,128]{3,2,1,0:T(8,128)}, u32[]{:S(2)}) %copy-start.1) | copy-done | bytes 524312
  1.8 1.0 %copy-done.3 = f32[16,8,8,128]{3,2,1,0:T(8,128)S(1)} copy-done((f32[16,8,8,128]{3,2,1,0:T(8,128)S(1)}, f32[16,8,8,128]{3,2,1,0:T(8,128)}, u32[]{:S(2)}) %copy-start.3) | copy-done | bytes 524312
  2.8 0.8 %copy-done.5 = f32[8,8,128]{2,1,0:T(8,128)S(1)} copy-done((f32[8,8,128]{2,1,0:T(8,128)S(1)}, f32[8,8,128]{2,1,0:T(8,128)}, u32[]{:S(2)}) %copy-start.5) | copy-done | bytes 32792
  3.6 0.8 %copy-done.7 = f32[8,8,128]{2,1,0:T(8,128)S(1)} copy-done((f32[8,8,128]{2,1,0:T(8,128)S(1)}, f32[8,8,128]{2,1,0:T(8,128)}, u32[]{:S(2)}) %copy-start.7) | copy-done | bytes 32792
  4.4 0.8 %copy-done.9 = f32[8,8,128]{2,1,0:T(8,128)S(1)} copy-done((f32[8,8,128]{2,1,0:T(8,128)S(1)}, f32[8,8,128]{2,1,0:T(8,128)}, u32[]{:S(2)}) %copy-start.9) | copy-done | bytes 32792
  5.1 0.8 %copy-done.11 = f32[8,8,128]{2,1,0:T(8,128)S(1)} copy-done((f32[8,8,128]{2,1,0:T(8,128)S(1)}, f32[8,8,128]{2,1,0:T(8,128)}, u32[]{:S(2)}) %copy-start.11) | copy-done | bytes 32792
  5.9 0.8 %copy-done.13 = f32[8,8,128]{2,1,0:T(8,128)S(1)} copy-done((f32[8,8,128]{2,1,0:T(8,128)S(1)}, f32[8,8,128]{2,1,0:T(8,128)}, u32[]{:S(2)}) %copy-start.13) | copy-done | bytes 32792
  6.6 0.7 %copy-done.19 = s32[8,128]{1,0:T(8,128)S(1)} copy-done((s32[8,128]{1,0:T(8,128)S(1)}, s32[8,128]{1,0:T(8,128)}, u32[]{:S(2)}) %copy-start.19) | copy-done | bytes 4120
  7.3 2.2 %pack.1 = (f32[8,112,128]{2,1,0:T(8,128)S(1)}, f32[8,112,128]{2,1,0:T(8,128)}, f32[7,128,128]{2,1,0:T(8,128)S(1)}) custom-call(s32[3]{0:T(128)S(1)} %pad_add_fusion.idx_ref, f32[1024,128]{1,0:T(8,128)S(1)} %bitcast.10, f32[1024,128]{1,0:T(8,128)S(1)} %bitcast.12, f32[8,8,128]{2,1,0:T(8,128)S(1)} %copy-done.5, f32[8,8,128]{2,1,0:T(8,128)S(1)} %copy-done.7, ...), custom_call_target="tpu_custom_call" | custom-call | tf_op jit(solution)/shard_map/pack/pallas_call | solution.py:563
  9.5 3.5 %collective-permute-start.1 = (f32[8,112,128]{2,1,0:T(8,128)}, f32[8,112,128]{2,1,0:T(8,128)S(1)}, u32[]{:S(2)}, u32[]{:S(2)}) collective-permute-start(f32[8,112,128]{2,1,0:T(8,128)} %get-tuple-element.16), channel_id=1, source_target_pairs={{4,8},{8,4},{5,9},{9,5},{6,10},{10,6},{7,11},{11,7},{20,24},{24,20... | collective-permute-start | bytes 1376264 | tf_op jit(solution)/shard_map/ppermute | solution.py:600
  13.2 10.7 %collective-permute-done.1.refs_7_ = f32[8,112,128]{2,1,0:T(8,128)S(1)} collective-permute-done((f32[8,112,128]{2,1,0:T(8,128)}, f32[8,112,128]{2,1,0:T(8,128)S(1)}, u32[]{:S(2)}, u32[]{:S(2)}) %collective-permute-start.1) | collective-permute-done | bytes 458784 | tf_op jit(solution)/shard_map/ppermute | solution.py:600
  23.9 1.2 %collective-permute-done.refs_6_ = f32[8,112,128]{2,1,0:T(8,128)S(1)} collective-permute-done((f32[8,112,128]{2,1,0:T(8,128)S(1)}, f32[8,112,128]{2,1,0:T(8,128)S(1)}, u32[]{:S(2)}, u32[]{:S(2)}) %collective-permute-start) | collective-permute-done | bytes 458784 | tf_op jit(solution)/shard_map/ppermute | solution.py:600
  25.2 1.5 %collective-permute-done.3.refs_9_ = f32[2,2,112,128]{3,2,1,0:T(8,128)S(1)} collective-permute-done((f32[2,2,112,128]{3,2,1,0:T(8,128)S(1)}, f32[2,2,112,128]{3,2,1,0:T(8,128)S(1)}, u32[]{:S(2)}, u32[]{:S(2)}) %collective-permute-start.3) | collective-permute-done | bytes 229408 | tf_op jit(solution)/shard_map/ppermute | solution.py:606
  26.7 0.7 %copy-done.12 = f32[8,8,128]{2,1,0:T(8,128)S(1)} copy-done((f32[8,8,128]{2,1,0:T(8,128)S(1)}, f32[8,8,128]{2,1,0:T(8,128)}, u32[]{:S(2)}) %copy-start.12) | copy-done | bytes 32792
  27.4 0.8 %copy-done.14 = f32[8,8,128]{2,1,0:T(8,128)S(1)} copy-done((f32[8,8,128]{2,1,0:T(8,128)S(1)}, f32[8,8,128]{2,1,0:T(8,128)}, u32[]{:S(2)}) %copy-start.14) | copy-done | bytes 32792
  28.8 12.7 %middle.1 = (f32[16,16,16,128]{3,2,1,0:T(8,128)}, f32[5,14,14,1,128]{4,3,2,1,0:T(1,128)S(1)}, f32[3,14,1,128]{3,2,1,0:T(1,128)S(1)}, f32[8,8,16,128]{3,2,1,0:T(8...) custom-call(s32[3]{0:T(128)S(1)} %copy-done.22, ...), custom_call_target="tpu_custom_call" | custom-call | tf_op jit(solution)/shard_map/middle/pallas_call | solution.py:563
  43.0 2.3 %collective-permute-start.5 = (f32[8,2,16,128]{3,2,1,0:T(8,128)}, f32[8,2,16,128]{3,2,1,0:T(8,128)S(1)}, u32[]{:S(2)}, u32[]{:S(2)}) collective-permute-start(f32[8,2,16,128]{3,2,1,0:T(8,128)} %get-tuple-element.24), channel_id=1, source_target_pairs={{4,8},{8,4},{5,9},{9,5},{6,10},{10,6},{7,11},{11,7},{20,24},{24,20... | collective-permute-start | bytes 393224 | tf_op jit(solution)/shard_map/ppermute | solution.py:629
  45.4 3.0 %collective-permute-done.4.refs_0_ = f32[8,2,16,128]{3,2,1,0:T(8,128)S(1)} collective-permute-done((f32[8,2,16,128]{3,2,1,0:T(8,128)}, f32[8,2,16,128]{3,2,1,0:T(8,128)S(1)}, u32[]{:S(2)}, u32[]{:S(2)}) %collective-permute-start.4) | collective-permute-done | bytes 131104 | tf_op jit(solution)/shard_map/ppermute | solution.py:629
  48.4 1.9 %collective-permute-done.5.refs_1_ = f32[8,2,16,128]{3,2,1,0:T(8,128)S(1)} collective-permute-done((f32[8,2,16,128]{3,2,1,0:T(8,128)}, f32[8,2,16,128]{3,2,1,0:T(8,128)S(1)}, u32[]{:S(2)}, u32[]{:S(2)}) %collective-permute-start.5) | collective-permute-done | bytes 131104 | tf_op jit(solution)/shard_map/ppermute | solution.py:629
  50.3 1.6 %copy-done = f32[16,16,16,128]{3,2,1,0:T(8,128)S(1)} copy-done((f32[16,16,16,128]{3,2,1,0:T(8,128)S(1)}, f32[16,16,16,128]{3,2,1,0:T(8,128)}, u32[]{:S(2)}) %copy-start) | copy-done | bytes 2097176
  51.9 0.9 %copy-done.16 = f32[3,8,8,128]{3,2,1,0:T(8,128)S(1)} copy-done((f32[3,8,8,128]{3,2,1,0:T(8,128)S(1)}, f32[3,8,8,128]{3,2,1,0:T(8,128)}, u32[]{:S(2)}) %copy-start.16) | copy-done | bytes 98328
  52.8 0.7 %copy-done.18 = f32[3,14,1,128]{3,2,1,0:T(1,128)S(1)} copy-done((f32[3,14,1,128]{3,2,1,0:T(1,128)S(1)}, f32[3,14,1,128]{3,2,1,0:T(1,128)}, u32[]{:S(2)}) %copy-start.18) | copy-done | bytes 21528
  54.1 6.2 %start.1 = (f32[1024,128]{1,0:T(8,128)}, f32[3,8,8,128]{3,2,1,0:T(8,128)S(1)}) custom-call(s32[3]{0:T(128)S(1)} %copy-done.23, f32[16,16,16,128]{3,2,1,0:T(8,128)S(1)} %copy-done, f32[5,14,14,1,128]{4,3,2,1,0:T(1,128)S(1)} %get-tuple-element.19.fe, f32[3,14,1,128]{3,2,1,0:T(1,128)S(1)} %copy-done.18, f32[8,8,16,128]{3,2,1,0:T(8,128)S(1)} %get-tuple-element.21.mc_ref, ...), custom_call_target="tpu_custom_call" | custom-call | tf_op jit(solution)/shard_map/start/pallas_call | solution.py:563
  60.9 3.6 %collective-permute-done.7 = f32[3,4,8,128]{3,2,1,0:T(8,128)S(1)} collective-permute-done((f32[3,4,8,128]{3,2,1,0:T(8,128)S(1)}, f32[3,4,8,128]{3,2,1,0:T(8,128)S(1)}, u32[]{:S(2)}, u32[]{:S(2)}) %collective-permute-start.7) | collective-permute-done | bytes 49184 | tf_op jit(solution)/shard_map/ppermute | solution.py:582
  (49 shorter events, 4.4 us)
Async XLA Ops:
  0.6 26.0 %copy-start.6 = (f32[8,8,128]{2,1,0:T(8,128)S(1)}, f32[8,8,128]{2,1,0:T(8,128)}, u32[]{:S(2)}) copy-start(f32[8,8,128]{2,1,0:T(8,128)} %refs_0_.3) | copy-start | bytes 98308
  0.6 26.0 %copy-start.8 = (f32[8,8,128]{2,1,0:T(8,128)S(1)}, f32[8,8,128]{2,1,0:T(8,128)}, u32[]{:S(2)}) copy-start(f32[8,8,128]{2,1,0:T(8,128)} %refs_1_.3) | copy-start | bytes 98308
  0.7 12.3 %copy-start.21 = (s32[3]{0:T(128)}, s32[3]{0:T(128)S(1)}, u32[]{:S(2)}) copy-start(s32[3]{0:T(128)S(1)} %pad_add_fusion.idx_ref) | copy-start | bytes 40
  0.8 1.0 %copy-start.1 = (f32[16,8,8,128]{3,2,1,0:T(8,128)S(1)}, f32[16,8,8,128]{3,2,1,0:T(8,128)}, u32[]{:S(2)}) copy-start(f32[16,8,8,128]{3,2,1,0:T(8,128)} %param.8) | copy-start | bytes 1572868
  1.8 1.0 %copy-start.3 = (f32[16,8,8,128]{3,2,1,0:T(8,128)S(1)}, f32[16,8,8,128]{3,2,1,0:T(8,128)}, u32[]{:S(2)}) copy-start(f32[16,8,8,128]{3,2,1,0:T(8,128)} %param.9) | copy-start | bytes 1572868
  2.8 0.8 %copy-start.5 = (f32[8,8,128]{2,1,0:T(8,128)S(1)}, f32[8,8,128]{2,1,0:T(8,128)}, u32[]{:S(2)}) copy-start(f32[8,8,128]{2,1,0:T(8,128)} %refs_0_.3) | copy-start | bytes 98308
  3.6 0.8 %copy-start.7 = (f32[8,8,128]{2,1,0:T(8,128)S(1)}, f32[8,8,128]{2,1,0:T(8,128)}, u32[]{:S(2)}) copy-start(f32[8,8,128]{2,1,0:T(8,128)} %refs_1_.3) | copy-start | bytes 98308
  4.4 0.8 %copy-start.9 = (f32[8,8,128]{2,1,0:T(8,128)S(1)}, f32[8,8,128]{2,1,0:T(8,128)}, u32[]{:S(2)}) copy-start(f32[8,8,128]{2,1,0:T(8,128)} %refs_2_.3) | copy-start | bytes 98308
  5.1 0.8 %copy-start.11 = (f32[8,8,128]{2,1,0:T(8,128)S(1)}, f32[8,8,128]{2,1,0:T(8,128)}, u32[]{:S(2)}) copy-start(f32[8,8,128]{2,1,0:T(8,128)} %refs_3_.3) | copy-start | bytes 98308
  7.3 19.3 %copy-start.2 = (f32[16,8,8,128]{3,2,1,0:T(8,128)S(1)}, f32[16,8,8,128]{3,2,1,0:T(8,128)}, u32[]{:S(2)}) copy-start(f32[16,8,8,128]{3,2,1,0:T(8,128)} %param.8) | copy-start | bytes 1572868
  7.3 19.3 %copy-start.4 = (f32[16,8,8,128]{3,2,1,0:T(8,128)S(1)}, f32[16,8,8,128]{3,2,1,0:T(8,128)}, u32[]{:S(2)}) copy-start(f32[16,8,8,128]{3,2,1,0:T(8,128)} %param.9) | copy-start | bytes 1572868
  7.3 19.3 %copy-start.10 = (f32[8,8,128]{2,1,0:T(8,128)S(1)}, f32[8,8,128]{2,1,0:T(8,128)}, u32[]{:S(2)}) copy-start(f32[8,8,128]{2,1,0:T(8,128)} %refs_2_.3) | copy-start | bytes 98308
  7.3 19.3 %copy-start.20 = (s32[8,128]{1,0:T(8,128)S(1)}, s32[8,128]{1,0:T(8,128)}, u32[]{:S(2)}) copy-start(s32[8,128]{1,0:T(8,128)} %refs_5_.3) | copy-start | bytes 12292
  9.5 14.4 %collective-permute-start.1 = (f32[8,112,128]{2,1,0:T(8,128)}, f32[8,112,128]{2,1,0:T(8,128)S(1)}, u32[]{:S(2)}, u32[]{:S(2)}) collective-permute-start(f32[8,112,128]{2,1,0:T(8,128)} %get-tuple-element.16), channel_id=1, source_target_pairs={{4,8},{8,4},{5,9},{9,5},{6,10},{10,6},{7,11},{11,7},{20,24},{24,20... | collective-permute-start | bytes 1376264 | tf_op jit(solution)/shard_map/ppermute | solution.py:600
  13.0 12.0 %collective-permute-start = (f32[8,112,128]{2,1,0:T(8,128)S(1)}, f32[8,112,128]{2,1,0:T(8,128)S(1)}, u32[]{:S(2)}, u32[]{:S(2)}) collective-permute-start(f32[8,112,128]{2,1,0:T(8,128)S(1)} %get-tuple-element.15), channel_id=1, source_target_pairs={{0,4},{4,0},{8,12},{12,8},{1,5},{5,1},{9,13},{13,9},{2,6},{6,2},{1... | collective-permute-start | bytes 1376264 | tf_op jit(solution)/shard_map/ppermute | solution.py:600
  13.1 12.1 %collective-permute-start.2 = (f32[7,128,128]{2,1,0:T(8,128)S(1)}, f32[7,128,128]{2,1,0:T(8,128)S(1)}, u32[]{:S(2)}, u32[]{:S(2)}) collective-permute-start(f32[7,128,128]{2,1,0:T(8,128)S(1)} %get-tuple-element.17), channel_id=1, source_target_pairs={{0,1},{1,0},{2,3},{3,2},{4,5},{5,4},{6,7},{7,6},{8,9},{9,8},{10,11... | collective-permute-start | bytes 1376264 | tf_op jit(solution)/shard_map/ppermute | solution.py:601
  25.1 1.6 %collective-permute-start.3 = (f32[2,2,112,128]{3,2,1,0:T(8,128)S(1)}, f32[2,2,112,128]{3,2,1,0:T(8,128)S(1)}, u32[]{:S(2)}, u32[]{:S(2)}) collective-permute-start(f32[2,2,112,128]{3,2,1,0:T(8,128)S(1)} %pad_maximum_fusion), channel_id=1, source_target_pairs={{0,1},{1,0},{2,3},{3,2},{4,5},{5,4},{6,7},{7,6},{8,9},{9,8},{10,11... | collective-permute-start | bytes 688136 | tf_op jit(solution)/shard_map/ppermute | solution.py:606
  26.7 0.8 %copy-start.12 = (f32[8,8,128]{2,1,0:T(8,128)S(1)}, f32[8,8,128]{2,1,0:T(8,128)}, u32[]{:S(2)}) copy-start(f32[8,8,128]{2,1,0:T(8,128)} %refs_3_.3) | copy-start | bytes 98308
  42.7 5.7 %collective-permute-start.4 = (f32[8,2,16,128]{3,2,1,0:T(8,128)}, f32[8,2,16,128]{3,2,1,0:T(8,128)S(1)}, u32[]{:S(2)}, u32[]{:S(2)}) collective-permute-start(f32[8,2,16,128]{3,2,1,0:T(8,128)} %get-tuple-element.23), channel_id=1, source_target_pairs={{0,4},{4,0},{8,12},{12,8},{1,5},{5,1},{9,13},{13,9},{2,6},{6,2},{1... | collective-permute-start | bytes 393224 | tf_op jit(solution)/shard_map/ppermute | solution.py:629
  43.0 7.3 %collective-permute-start.5 = (f32[8,2,16,128]{3,2,1,0:T(8,128)}, f32[8,2,16,128]{3,2,1,0:T(8,128)S(1)}, u32[]{:S(2)}, u32[]{:S(2)}) collective-permute-start(f32[8,2,16,128]{3,2,1,0:T(8,128)} %get-tuple-element.24), channel_id=1, source_target_pairs={{4,8},{8,4},{5,9},{9,5},{6,10},{10,6},{7,11},{11,7},{20,24},{24,20... | collective-permute-start | bytes 393224 | tf_op jit(solution)/shard_map/ppermute | solution.py:629
  45.3 5.0 %collective-permute-start.6 = (f32[2,8,16,128]{3,2,1,0:T(8,128)}, f32[2,8,16,128]{3,2,1,0:T(8,128)S(1)}, u32[]{:S(2)}, u32[]{:S(2)}) collective-permute-start(f32[2,8,16,128]{3,2,1,0:T(8,128)} %get-tuple-element.25), channel_id=1, source_target_pairs={{0,1},{1,0},{2,3},{3,2},{4,5},{5,4},{6,7},{7,6},{8,9},{9,8},{10,11... | collective-permute-start | bytes 393224 | tf_op jit(solution)/shard_map/ppermute | solution.py:630
  50.3 1.6 %copy-start = (f32[16,16,16,128]{3,2,1,0:T(8,128)S(1)}, f32[16,16,16,128]{3,2,1,0:T(8,128)}, u32[]{:S(2)}) copy-start(f32[16,16,16,128]{3,2,1,0:T(8,128)} %get-tuple-element.18.qe) | copy-start | bytes 6291460
  51.9 0.9 %copy-start.16 = (f32[3,8,8,128]{3,2,1,0:T(8,128)S(1)}, f32[3,8,8,128]{3,2,1,0:T(8,128)}, u32[]{:S(2)}) copy-start(f32[3,8,8,128]{3,2,1,0:T(8,128)} %copy-done.15) | copy-start | bytes 294916
  60.4 4.1 %collective-permute-start.7 = (f32[3,4,8,128]{3,2,1,0:T(8,128)S(1)}, f32[3,4,8,128]{3,2,1,0:T(8,128)S(1)}, u32[]{:S(2)}, u32[]{:S(2)}) collective-permute-start(f32[3,4,8,128]{3,2,1,0:T(8,128)S(1)} %constant_dynamic-slice_fusion), channel_id=1, source_target_pairs={{0,2},{2,0},{1,3},{3,1},{4,6},{6,4},{5,7},{7,5},{8,10},{10,8},{9,1... | collective-permute-start | bytes 147464 | tf_op jit(solution)/shard_map/ppermute | solution.py:582
  (8 other events, 5.4 us)

commit v2 on v0

v2 whole, which is shorter than its diff:
```python
import functools

import jax
import jax.numpy as jnp
from jax import lax
from jax.experimental import pallas as pl
from jax.experimental.pallas import tpu as pltpu
from jax.sharding import PartitionSpec as P

albada_floor = 0.01
H = 4
E = 2
W = 3
NF = 5
YC = 8
MIB = 60
FPAD = 16


def pairings(count):
    phases = []
    for first in (0, 1):
        pairs = []
        for i in range(first, count - 1, 2):
            pairs += [(i, i + 1), (i + 1, i)]
        if pairs:
            phases.append(pairs)
    return phases


def by_parity(even, phase, act):
    @pl.when(even)
    def _():
        act(phase == 0)

    @pl.when(jnp.logical_not(even))
    def _():
        act(phase == 1)


def limiter(x, y, xx, yy):
    s = x * y
    r = 1.0 / (xx + yy + albada_floor)
    a = s * (x + y) * r
    return s, r, a


def slopes(x, y, xx, yy, s, r, a):
    return r * (0.5 * yy + s - x * a), r * (0.5 * xx + s - y * a)


def forward_chain(n, get_u, get_co, emit, keep=None):
    u_a, u_b = get_u(-2), get_u(-1)
    d_b = u_b - u_a
    xx_b = d_b * d_b
    half_b = None
    flux_b = None
    for f in range(0, n + 2):
        u_c = get_u(f)
        d_c = u_c - u_b
        xx_c = d_c * d_c
        s, r, a = limiter(d_b, d_c, xx_b, xx_c)
        half_c = 0.5 * a
        carried = None
        if f >= 1:
            v, m = get_co(f - 1)
            carried = jnp.where(v >= 0.0, u_a + half_b, u_b - half_c)
            flux = v * carried - m * d_b
            if f >= 2:
                emit(f - 2, flux_b - flux)
            flux_b = flux
        if keep is not None:
            keep(f - 1, lambda: slopes(d_b, d_c, xx_b, xx_c, s, r, a), carried)
        u_a, u_b, d_b, xx_b, half_b = u_b, u_c, d_c, xx_c, half_c


def fresh_limits(get_u):
    state = {"u_a": get_u(-2), "u_b": get_u(-1), "half": None}
    state["d"] = state["u_b"] - state["u_a"]
    state["xx"] = state["d"] * state["d"]

    def step(f, v):
        u_a, u_b, d_b, xx_b = state["u_a"], state["u_b"], state["d"], state["xx"]
        u_c = get_u(f)
        d_c = u_c - u_b
        xx_c = d_c * d_c
        s, r, a = limiter(d_b, d_c, xx_b, xx_c)
        half_c = 0.5 * a
        carried = None
        if f >= 1:
            carried = jnp.where(v >= 0.0, u_a + state["half"], u_b - half_c)
        state.update(u_a=u_b, u_b=u_c, half=half_c, d=d_c, xx=xx_c)
        up, down = slopes(d_b, d_c, xx_b, xx_c, s, r, a)
        return up, down, carried

    return step


def adjoint_chain(n, limits, get_l, get_co, emit, emit_speed):
    l_b = get_l(-1)
    g_b = l_b - get_l(-2)
    v_b, _ = get_co(-1)
    n_b = jnp.minimum(v_b, 0.0) * g_b
    p_b = dm_b = down_a = dd_a = n_a = None
    for f in range(0, n + 2):
        l_c = get_l(f)
        g_c = l_c - l_b
        v_c, m_c = get_co(f)
        p_c = jnp.maximum(v_c, 0.0) * g_c
        n_c = jnp.minimum(v_c, 0.0) * g_c
        up, down, carried = limits(f, v_b)
        e = p_c - n_b
        if f >= 1:
            dd_b = e * up + down_a - dm_b
            if f >= 2:
                emit(f - 2, n_a + p_b + dd_a - dd_b)
            if f - 1 < n:
                emit_speed(f - 1, g_b * carried)
            dd_a = dd_b
        down_a = e * down
        n_a = n_b
        p_b, n_b, v_b = p_c, n_c, v_c
        dm_b = m_c * g_c
        g_b, l_b = g_c, l_c


def lanes(T, Y):
    lane = lax.broadcasted_iota(jnp.int32, (T, Y), 1)
    return lane == 0, lane == Y - 1


def along_values(u, v, ends):
    first, last = ends
    Y = u.shape[-1]
    before = jnp.where(first, 0.0, pltpu.roll(u, 1, 1))
    d = u - before
    nxt = jnp.where(last, -u, pltpu.roll(d, Y - 1, 1))
    xx, yy = d * d, nxt * nxt
    s, r, a = limiter(d, nxt, xx, yy)
    half = 0.5 * a
    carried = jnp.where(v >= 0.0, before + pltpu.roll(half, 1, 1), u - half)
    return d, carried, lambda: slopes(d, nxt, xx, yy, s, r, a)


def along_forward(d, carried, v, m):
    flux = v * carried - m * d
    return flux - pltpu.roll(flux, flux.shape[-1] - 1, 1)


def along_adjoint(l, v, m, up, down, ends):
    first, last = ends
    Y = l.shape[-1]
    g = l - pltpu.roll(l, 1, 1)
    p = jnp.maximum(v, 0.0) * g
    n = jnp.minimum(v, 0.0) * g
    e = pltpu.roll(p, Y - 1, 1) - n
    z = e * up - m * g
    y = e * down
    add = (
        (n + z - y)
        + jnp.where(first, 0.0, pltpu.roll(y, 1, 1))
        + jnp.where(last, 0.0, pltpu.roll(p - z, Y - 1, 1))
    )
    return add, g


class Fields:
    def __init__(self, f_ref, d_ref, level0):
        self.f, self.d, self.level0 = f_ref, d_ref, level0

    def at(self, direction, k, c):
        depth = self.d[direction, W + c]
        level = (self.level0 + k).astype(jnp.float32)
        if direction == 2:
            level = jnp.where(level >= 1.0, level, 1e9)
        is_open = depth > level
        speed = self.f[direction, W + k, W + c]
        mix = self.f[(3, 3, 4)[direction], W + k, W + c]
        return jnp.where(is_open, speed, 0.0), jnp.where(is_open, mix, 0.0), is_open


def parities():
    return lax.axis_index("tile") % 2 == 0, lax.axis_index("lev") % 2 == 0


def depth_rows(de, columns):
    Y = de.shape[-1]
    lane0 = lax.broadcasted_iota(jnp.int32, (1, Y), 1) == 0
    for c in columns:
        here = de[2, W + c]
        de[1, W + c] = jnp.where(lane0, 0.0, jnp.minimum(pltpu.roll(here, 1, 1), here))


def fetch(pairs, sem):
    copies = [pltpu.make_async_copy(a, b, sem.at[i]) for i, (a, b) in enumerate(pairs)]
    for c in copies:
        c.start()
    return copies


def edges_body(dims, n_tile, *refs):
    T, L, C, _ = dims
    sources, tile_out, (q_ref, l_ref, f_ref, d_ref, sem) = refs[:8], refs[8 : 8 + n_tile], refs[8 + n_tile :]
    targets = [q_ref, l_ref] + [f_ref.at[f] for f in range(NF)] + [d_ref]
    copies = fetch(zip(sources, targets), sem)
    for c in copies[2:] + copies[:2]:
        c.wait()
    tile_even, _ = parities()

    def slab(ref, k, c):
        return ref[pl.ds(k * C + c, T, stride=L * C), :]

    for phase, out in enumerate(tile_out):

        def send_tile(high, out=out):
            q0 = C - H if high else 0
            l0 = C - E if high else 0
            f0 = C - W if high else 0

            def level(k, carry):
                for j in range(H):
                    out[k, j * T : (j + 1) * T, :] = slab(q_ref, k, q0 + j)
                for j in range(E):
                    out[k, (H + j) * T : (H + j + 1) * T, :] = slab(l_ref, k, l0 + j)
                base = (H + E) * T
                for f in range(NF):
                    out[k, base + W * f : base + W * (f + 1), :] = f_ref[f, k, f0 : f0 + W, :]
                out[k, base + W * NF : base + W * NF + 1, :] = d_ref[f0 : f0 + 1, :].astype(jnp.float32)
                return carry

            lax.fori_loop(0, L, level, 0, unroll=2)
            base = (H + E) * T + W * NF
            for j in range(1, W):
                out[j, base : base + 1, :] = d_ref[f0 + j : f0 + j + 1, :].astype(jnp.float32)

        by_parity(tile_even, phase, send_tile)


def own_body(dims, n_lev, *refs):
    T, L, C, Y = dims
    sources, lev_out = refs[:8], refs[9 : 9 + n_lev]
    qe, le, fe, de, q_ref, l_ref, f_ref, d_ref, sem = refs[9 + n_lev :]
    targets = [q_ref, l_ref] + [f_ref.at[f] for f in range(NF)] + [d_ref]
    copies = fetch(zip(sources, targets), sem)
    for c in copies[2:] + copies[:2]:
        c.wait()
    _, lev_even = parities()
    zero = jnp.zeros((T, Y), jnp.float32)
    zero_row = jnp.zeros((1, Y), jnp.float32)

    def own_level(k, carry):
        for c in range(C):
            qe[H + k, H + c] = q_ref[pl.ds(k * C + c, T, stride=L * C), :]
            le[E + k, E + c] = l_ref[pl.ds(k * C + c, T, stride=L * C), :]
            for f in range(NF):
                fe[f, W + k, W + c] = f_ref[f, k, c : c + 1, :]
        return carry

    lax.fori_loop(0, L, own_level, 0)
    for c in range(C):
        de[2, W + c] = d_ref[c : c + 1, :].astype(jnp.float32)
    depth_rows(de, range(C))

    for phase, out in enumerate(lev_out):

        def send_lev(high, out=out):
            def column(c, carry):
                rows = pl.ds(pl.multiple_of(c * T, 8), T)
                for j in range(H):
                    out[j, rows, :] = qe[H + (L - H if high else 0) + j, H + c]
                for j in range(E):
                    out[H + j, rows, :] = le[E + (L - E if high else 0) + j, E + c]
                return carry

            lax.fori_loop(0, C, column, 0)
            for j in range(W):
                k = (L - W if high else 0) + j
                for f in range(NF):
                    out[H + E, (j * NF + f) * C : (j * NF + f + 1) * C, :] = f_ref[f, k]

        by_parity(lev_even, phase, send_lev)

    def blank_lev(high):
        def column(c, carry):
            for j in range(H):
                qe[(H + L if high else 0) + j, H + c] = zero
            for j in range(E):
                le[(E + L if high else 0) + j, E + c] = zero
            for j in range(W):
                for f in range(NF):
                    fe[f, (W + L if high else 0) + j, W + c] = zero_row
            return carry

        lax.fori_loop(0, C, column, 0)
        for j in range(E):
            for i in range(E):
                for col in (H - E + i, H + C + i):
                    qe[(H + L if high else H - E) + j, col] = zero
                for f in range(NF):
                    for col in (W - E + i, W + C + i):
                        fe[f, (W + L if high else W - E) + j, col] = zero_row

    for phase in range(n_lev, 2):
        by_parity(lev_even, phase, blank_lev)


def inner_body(dims, n_lev, *refs):
    T, L, C, Y = dims
    lev_in = refs[:n_lev]
    de = refs[n_lev + 3]
    qe, le, fe, me, yu, yd, yc, vu, vd, vc = refs[n_lev + 4 :]
    _, lev_even = parities()
    zero = jnp.zeros((T, Y), jnp.float32)

    for phase, source in enumerate(lev_in):

        def place_lev(high, source=source):
            q0 = H + L if high else 0
            l0 = E + L if high else 0
            f0 = W + L if high else 0

            def column(c, carry):
                rows = pl.ds(pl.multiple_of(c * T, 8), T)
                for j in range(H):
                    qe[q0 + j, H + c] = source[j, rows, :]
                for j in range(E):
                    le[l0 + j, E + c] = source[H + j, rows, :]
                return carry

            lax.fori_loop(0, C, column, 0)
            for j in range(W):
                for f in range(NF):
                    for c in range(C):
                        r = (j * NF + f) * C + c
                        fe[f, f0 + j, W + c] = source[H + E, r : r + 1, :]

        by_parity(lev_even, phase, place_lev)

    fields = Fields(fe, de, lax.axis_index("lev") * L)
    ends = lanes(T, Y)

    def own_y(i, carry):
        k = i // (C // YC)
        c0 = (i % (C // YC)) * YC
        for j in range(YC):
            c = c0 + j
            u = qe[H + k, H + c]
            v, m, _ = fields.at(1, k, c)
            d, carried, coefs = along_values(u, v, ends)
            yu[k, c], yd[k, c] = coefs()
            yc[k, c] = carried
            me[E + k, E + c] = u + along_forward(d, carried, v, m)
        return carry

    lax.fori_loop(0, L * (C // YC), own_y, 0)

    for phase in range(2):
        if phase < n_lev:
            high = lev_even if phase == 0 else jnp.logical_not(lev_even)
            k0 = jnp.where(high, L, -E)

            def beside(i, carry, k0=k0):
                k = k0 + i // (C // YC)
                c0 = (i % (C // YC)) * YC
                for j in range(YC):
                    c = c0 + j
                    u = qe[H + k, H + c]
                    v, m, _ = fields.at(1, k, c)
                    d, carried, _ = along_values(u, v, ends)
                    me[E + k, E + c] = u + along_forward(d, carried, v, m)
                return carry

            lax.fori_loop(0, E * (C // YC), beside, 0)
        else:

            def blank(high):
                def column(c, carry):
                    for j in range(E):
                        me[(E + L if high else 0) + j, E + c] = zero
                    return carry

                lax.fori_loop(0, C, column, 0)

            by_parity(lev_even, phase, blank)

    def own_v(c, carry):
        def emit(k, value):
            me[k, E + c] = me[k, E + c] + value

        def keep(k, coefs, carried):
            k = k - E
            if -1 <= k <= L:
                vu[1 + k, c], vd[1 + k, c] = coefs()
            if 0 <= k < L:
                vc[k, c] = carried

        forward_chain(
            L + 2 * E, lambda k: qe[H - E + k, H + c], lambda k: fields.at(2, k - E, c)[:2], emit, keep
        )
        return carry

    lax.fori_loop(0, C, own_v, 0)


def corner_body(dims, n_tile, *refs):
    L = dims[1]
    tile_in, lev_out = refs[:n_tile], refs[n_tile + 1 :]
    _, lev_even = parities()
    for phase, out in enumerate(lev_out):

        def send(high, out=out):
            for t in range(n_tile):
                for j in range(E):
                    out[t, j] = tile_in[t][(L - E if high else 0) + j]

        by_parity(lev_even, phase, send)


def beside_body(dims, n_tile, *refs):
    T, L, C, Y = dims
    tile_in = refs[:n_tile]
    qe, le, fe, de, me = refs[n_tile + 5 :]
    tile_even, _ = parities()
    zero = jnp.zeros((T, Y), jnp.float32)
    zero_row = jnp.zeros((1, Y), jnp.float32)

    def place_tile(source, high):
        q0 = H + C if high else 0
        l0 = E + C if high else 0
        f0 = W + C if high else 0

        def level(k, carry):
            for j in range(H):
                qe[H + k, q0 + j] = zero if source is None else source[k, j * T : (j + 1) * T, :]
            for j in range(E):
                le[E + k, l0 + j] = zero if source is None else source[k, (H + j) * T : (H + j + 1) * T, :]
            base = (H + E) * T
            for f in range(NF):
                for j in range(W):
                    r = base + W * f + j
                    fe[f, W + k, f0 + j] = zero_row if source is None else source[k, r : r + 1, :]
            return carry

        lax.fori_loop(0, L, level, 0, unroll=4)
        base = (H + E) * T + W * NF
        for j in range(W):
            de[2, f0 + j] = zero_row if source is None else source[j, base : base + 1, :]

    for phase in range(2):
        source = tile_in[phase] if phase < n_tile else None
        by_parity(tile_even, phase, lambda high, s=source: place_tile(s, high))

    depth_rows(de, [-2, -1, C, C + 1])
    for c in range(-E, C + E + 1):
        de[0, W + c] = jnp.minimum(de[2, W + c - 1], de[2, W + c])

    fields = Fields(fe, de, lax.axis_index("lev") * L)
    ends = lanes(T, Y)

    def level_y(k, carry):
        for c in (-2, -1, C, C + 1):
            u = qe[H + k, H + c]
            v, m, _ = fields.at(1, k, c)
            d, carried, _ = along_values(u, v, ends)
            me[E + k, E + c] = u + along_forward(d, carried, v, m)
        return carry

    lax.fori_loop(0, L, level_y, 0, unroll=2)

    def level_z(k, carry):
        def emit(c, value):
            me[E + k, c] = me[E + k, c] + value

        forward_chain(
            C + 2 * E, lambda c: qe[H + k, H - E + c], lambda c: fields.at(0, k, c - E)[:2], emit
        )
        return carry

    lax.fori_loop(0, L, level_z, 0)


def late_body(dims, n_tile, n_lev, *refs):
    T, L, C, Y = dims
    corner_in = refs[:n_lev]
    le, de = refs[n_lev : n_lev + 2]
    qe, fe, me, mc_ref, sp_ref = refs[n_lev + 5 : n_lev + 10]
    tile_out = refs[n_lev + 10 : n_lev + 10 + n_tile]
    lev_out = refs[n_lev + 10 + n_tile :]
    tile_even, lev_even = parities()
    zero = jnp.zeros((T, Y), jnp.float32)
    zero_row = jnp.zeros((1, Y), jnp.float32)

    def place_corner(source, tile_high, lev_high):
        for j in range(E):
            q_lev = H + L + j if lev_high else H - E + j
            f_lev = W + L + j if lev_high else W - E + j
            for i in range(E):
                s = i if tile_high else H - E + i
                col = (H + C + i) if tile_high else (H - E + i)
                qe[q_lev, col] = zero if source is None else source[j, s * T : (s + 1) * T, :]
                for f in range(NF):
                    r = (H + E) * T + W * f + (i if tile_high else W - E + i)
                    col = (W + C + i) if tile_high else (W - E + i)
                    fe[f, f_lev, col] = zero_row if source is None else source[j, r : r + 1, :]

    for phase in range(n_lev):
        for other in range(2):

            def corner(lev_high, p=phase, t=other):
                source = corner_in[p].at[t] if t < n_tile else None
                by_parity(tile_even, t, lambda tile_high: place_corner(source, tile_high, lev_high))

            by_parity(lev_even, phase, corner)

    fields = Fields(fe, de, lax.axis_index("lev") * L)

    for phase in range(n_lev):
        high = lev_even if phase == 0 else jnp.logical_not(lev_even)
        k0 = jnp.where(high, L, -E)

        def beside(j, carry, k0=k0):
            k = k0 + j

            def emit(c, value):
                me[E + k, E + c] = me[E + k, E + c] + value

            forward_chain(C, lambda c: qe[H + k, H + c], lambda c: fields.at(0, k, c)[:2], emit)
            return carry

        lax.fori_loop(0, E, beside, 0)

    def side_v(i, carry):
        c = jnp.where(i < E, i - E, C - E + i)

        def emit(k, value):
            me[E + k, E + c] = me[E + k, E + c] + value

        forward_chain(L, lambda k: qe[H + k, H + c], lambda k: fields.at(2, k, c)[:2], emit)
        return carry

    lax.fori_loop(0, 2 * E, side_v, 0)

    def done(k, c, value):
        mc_ref[k, c] = value

    adjoint(dims, fields, me, E, le, mc_ref, done, sp_ref)

    for phase, out in enumerate(tile_out):

        def send_tile(high, out=out):
            def level(k, carry):
                for j in range(E):
                    out[k, j] = mc_ref[k, (C - E if high else 0) + j]
                return carry

            lax.fori_loop(0, L, level, 0)

        by_parity(tile_even, phase, send_tile)
    for phase, out in enumerate(lev_out):

        def send_lev(high, out=out):
            def column(c, carry):
                for j in range(E):
                    out[j, c] = mc_ref[(L - E if high else 0) + j, c]
                return carry

            lax.fori_loop(0, C, column, 0)

        by_parity(lev_even, phase, send_lev)


def adjoint(dims, fields, u_ref, uo, l_ref, acc_ref, done, speed_ref, kept=None):
    T, L, C, Y = dims
    ends = lanes(T, Y)
    yu, yd, yc, vu, vd, vc = kept or [None] * 6

    def store_speed(direction, k, c, is_open, value):
        row = jnp.sum(value, axis=0, keepdims=True)
        speed_ref[direction, k, pl.ds(c, 1), :] = jnp.where(is_open, row, 0.0)

    def along(i, carry):
        k = i // (C // YC)
        c0 = (i % (C // YC)) * YC
        for j in range(YC):
            c = c0 + j
            l = l_ref[E + k, E + c]
            v, m, is_open = fields.at(1, k, c)
            if kept is None:
                _, carried, coefs = along_values(u_ref[uo + k, uo + c], v, ends)
                up, down = coefs()
            else:
                up, down, carried = yu[k, c], yd[k, c], yc[k, c]
            add, g = along_adjoint(l, v, m, up, down, ends)
            acc_ref[k, c] = l + add
            store_speed(1, k, c, is_open, g * carried)
        return carry

    lax.fori_loop(0, L * (C // YC), along, 0)

    def level_z(k, carry):
        opened = {}

        def co(c):
            v, m, opened[c] = fields.at(0, k, c)
            return v, m

        def emit(c, value):
            acc_ref[k, c] = acc_ref[k, c] + value

        adjoint_chain(
            C,
            fresh_limits(lambda c: u_ref[uo + k, uo + c]),
            lambda c: l_ref[E + k, E + c],
            co,
            emit,
            lambda c, value: store_speed(0, k, c, opened[c], value),
        )
        return carry

    lax.fori_loop(0, L, level_z, 0)

    def column_v(c, carry):
        opened = {}

        def co(k):
            v, m, opened[k] = fields.at(2, k, c)
            return v, m

        def emit(k, value):
            done(k, c, acc_ref[k, c] + value)

        if kept is None:
            limits = fresh_limits(lambda k: u_ref[uo + k, uo + c])
        else:

            def limits(f, v):
                k = f - 1
                return vu[1 + k, c], vd[1 + k, c], vc[k, c] if 0 <= k < L else None

        adjoint_chain(
            L,
            limits,
            lambda k: l_ref[E + k, E + c],
            co,
            emit,
            lambda k, value: store_speed(2, k, c, opened[k], value),
        )
        return carry

    lax.fori_loop(0, C, column_v, 0)


def start_body(dims, n_tile, n_lev, *refs):
    T, L, C, Y = dims
    qe, fe, de, mc_ref, late_ref = refs[:5]
    kept = refs[5:11]
    tile_in = refs[11 : 11 + n_tile]
    lev_in = refs[11 + n_tile : 11 + n_tile + n_lev]
    out_ref, sp_out, *rest = refs[11 + n_tile + n_lev :]
    given_ref = rest[0] if len(rest) == 4 else None
    le, acc, sp_ref = rest[-3:]
    tile_even, lev_even = parities()
    zero = jnp.zeros((T, Y), jnp.float32)

    def own(k, carry):
        for c in range(C):
            le[E + k, E + c] = mc_ref[k, c]
        return carry

    lax.fori_loop(0, L, own, 0)

    def place_tile(source, high):
        def level(k, carry):
            for j in range(E):
                le[E + k, (E + C if high else 0) + j] = zero if source is None else source[k, j]
            return carry

        lax.fori_loop(0, L, level, 0)

    def place_lev(source, high):
        def column(c, carry):
            for j in range(E):
                le[(E + L if high else 0) + j, E + c] = zero if source is None else source[j, c]
            return carry

        lax.fori_loop(0, C, column, 0)

    for phase in range(2):
        by_parity(
            tile_even, phase, lambda high, p=phase: place_tile(tile_in[p] if p < n_tile else None, high)
        )
        by_parity(lev_even, phase, lambda high, p=phase: place_lev(lev_in[p] if p < n_lev else None, high))

    def done(k, c, value):
        out_ref[pl.ds(k * C + c, T, stride=L * C), :] = value

    adjoint(dims, Fields(fe, de, lax.axis_index("lev") * L), qe, H, le, acc, done, sp_ref, kept)
    if given_ref is None:
        sp_out[...] = sp_ref[...] + late_ref[...]
        return
    half = L // 2
    low = lax.axis_index("trc") == 0
    for keeps_low in (True, False):

        @pl.when(low if keeps_low else jnp.logical_not(low))
        def _(keeps_low=keeps_low):
            for out, first in ((sp_out, keeps_low), (given_ref, not keeps_low)):
                k0 = 0 if first else half
                out[...] = sp_ref[:, k0 : k0 + half] + late_ref[:, k0 : k0 + half]


def f32(*shape):
    return jax.ShapeDtypeStruct(shape, jnp.float32)


def call(body, outs, scratch, args, hbm=0, aliases=None, mib=4):
    return run(body, outs, scratch, args, hbm, aliases, mib)


def run(body, outs, scratch, args, hbm, aliases, mib):
    vmem = pl.BlockSpec(memory_space=pltpu.VMEM)
    return pl.pallas_call(
        body,
        out_shape=outs,
        in_specs=[pl.BlockSpec(memory_space=pltpu.HBM)] * hbm + [vmem] * (len(args) - hbm),
        out_specs=[vmem] * len(outs),
        scratch_shapes=scratch,
        input_output_aliases=aliases or {},
        compiler_params=pltpu.CompilerParams(vmem_limit_bytes=mib * 1024 * 1024),
    )(*args)


def swap(values, axis, pairings_):
    received = []
    for x, pairs in zip(values, pairings_):
        received.append(lax.ppermute(x, axis, pairs))
    return received


def program(tracers, cotangent, zonal_speed, meridional_speed, vertical_speed, lateral_mixing, vertical_mixing, column_depth):
    dims = T, L, C, Y = tracers.shape
    tile_pairs = pairings(lax.axis_size("tile"))
    lev_pairs = pairings(lax.axis_size("lev"))
    n_tile, n_lev = len(tile_pairs), len(lev_pairs)
    q = tracers.reshape(T * L * C, Y)
    l = cotangent.reshape(T * L * C, Y)
    inputs = [q, l, zonal_speed, meridional_speed, vertical_speed, lateral_mixing, vertical_mixing, column_depth]
    landing = [
        pltpu.VMEM((T * L * C, Y), jnp.float32),
        pltpu.VMEM((T * L * C, Y), jnp.float32),
        pltpu.VMEM((NF, L, C, Y), jnp.float32),
        pltpu.VMEM((C, Y), jnp.int32),
        pltpu.SemaphoreType.DMA((8,)),
    ]

    tile_rows = (H + E) * T + FPAD
    lev_rows = max(C * T, W * NF * C)
    to_tile = call(
        functools.partial(edges_body, dims, n_tile), [f32(L, tile_rows, Y)] * n_tile, landing, inputs, hbm=8, mib=MIB
    )
    from_tile = swap(to_tile, "tile", tile_pairs)

    qe_s = f32(L + 2 * H, C + 2 * H, T, Y)
    ext_s = f32(L + 2 * E, C + 2 * E, T, Y)
    fe_s = f32(NF, L + 2 * W, C + 2 * W, 1, Y)
    de_s = f32(3, C + 2 * W, 1, Y)
    own_s = f32(L, C, T, Y)
    *to_lev, qe, le, fe, de = call(
        functools.partial(own_body, dims, n_lev),
        [f32(H + E + 1, lev_rows, Y)] * n_lev + [qe_s, ext_s, fe_s, de_s],
        landing,
        inputs + [to_tile[0]],
        hbm=8,
    )
    from_lev = swap(to_lev, "lev", lev_pairs)
    n = n_lev
    qe, le, fe, me, *kept = call(
        functools.partial(inner_body, dims, n_lev),
        [qe_s, ext_s, fe_s, ext_s] + [own_s] * 3 + [f32(L + 2, C, T, Y)] * 2 + [own_s],
        [],
        [*from_lev, qe, le, fe, de],
        aliases={n: 0, n + 1: 1, n + 2: 2},
    )
    to_lev = call(
        functools.partial(corner_body, dims, n_tile), [f32(n_tile, E, tile_rows, Y)] * n_lev, [], [*from_tile, me]
    )
    corners = swap(to_lev, "lev", lev_pairs)
    n = n_tile
    qe, le, fe, de, me = call(
        functools.partial(beside_body, dims, n_tile),
        [qe_s, ext_s, fe_s, de_s, ext_s],
        [],
        [*from_tile, qe, le, fe, de, me],
        aliases={n + i: i for i in range(5)},
    )
    n = n_lev
    qe, fe, me, mc, late, *mc_edges = call(
        functools.partial(late_body, dims, n_tile, n_lev),
        [qe_s, fe_s, ext_s, own_s, f32(3, L, C, Y)] + [f32(L, E, T, Y)] * n_tile + [f32(E, C, T, Y)] * n_lev,
        [],
        [*corners, le, de, qe, fe, me],
        aliases={n + 2: 0, n + 3: 1, n + 4: 2},
    )
    mc_tile = swap(mc_edges[:n_tile], "tile", tile_pairs)
    mc_lev = swap(mc_edges[n_tile:], "lev", lev_pairs)
    pair = lax.axis_size("trc") == 2 and L % 2 == 0
    start, speeds, *given = call(
        functools.partial(start_body, dims, n_tile, n_lev),
        [f32(T * L * C, Y)] + ([f32(3, L // 2, C, Y)] * 2 if pair else [f32(3, L, C, Y)]),
        [pltpu.VMEM(x.shape, jnp.float32) for x in (ext_s, own_s, f32(3, L, C, Y))],
        [qe, fe, de, mc, late, *kept, *mc_tile, *mc_lev],
    )
    if pair:
        speeds = speeds + lax.ppermute(given[0], "trc", [(0, 1), (1, 0)])
    else:
        speeds = lax.psum_scatter(speeds, "trc", scatter_dimension=1, tiled=True)
    return start.reshape(T, L, C, Y), speeds


def solution(mesh):
    return jax.shard_map(
        program,
        mesh=mesh,
        in_specs=(
            P("trc", "lev", ("ens", "tile"), None),
            P("trc", "lev", ("ens", "tile"), None),
            P("lev", ("ens", "tile"), None),
            P("lev", ("ens", "tile"), None),
            P("lev", ("ens", "tile"), None),
            P("lev", ("ens", "tile"), None),
            P("lev", ("ens", "tile"), None),
            P(("ens", "tile"), None),
        ),
        out_specs=(
            P("trc", "lev", ("ens", "tile"), None),
            P(None, ("lev", "trc"), ("ens", "tile"), None),
        ),
        check_vma=False,
    )
```

time: 134 us -> 47.2 us (0.35)
  waiting for transfers between devices: 42.8 us -> 12.4 us
  starting transfers between devices: 39.2 us -> 11 us
  other arithmetic: 26.9 us -> 0.63 us
  Pallas kernels: 0 us -> 20.5 us
  between operations: 15.8 us -> 0.87 us
  local copies, waits for them, and re-layouts: 8.55 us -> 1.05 us
    ppermute x16 -> x8, starting transfers between devices: 39.2 us -> 11 us  [the longest x7 9.48 us: swap(): received.append(lax.ppermute(x, axis, pairs))]
    unnamed x2 -> x0, waiting for transfers between devices: 21.4 us -> none
    pallas_call x0 -> x7, Pallas kernels: none -> 20.5 us  [run(): pl.pallas_call(body, out_shape=outs, in_specs=[pl.BlockSpec(memory_space=...]
    add_any x19 -> x0, other arithmetic: 13.1 us -> none  [the longest x7 7.63 us: face_flux(): rising = behind + 0.5 * albada(behind - far_behind, beyond - behind)]
    ppermute x16 -> x8, waiting for transfers between devices: 21.4 us -> 12.4 us  [the longest x7 9.79 us: swap(): received.append(lax.ppermute(x, axis, pairs))]
    mul x15 -> x0, other arithmetic: 4.18 us -> none  [the longest x3 3.73 us: face_flux(): return opened * (velocity * carried - spread * (beyond - behind))]
    reduce_sum x6 -> x0, other arithmetic: 3.6 us -> none  [face_flux(): return opened * (velocity * carried - spread * (beyond - behind))]
    unnamed x34 -> x22, local copies, waits for them, and re-layouts: 4.53 us -> 1.05 us
  transfers between devices with their start and end apart: 17 -> 8, of which waited for: 10 -> 3; matrix products, arithmetic and copies ran while one was open for 4% -> 0% of each run, Pallas kernels for 0% -> 14%
where the time goes in v2:
time: 47.2 us; the launch traced here: 46.4 us
  Pallas kernels  20.5 us (43%)
  waiting for transfers between devices  12.4 us (26%)
  starting transfers between devices  11 us (23%)
  local copies, waits for them, and re-layouts  1.05 us (2%)
  between operations  0.87 us (2%)
  other arithmetic  0.63 us (1%)
    pallas_call x7, Pallas kernels, run(): pl.pallas_call(body, out_shape=outs, in_specs=[pl.BlockSpec(memory_space=...  20.5 us
    ppermute x7, waiting for transfers between devices, swap(): received.append(lax.ppermute(x, axis, pairs))  9.79 us
    ppermute x7, starting transfers between devices, swap(): received.append(lax.ppermute(x, axis, pairs))  9.48 us
    ppermute x1, waiting for transfers between devices, program(): speeds = speeds + lax.ppermute(given[0], 'trc', [(0, 1), (1, 0)])  2.6 us
    ppermute x1, starting transfers between devices, program(): speeds = speeds + lax.ppermute(given[0], 'trc', [(0, 1), (1, 0)])  1.49 us
    unnamed x22, local copies, waits for them, and re-layouts  1.05 us
  transfers between devices with their start and end apart: 8, of which 3 were waited for; matrix products, arithmetic and copies ran while one was open for 0% of the time, Pallas kernels for 14%

profile of v2, /device:TPU:0, one launch (start us, length us, event | category | flops | bytes accessed | tf_op | source)
XLA Modules:
  0.0 46.4 jit_solution(11872578494565099252)
XLA Ops:
  0.7 2.8 %shard_map.95 = (f32[8,112,128]{2,1,0:T(8,128)}, f32[8,112,128]{2,1,0:T(8,128)}) custom-call(f32[1024,128]{1,0:T(8,128)} %bitcast.3, f32[1024,128]{1,0:T(8,128)} %bitcast.5, f32[8,8,128]{2,1,0:T(8,128)} %refs_2_.3, f32[8,8,128]{2,1,0:T(8,128)} %refs_3_.3, f32[8,8,128]{2,1,0:T(8,128)} %refs_4_.3, f32[8,8,128]{2,1,0:T(8,128)} %refs_5_.3, ...), custom_call_target="tpu_custom_call" | custom-call | tf_op jit(solution)/shard_map/pallas_call | solution.py:722
  3.6 0.0 copy-start.2
  3.6 1.0 %copy-done.2 = f32[8,112,128]{2,1,0:T(8,128)S(1)} copy-done((f32[8,112,128]{2,1,0:T(8,128)S(1)}, f32[8,112,128]{2,1,0:T(8,128)}, u32[]{:S(2)}) %copy-start.2) | copy-done | bytes 458776
  4.6 1.3 %shard_map.96 = (f32[7,128,128]{2,1,0:T(8,128)S(1)}, f32[16,16,16,128]{3,2,1,0:T(8,128)S(1)}, f32[12,12,16,128]{3,2,1,0:T(8,128)S(1)}, f32[5,14,14,1,128]{4,3,2,1,0:T(1,128)S(1)}, f32[3,14,1,128]{3,2,1,0:T(1,128)S(1)}) custom-call(f32[1024,128]{1,0:T(8,128)S(1)} %bitcast.4, f32[1024,128]{1,0:T(8,128)S(1)} %bitcast.6, f32[8,8,128]{2,1,0:T(8,128)S(1)} %copy-done.4, ...), custom_call_target="tpu_custom_call" | custom-call | tf_op jit(solution)/shard_map/pallas_call | solution.py:722
  5.9 0.6 %collective-permute-start.2 = (f32[7,128,128]{2,1,0:T(8,128)S(1)}, f32[7,128,128]{2,1,0:T(8,128)S(1)}, u32[]{:S(2)}, u32[]{:S(2)}) collective-permute-start(f32[7,128,128]{2,1,0:T(8,128)S(1)} %get-tuple-element.36), channel_id=1, source_target_pairs={{0,1},{1,0},{2,3},{3,2},{4,5},{5,4},{6,7},{7,6},{8,9},{9,8},{10,11... | collective-permute-start | bytes 1376264 | tf_op jit(solution)/shard_map/ppermute | solution.py:736
  6.5 0.7 %collective-permute-start.1 = (f32[8,112,128]{2,1,0:T(8,128)S(1)}, f32[8,112,128]{2,1,0:T(8,128)S(1)}, u32[]{:S(2)}, u32[]{:S(2)}) collective-permute-start(f32[8,112,128]{2,1,0:T(8,128)S(1)} %copy-done.10), channel_id=1, source_target_pairs={{4,8},{8,4},{5,9},{9,5},{6,10},{10,6},{7,11},{11,7},{20,24},{24,20... | collective-permute-start | bytes 1376264 | tf_op jit(solution)/shard_map/ppermute | solution.py:736
  7.2 5.5 %collective-permute-start = (f32[8,112,128]{2,1,0:T(8,128)S(1)}, f32[8,112,128]{2,1,0:T(8,128)S(1)}, u32[]{:S(2)}, u32[]{:S(2)}) collective-permute-start(f32[8,112,128]{2,1,0:T(8,128)S(1)} %copy-done.3), channel_id=1, source_target_pairs={{0,4},{4,0},{8,12},{12,8},{1,5},{5,1},{9,13},{13,9},{2,6},{6,2},{1... | collective-permute-start | bytes 1376264 | tf_op jit(solution)/shard_map/ppermute | solution.py:736
  12.6 0.0 collective-permute-done.2.refs_0_
  12.6 4.3 %shard_map.97 = (f32[16,16,16,128]{3,2,1,0:T(8,128)S(1)}, f32[12,12,16,128]{3,2,1,0:T(8,128)S(1)}, f32[5,14,14,1,128]{4,3,2,1,0:T(1,128)S(1)}, f32[12,12,16,128]...) custom-call(f32[7,128,128]{2,1,0:T(8,128)S(1)} %collective-permute-d, ...), custom_call_target="tpu_custom_call", output_to_operand_aliasing={{0}: (1, {}), {1}: (2, {}), {2}: (3, {})} | custom-call | tf_op jit(solution)/shard_map/pallas_call | solution.py:722
  16.9 0.0 collective-permute-done.1.refs_1_
  17.0 6.6 %collective-permute-done.refs_0_ = f32[8,112,128]{2,1,0:T(8,128)S(1)} collective-permute-done((f32[8,112,128]{2,1,0:T(8,128)S(1)}, f32[8,112,128]{2,1,0:T(8,128)S(1)}, u32[]{:S(2)}, u32[]{:S(2)}) %collective-permute-start) | collective-permute-done | bytes 458784 | tf_op jit(solution)/shard_map/ppermute | solution.py:736
  23.5 0.1 collective-permute-start.3
  23.6 2.2 %shard_map.99 = (f32[16,16,16,128]{3,2,1,0:T(8,128)S(1)}, f32[12,12,16,128]{3,2,1,0:T(8,128)S(1)}, f32[5,14,14,1,128]{4,3,2,1,0:T(1,128)S(1)}, f32[3,14,1,128]{3,2,1,0:T(1,128)S(1)}, f32[12,12,16,128]{3,2,1,0:T(8,128)S(1)}) custom-call(f32[8,112,128]{2,1,0:T(8,128)S(1)} %collective-permute-d, ...), custom_call_target="tpu_custom_call", output_to_operand_aliasing={{0}: (2, {}), {1}: (3, {}), {2}: (4, {}), {3}: (5, {}), {4}... | custom-call | tf_op jit(solution)/shard_map/pallas_call | solution.py:722
  25.8 0.0 collective-permute-done.3.refs_0_
  25.9 5.0 %shard_map.100 = (f32[16,16,16,128]{3,2,1,0:T(8,128)S(1)}, f32[5,14,14,1,128]{4,3,2,1,0:T(1,128)S(1)}, f32[12,12,16,128]{3,2,1,0:T(8,128)S(1)}, f32[8,8,16,128]{...) custom-call(f32[2,2,112,128]{3,2,1,0:T(8,128)S(1)} %collective-permu, ...), custom_call_target="tpu_custom_call", output_to_operand_aliasing={{0}: (3, {}), {1}: (4, {}), {2}: (5, {})} | custom-call | tf_op jit(solution)/shard_map/pallas_call | solution.py:722
  30.9 1.8 %collective-permute-start.4 = (f32[8,2,16,128]{3,2,1,0:T(8,128)S(1)}, f32[8,2,16,128]{3,2,1,0:T(8,128)S(1)}, u32[]{:S(2)}, u32[]{:S(2)}) collective-permute-start(f32[8,2,16,128]{3,2,1,0:T(8,128)S(1)} %get-tuple-element.60), channel_id=1, source_target_pairs={{0,4},{4,0},{8,12},{12,8},{1,5},{5,1},{9,13},{13,9},{2,6},{6,2},{1... | collective-permute-start | bytes 393224 | tf_op jit(solution)/shard_map/ppermute | solution.py:736
  32.7 0.7 %collective-permute-start.5 = (f32[8,2,16,128]{3,2,1,0:T(8,128)S(1)}, f32[8,2,16,128]{3,2,1,0:T(8,128)S(1)}, u32[]{:S(2)}, u32[]{:S(2)}) collective-permute-start(f32[8,2,16,128]{3,2,1,0:T(8,128)S(1)} %get-tuple-element.61), channel_id=1, source_target_pairs={{4,8},{8,4},{5,9},{9,5},{6,10},{10,6},{7,11},{11,7},{20,24},{24,20... | collective-permute-start | bytes 393224 | tf_op jit(solution)/shard_map/ppermute | solution.py:736
  33.3 0.3 collective-permute-start.6
  33.6 3.2 %collective-permute-done.4.refs_11_ = f32[8,2,16,128]{3,2,1,0:T(8,128)S(1)} collective-permute-done((f32[8,2,16,128]{3,2,1,0:T(8,128)S(1)}, f32[8,2,16,128]{3,2,1,0:T(8,128)S(1)}, u32[]{:S(2)}, u32[]{:S(2)}) %collective-permute-start.4) | collective-permute-done | bytes 131104 | tf_op jit(solution)/shard_map/ppermute | solution.py:736
  36.8 0.0 collective-permute-done.6.refs_13_
  36.8 4.9 %shard_map.101 = (f32[1024,128]{1,0:T(8,128)}, f32[3,4,8,128]{3,2,1,0:T(8,128)S(1)}, f32[3,4,8,128]{3,2,1,0:T(8,128)S(1)}) custom-call(f32[16,16,16,128]{3,2,1,0:T(8,128)S(1)} %get-tuple-element.50.refs_0_, f32[5,14,14,1,128]{4,3,2,1,0:T(1,128)S(1)} %get-tuple-element.51.refs_1_, f32[3,14,1,128]{3,2,1,0:T(1,128)S(1)} %get-tuple-element.46.refs_2_, ...), custom_call_target="tpu_custom_call" | custom-call | tf_op jit(solution)/shard_map/pallas_call | solution.py:722
  41.7 1.5 %collective-permute-start.7 = (f32[3,4,8,128]{3,2,1,0:T(8,128)S(1)}, f32[3,4,8,128]{3,2,1,0:T(8,128)S(1)}, u32[]{:S(2)}, u32[]{:S(2)}) collective-permute-start(f32[3,4,8,128]{3,2,1,0:T(8,128)S(1)} %get-tuple-element.65), channel_id=1, source_target_pairs={{0,2},{2,0},{1,3},{3,1},{4,6},{6,4},{5,7},{7,5},{8,10},{10,8},{9,1... | collective-permute-start | bytes 147464 | tf_op jit(solution)/shard_map/ppermute | solution.py:814
  43.2 2.6 %collective-permute-done.7 = f32[3,4,8,128]{3,2,1,0:T(8,128)S(1)} collective-permute-done((f32[3,4,8,128]{3,2,1,0:T(8,128)S(1)}, f32[3,4,8,128]{3,2,1,0:T(8,128)S(1)}, u32[]{:S(2)}, u32[]{:S(2)}) %collective-permute-start.7) | collective-permute-done | bytes 49184 | tf_op jit(solution)/shard_map/ppermute | solution.py:814
  45.8 0.6 %add.3 = f32[3,4,8,128]{3,2,1,0:T(8,128)} add(f32[3,4,8,128]{3,2,1,0:T(8,128)S(1)} %get-tuple-element.64, f32[3,4,8,128]{3,2,1,0:T(8,128)S(1)} %collective-permute-done.7) | non-fusion elementwise | flops 12288 | bytes 147456 | tf_op jit(solution)/shard_map/add | solution.py:814
  (22 shorter events, 0.1 us)
Async XLA Ops:
  0.6 2.9 %copy-start.9 = (s32[8,128]{1,0:T(8,128)S(1)}, s32[8,128]{1,0:T(8,128)}, u32[]{:S(2)}) copy-start(s32[8,128]{1,0:T(8,128)} %refs_7_.3) | copy-start | bytes 12292
  0.6 2.9 %copy-start.8 = (f32[8,8,128]{2,1,0:T(8,128)S(1)}, f32[8,8,128]{2,1,0:T(8,128)}, u32[]{:S(2)}) copy-start(f32[8,8,128]{2,1,0:T(8,128)} %refs_6_.3) | copy-start | bytes 98308
  0.7 2.9 %copy-start.7 = (f32[8,8,128]{2,1,0:T(8,128)S(1)}, f32[8,8,128]{2,1,0:T(8,128)}, u32[]{:S(2)}) copy-start(f32[8,8,128]{2,1,0:T(8,128)} %refs_5_.3) | copy-start | bytes 98308
  0.7 2.9 %copy-start.6 = (f32[8,8,128]{2,1,0:T(8,128)S(1)}, f32[8,8,128]{2,1,0:T(8,128)}, u32[]{:S(2)}) copy-start(f32[8,8,128]{2,1,0:T(8,128)} %refs_4_.3) | copy-start | bytes 98308
  0.7 2.9 %copy-start.5 = (f32[8,8,128]{2,1,0:T(8,128)S(1)}, f32[8,8,128]{2,1,0:T(8,128)}, u32[]{:S(2)}) copy-start(f32[8,8,128]{2,1,0:T(8,128)} %refs_3_.3) | copy-start | bytes 98308
  0.7 2.9 %copy-start.4 = (f32[8,8,128]{2,1,0:T(8,128)S(1)}, f32[8,8,128]{2,1,0:T(8,128)}, u32[]{:S(2)}) copy-start(f32[8,8,128]{2,1,0:T(8,128)} %refs_2_.3) | copy-start | bytes 98308
  0.7 2.9 %copy-start.1 = (f32[16,8,8,128]{3,2,1,0:T(8,128)S(1)}, f32[16,8,8,128]{3,2,1,0:T(8,128)}, u32[]{:S(2)}) copy-start(f32[16,8,8,128]{3,2,1,0:T(8,128)} %param.9) | copy-start | bytes 1572868
  0.7 2.9 %copy-start = (f32[16,8,8,128]{3,2,1,0:T(8,128)S(1)}, f32[16,8,8,128]{3,2,1,0:T(8,128)}, u32[]{:S(2)}) copy-start(f32[16,8,8,128]{3,2,1,0:T(8,128)} %param.8) | copy-start | bytes 1572868
  3.6 1.0 %copy-start.2 = (f32[8,112,128]{2,1,0:T(8,128)S(1)}, f32[8,112,128]{2,1,0:T(8,128)}, u32[]{:S(2)}) copy-start(f32[8,112,128]{2,1,0:T(8,128)} %get-tuple-element.34.refs_8_) | copy-start | bytes 1376260
  4.6 1.8 %copy-start.10 = (f32[8,112,128]{2,1,0:T(8,128)S(1)}, f32[8,112,128]{2,1,0:T(8,128)}, u32[]{:S(2)}) copy-start(f32[8,112,128]{2,1,0:T(8,128)} %get-tuple-element.35) | copy-start | bytes 1376260
  4.6 2.5 %copy-start.3 = (f32[8,112,128]{2,1,0:T(8,128)S(1)}, f32[8,112,128]{2,1,0:T(8,128)}, u32[]{:S(2)}) copy-start(f32[8,112,128]{2,1,0:T(8,128)} %get-tuple-element.34.refs_8_) | copy-start | bytes 1376260
  5.9 6.7 %collective-permute-start.2 = (f32[7,128,128]{2,1,0:T(8,128)S(1)}, f32[7,128,128]{2,1,0:T(8,128)S(1)}, u32[]{:S(2)}, u32[]{:S(2)}) collective-permute-start(f32[7,128,128]{2,1,0:T(8,128)S(1)} %get-tuple-element.36), channel_id=1, source_target_pairs={{0,1},{1,0},{2,3},{3,2},{4,5},{5,4},{6,7},{7,6},{8,9},{9,8},{10,11... | collective-permute-start | bytes 1376264 | tf_op jit(solution)/shard_map/ppermute | solution.py:736
  6.5 10.5 %collective-permute-start.1 = (f32[8,112,128]{2,1,0:T(8,128)S(1)}, f32[8,112,128]{2,1,0:T(8,128)S(1)}, u32[]{:S(2)}, u32[]{:S(2)}) collective-permute-start(f32[8,112,128]{2,1,0:T(8,128)S(1)} %copy-done.10), channel_id=1, source_target_pairs={{4,8},{8,4},{5,9},{9,5},{6,10},{10,6},{7,11},{11,7},{20,24},{24,20... | collective-permute-start | bytes 1376264 | tf_op jit(solution)/shard_map/ppermute | solution.py:736
  7.2 16.3 %collective-permute-start = (f32[8,112,128]{2,1,0:T(8,128)S(1)}, f32[8,112,128]{2,1,0:T(8,128)S(1)}, u32[]{:S(2)}, u32[]{:S(2)}) collective-permute-start(f32[8,112,128]{2,1,0:T(8,128)S(1)} %copy-done.3), channel_id=1, source_target_pairs={{0,4},{4,0},{8,12},{12,8},{1,5},{5,1},{9,13},{13,9},{2,6},{6,2},{1... | collective-permute-start | bytes 1376264 | tf_op jit(solution)/shard_map/ppermute | solution.py:736
  23.5 2.3 %collective-permute-start.3 = (f32[2,2,112,128]{3,2,1,0:T(8,128)S(1)}, f32[2,2,112,128]{3,2,1,0:T(8,128)S(1)}, u32[]{:S(2)}, u32[]{:S(2)}) collective-permute-start(f32[2,2,112,128]{3,2,1,0:T(8,128)S(1)} %shard_map.98), channel_id=1, source_target_pairs={{0,1},{1,0},{2,3},{3,2},{4,5},{5,4},{6,7},{7,6},{8,9},{9,8},{10,11... | collective-permute-start | bytes 688136 | tf_op jit(solution)/shard_map/ppermute | solution.py:736
  30.9 5.9 %collective-permute-start.4 = (f32[8,2,16,128]{3,2,1,0:T(8,128)S(1)}, f32[8,2,16,128]{3,2,1,0:T(8,128)S(1)}, u32[]{:S(2)}, u32[]{:S(2)}) collective-permute-start(f32[8,2,16,128]{3,2,1,0:T(8,128)S(1)} %get-tuple-element.60), channel_id=1, source_target_pairs={{0,4},{4,0},{8,12},{12,8},{1,5},{5,1},{9,13},{13,9},{2,6},{6,2},{1... | collective-permute-start | bytes 393224 | tf_op jit(solution)/shard_map/ppermute | solution.py:736
  32.7 4.1 %collective-permute-start.5 = (f32[8,2,16,128]{3,2,1,0:T(8,128)S(1)}, f32[8,2,16,128]{3,2,1,0:T(8,128)S(1)}, u32[]{:S(2)}, u32[]{:S(2)}) collective-permute-start(f32[8,2,16,128]{3,2,1,0:T(8,128)S(1)} %get-tuple-element.61), channel_id=1, source_target_pairs={{4,8},{8,4},{5,9},{9,5},{6,10},{10,6},{7,11},{11,7},{20,24},{24,20... | collective-permute-start | bytes 393224 | tf_op jit(solution)/shard_map/ppermute | solution.py:736
  33.3 3.5 %collective-permute-start.6 = (f32[2,8,16,128]{3,2,1,0:T(8,128)S(1)}, f32[2,8,16,128]{3,2,1,0:T(8,128)S(1)}, u32[]{:S(2)}, u32[]{:S(2)}) collective-permute-start(f32[2,8,16,128]{3,2,1,0:T(8,128)S(1)} %get-tuple-element.62), channel_id=1, source_target_pairs={{0,1},{1,0},{2,3},{3,2},{4,5},{5,4},{6,7},{7,6},{8,9},{9,8},{10,11... | collective-permute-start | bytes 393224 | tf_op jit(solution)/shard_map/ppermute | solution.py:736
  41.7 4.1 %collective-permute-start.7 = (f32[3,4,8,128]{3,2,1,0:T(8,128)S(1)}, f32[3,4,8,128]{3,2,1,0:T(8,128)S(1)}, u32[]{:S(2)}, u32[]{:S(2)}) collective-permute-start(f32[3,4,8,128]{3,2,1,0:T(8,128)S(1)} %get-tuple-element.65), channel_id=1, source_target_pairs={{0,2},{2,0},{1,3},{3,1},{4,6},{6,4},{5,7},{7,5},{8,10},{10,8},{9,1... | collective-permute-start | bytes 147464 | tf_op jit(solution)/shard_map/ppermute | solution.py:814

commit v3 on v2

--- a/solution.py
+++ b/solution.py
@@ -12,8 +12,7 @@
 E = 2
 W = 3
 NF = 5
-YC = 8
-MIB = 60
+MIB = 4
 FPAD = 16
 
 
@@ -114,7 +113,7 @@
             dd_b = e * up + down_a - dm_b
             if f >= 2:
                 emit(f - 2, n_a + p_b + dd_a - dd_b)
-            if f - 1 < n:
+            if emit_speed is not None and f - 1 < n:
                 emit_speed(f - 1, g_b * carried)
             dd_a = dd_b
         down_a = e * down
@@ -168,12 +167,14 @@
     def __init__(self, f_ref, d_ref, level0):
         self.f, self.d, self.level0 = f_ref, d_ref, level0
 
-    def at(self, direction, k, c):
-        depth = self.d[direction, W + c]
+    def open(self, direction, k, c):
         level = (self.level0 + k).astype(jnp.float32)
         if direction == 2:
             level = jnp.where(level >= 1.0, level, 1e9)
-        is_open = depth > level
+        return self.d[direction, W + c] > level
+
+    def at(self, direction, k, c):
+        is_open = self.open(direction, k, c)
         speed = self.f[direction, W + k, W + c]
         mix = self.f[(3, 3, 4)[direction], W + k, W + c]
         return jnp.where(is_open, speed, 0.0), jnp.where(is_open, mix, 0.0), is_open
@@ -191,60 +192,49 @@
         de[1, W + c] = jnp.where(lane0, 0.0, jnp.minimum(pltpu.roll(here, 1, 1), here))
 
 
-def fetch(pairs, sem):
-    copies = [pltpu.make_async_copy(a, b, sem.at[i]) for i, (a, b) in enumerate(pairs)]
-    for c in copies:
-        c.start()
-    return copies
-
-
 def edges_body(dims, n_tile, *refs):
     T, L, C, _ = dims
     sources, tile_out, (q_ref, l_ref, f_ref, d_ref, sem) = refs[:8], refs[8 : 8 + n_tile], refs[8 + n_tile :]
     targets = [q_ref, l_ref] + [f_ref.at[f] for f in range(NF)] + [d_ref]
-    copies = fetch(zip(sources, targets), sem)
-    for c in copies[2:] + copies[:2]:
+    order = [0] + list(range(2, 8)) + [1]
+    copies = [pltpu.make_async_copy(sources[i], targets[i], sem.at[i]) for i in order]
+    for c in copies:
+        c.start()
+    for c in copies[1:-1] + copies[:1]:
         c.wait()
     tile_even, _ = parities()
 
-    def slab(ref, k, c):
-        return ref[pl.ds(k * C + c, T, stride=L * C), :]
-
     for phase, out in enumerate(tile_out):
 
         def send_tile(high, out=out):
             q0 = C - H if high else 0
-            l0 = C - E if high else 0
             f0 = C - W if high else 0
 
             def level(k, carry):
                 for j in range(H):
-                    out[k, j * T : (j + 1) * T, :] = slab(q_ref, k, q0 + j)
-                for j in range(E):
-                    out[k, (H + j) * T : (H + j + 1) * T, :] = slab(l_ref, k, l0 + j)
-                base = (H + E) * T
+                    out[k, j * T : (j + 1) * T, :] = q_ref[pl.ds(k * C + q0 + j, T, stride=L * C), :]
                 for f in range(NF):
-                    out[k, base + W * f : base + W * (f + 1), :] = f_ref[f, k, f0 : f0 + W, :]
-                out[k, base + W * NF : base + W * NF + 1, :] = d_ref[f0 : f0 + 1, :].astype(jnp.float32)
+                    r = H * T + W * f
+                    out[k, r : r + W, :] = f_ref[f, k, f0 : f0 + W, :]
+                r = H * T + W * NF
+                out[k, r : r + 1, :] = d_ref[f0 : f0 + 1, :].astype(jnp.float32)
                 return carry
 
             lax.fori_loop(0, L, level, 0, unroll=2)
-            base = (H + E) * T + W * NF
+            r = H * T + W * NF
             for j in range(1, W):
-                out[j, base : base + 1, :] = d_ref[f0 + j : f0 + j + 1, :].astype(jnp.float32)
+                out[j, r : r + 1, :] = d_ref[f0 + j : f0 + j + 1, :].astype(jnp.float32)
 
         by_parity(tile_even, phase, send_tile)
-
-
-def own_body(dims, n_lev, *refs):
+    copies[-1].wait()
+
+
+def own_body(dims, n_tile, n_lev, *refs):
     T, L, C, Y = dims
-    sources, lev_out = refs[:8], refs[9 : 9 + n_lev]
-    qe, le, fe, de, q_ref, l_ref, f_ref, d_ref, sem = refs[9 + n_lev :]
-    targets = [q_ref, l_ref] + [f_ref.at[f] for f in range(NF)] + [d_ref]
-    copies = fetch(zip(sources, targets), sem)
-    for c in copies[2:] + copies[:2]:
-        c.wait()
-    _, lev_even = parities()
+    q_ref, l_ref, f_ref, d_ref = refs[:4]
+    tile_out, lev_out = refs[4 : 4 + n_tile], refs[4 + n_tile : 4 + n_tile + n_lev]
+    qe, le, fe, de = refs[4 + n_tile + n_lev :]
+    tile_even, lev_even = parities()
     zero = jnp.zeros((T, Y), jnp.float32)
     zero_row = jnp.zeros((1, Y), jnp.float32)
 
@@ -260,6 +250,18 @@
     for c in range(C):
         de[2, W + c] = d_ref[c : c + 1, :].astype(jnp.float32)
     depth_rows(de, range(C))
+
+    for phase, out in enumerate(tile_out):
+
+        def send_tile(high, out=out):
+            def level(k, carry):
+                for j in range(E):
+                    out[k, j] = le[E + k, E + (C - E if high else 0) + j]
+                return carry
+
+            lax.fori_loop(0, L, level, 0, unroll=2)
+
+        by_parity(tile_even, phase, send_tile)
 
     for phase, out in enumerate(lev_out):
 
@@ -304,11 +306,29 @@
         by_parity(lev_even, phase, blank_lev)
 
 
-def inner_body(dims, n_lev, *refs):
+def inner_y_body(dims, qe, fe, de, me, yu, yd, yc):
+    T, L, C, Y = dims
+    fields = Fields(fe, de, lax.axis_index("lev") * L)
+    ends = lanes(T, Y)
+
+    def own_y(k, carry):
+        for c in range(C):
+            u = qe[H + k, H + c]
+            v, m, _ = fields.at(1, k, c)
+            d, carried, coefs = along_values(u, v, ends)
+            yu[k, c], yd[k, c] = coefs()
+            yc[k, c] = carried
+            me[E + k, E + c] = u + along_forward(d, carried, v, m)
+        return carry
+
+    lax.fori_loop(0, L, own_y, 0)
+
+
+def inner_v_body(dims, n_lev, *refs):
     T, L, C, Y = dims
     lev_in = refs[:n_lev]
-    de = refs[n_lev + 3]
-    qe, le, fe, me, yu, yd, yc, vu, vd, vc = refs[n_lev + 4 :]
+    de = refs[n_lev + 4]
+    qe, le, fe, me, vu, vd, vc = refs[n_lev + 5 :]
     _, lev_even = parities()
     zero = jnp.zeros((T, Y), jnp.float32)
 
@@ -339,38 +359,21 @@
     fields = Fields(fe, de, lax.axis_index("lev") * L)
     ends = lanes(T, Y)
 
-    def own_y(i, carry):
-        k = i // (C // YC)
-        c0 = (i % (C // YC)) * YC
-        for j in range(YC):
-            c = c0 + j
-            u = qe[H + k, H + c]
-            v, m, _ = fields.at(1, k, c)
-            d, carried, coefs = along_values(u, v, ends)
-            yu[k, c], yd[k, c] = coefs()
-            yc[k, c] = carried
-            me[E + k, E + c] = u + along_forward(d, carried, v, m)
-        return carry
-
-    lax.fori_loop(0, L * (C // YC), own_y, 0)
-
     for phase in range(2):
         if phase < n_lev:
             high = lev_even if phase == 0 else jnp.logical_not(lev_even)
             k0 = jnp.where(high, L, -E)
 
             def beside(i, carry, k0=k0):
-                k = k0 + i // (C // YC)
-                c0 = (i % (C // YC)) * YC
-                for j in range(YC):
-                    c = c0 + j
+                k = k0 + i
+                for c in range(C):
                     u = qe[H + k, H + c]
                     v, m, _ = fields.at(1, k, c)
                     d, carried, _ = along_values(u, v, ends)
                     me[E + k, E + c] = u + along_forward(d, carried, v, m)
                 return carry
 
-            lax.fori_loop(0, E * (C // YC), beside, 0)
+            lax.fori_loop(0, E, beside, 0)
         else:
 
             def blank(high):
@@ -419,22 +422,19 @@
 def beside_body(dims, n_tile, *refs):
     T, L, C, Y = dims
     tile_in = refs[:n_tile]
-    qe, le, fe, de, me = refs[n_tile + 5 :]
+    qe, fe, de, me, zc = refs[n_tile + 4 :]
     tile_even, _ = parities()
     zero = jnp.zeros((T, Y), jnp.float32)
     zero_row = jnp.zeros((1, Y), jnp.float32)
 
     def place_tile(source, high):
         q0 = H + C if high else 0
-        l0 = E + C if high else 0
         f0 = W + C if high else 0
 
         def level(k, carry):
             for j in range(H):
                 qe[H + k, q0 + j] = zero if source is None else source[k, j * T : (j + 1) * T, :]
-            for j in range(E):
-                le[E + k, l0 + j] = zero if source is None else source[k, (H + j) * T : (H + j + 1) * T, :]
-            base = (H + E) * T
+            base = H * T
             for f in range(NF):
                 for j in range(W):
                     r = base + W * f + j
@@ -442,7 +442,7 @@
             return carry
 
         lax.fori_loop(0, L, level, 0, unroll=4)
-        base = (H + E) * T + W * NF
+        base = H * T + W * NF
         for j in range(W):
             de[2, f0 + j] = zero_row if source is None else source[j, base : base + 1, :]
 
@@ -471,8 +471,12 @@
         def emit(c, value):
             me[E + k, c] = me[E + k, c] + value
 
+        def keep(c, coefs, carried):
+            if 0 <= c - E < C:
+                zc[k, c - E] = carried
+
         forward_chain(
-            C + 2 * E, lambda c: qe[H + k, H - E + c], lambda c: fields.at(0, k, c - E)[:2], emit
+            C + 2 * E, lambda c: qe[H + k, H - E + c], lambda c: fields.at(0, k, c - E)[:2], emit, keep
         )
         return carry
 
@@ -481,11 +485,9 @@
 
 def late_body(dims, n_tile, n_lev, *refs):
     T, L, C, Y = dims
-    corner_in = refs[:n_lev]
-    le, de = refs[n_lev : n_lev + 2]
-    qe, fe, me, mc_ref, sp_ref = refs[n_lev + 5 : n_lev + 10]
-    tile_out = refs[n_lev + 10 : n_lev + 10 + n_tile]
-    lev_out = refs[n_lev + 10 + n_tile :]
+    corner_in, tile_in = refs[:n_lev], refs[n_lev : n_lev + n_tile]
+    de = refs[n_lev + n_tile]
+    qe, le, fe, me, mc_ref, sp_ref, *tile_out = refs[n_lev + n_tile + 5 :]
     tile_even, lev_even = parities()
     zero = jnp.zeros((T, Y), jnp.float32)
     zero_row = jnp.zeros((1, Y), jnp.float32)
@@ -499,7 +501,7 @@
                 col = (H + C + i) if tile_high else (H - E + i)
                 qe[q_lev, col] = zero if source is None else source[j, s * T : (s + 1) * T, :]
                 for f in range(NF):
-                    r = (H + E) * T + W * f + (i if tile_high else W - E + i)
+                    r = H * T + W * f + (i if tile_high else W - E + i)
                     col = (W + C + i) if tile_high else (W - E + i)
                     fe[f, f_lev, col] = zero_row if source is None else source[j, r : r + 1, :]
 
@@ -512,6 +514,18 @@
 
             by_parity(lev_even, phase, corner)
 
+    def place_tile(source, high):
+        def level(k, carry):
+            for j in range(E):
+                le[E + k, (E + C if high else 0) + j] = zero if source is None else source[k, j]
+            return carry
+
+        lax.fori_loop(0, L, level, 0, unroll=2)
+
+    for phase in range(2):
+        source = tile_in[phase] if phase < n_tile else None
+        by_parity(tile_even, phase, lambda high, s=source: place_tile(s, high))
+
     fields = Fields(fe, de, lax.axis_index("lev") * L)
 
     for phase in range(n_lev):
@@ -543,7 +557,7 @@
     def done(k, c, value):
         mc_ref[k, c] = value
 
-    adjoint(dims, fields, me, E, le, mc_ref, done, sp_ref)
+    adjoint(dims, fields, me, E, le, mc_ref, done, parts(C)[0], sp_ref)
 
     for phase, out in enumerate(tile_out):
 
@@ -553,9 +567,23 @@
                     out[k, j] = mc_ref[k, (C - E if high else 0) + j]
                 return carry
 
-            lax.fori_loop(0, L, level, 0)
+            lax.fori_loop(0, L, level, 0, unroll=2)
 
         by_parity(tile_even, phase, send_tile)
+
+
+def late_inner_body(dims, *refs):
+    _, L, C, _ = dims
+    le, fe, de, me = refs[:4]
+    mc_ref, sp_ref, *lev_out = refs[6:]
+    _, lev_even = parities()
+
+    def done(k, c, value):
+        mc_ref[k, c] = value
+
+    fields = Fields(fe, de, lax.axis_index("lev") * L)
+    adjoint(dims, fields, me, E, le, mc_ref, done, parts(C)[1], sp_ref)
+
     for phase, out in enumerate(lev_out):
 
         def send_lev(high, out=out):
@@ -564,62 +592,75 @@
                     out[j, c] = mc_ref[(L - E if high else 0) + j, c]
                 return carry
 
-            lax.fori_loop(0, C, column, 0)
+            lax.fori_loop(0, C, column, 0, unroll=2)
 
         by_parity(lev_even, phase, send_lev)
 
 
-def adjoint(dims, fields, u_ref, uo, l_ref, acc_ref, done, speed_ref, kept=None):
-    T, L, C, Y = dims
+def parts(C):
+    edge = (list(range(E)) + list(range(C - E, C)), [(0, E), (C - E, E)], lambda i: jnp.where(i < E, i, C - 2 * E + i))
+    inner = (list(range(E, C - E)), [(E, C - 2 * E)] if C > 2 * E else [], lambda i: E + i)
+    return edge, inner
+
+
+def adjoint(dims, fields, u_ref, uo, l_ref, acc_ref, done, part, speed_ref=None, kept=None, passes="yzv"):
+    T, L, _, Y = dims
     ends = lanes(T, Y)
-    yu, yd, yc, vu, vd, vc = kept or [None] * 6
+    yu, yd, vu, vd = kept or [None] * 4
+    columns, runs, column_of = part
 
     def store_speed(direction, k, c, is_open, value):
-        row = jnp.sum(value, axis=0, keepdims=True)
-        speed_ref[direction, k, pl.ds(c, 1), :] = jnp.where(is_open, row, 0.0)
-
-    def along(i, carry):
-        k = i // (C // YC)
-        c0 = (i % (C // YC)) * YC
-        for j in range(YC):
-            c = c0 + j
+        if speed_ref is not None:
+            row = jnp.sum(value, axis=0, keepdims=True)
+            speed_ref[direction, k, pl.ds(c, 1), :] = jnp.where(is_open, row, 0.0)
+
+    def along(k, carry):
+        for c in columns:
             l = l_ref[E + k, E + c]
             v, m, is_open = fields.at(1, k, c)
             if kept is None:
                 _, carried, coefs = along_values(u_ref[uo + k, uo + c], v, ends)
                 up, down = coefs()
             else:
-                up, down, carried = yu[k, c], yd[k, c], yc[k, c]
+                up, down = yu[k, c], yd[k, c]
             add, g = along_adjoint(l, v, m, up, down, ends)
             acc_ref[k, c] = l + add
-            store_speed(1, k, c, is_open, g * carried)
-        return carry
-
-    lax.fori_loop(0, L * (C // YC), along, 0)
+            if speed_ref is not None:
+                store_speed(1, k, c, is_open, g * carried)
+        return carry
+
+    if "y" in passes:
+        lax.fori_loop(0, L, along, 0, unroll=2)
 
     def level_z(k, carry):
-        opened = {}
-
-        def co(c):
-            v, m, opened[c] = fields.at(0, k, c)
-            return v, m
-
-        def emit(c, value):
-            acc_ref[k, c] = acc_ref[k, c] + value
-
-        adjoint_chain(
-            C,
-            fresh_limits(lambda c: u_ref[uo + k, uo + c]),
-            lambda c: l_ref[E + k, E + c],
-            co,
-            emit,
-            lambda c, value: store_speed(0, k, c, opened[c], value),
-        )
-        return carry
-
-    lax.fori_loop(0, L, level_z, 0)
-
-    def column_v(c, carry):
+        for c0, n in runs:
+            opened = {}
+
+            def co(c, c0=c0, opened=opened):
+                v, m, opened[c] = fields.at(0, k, c0 + c)
+                return v, m
+
+            def emit(c, value, c0=c0):
+                acc_ref[k, c0 + c] = acc_ref[k, c0 + c] + value
+
+            def speed(c, value, c0=c0, opened=opened):
+                store_speed(0, k, c0 + c, opened[c], value)
+
+            adjoint_chain(
+                n,
+                fresh_limits(lambda c, c0=c0: u_ref[uo + k, uo + c0 + c]),
+                lambda c, c0=c0: l_ref[E + k, E + c0 + c],
+                co,
+                emit,
+                speed if speed_ref is not None else None,
+            )
+        return carry
+
+    if "z" in passes:
+        lax.fori_loop(0, L, level_z, 0)
+
+    def column_v(i, carry):
+        c = column_of(i)
         opened = {}
 
         def co(k):
@@ -634,8 +675,7 @@
         else:
 
             def limits(f, v):
-                k = f - 1
-                return vu[1 + k, c], vd[1 + k, c], vc[k, c] if 0 <= k < L else None
+                return vu[f, c], vd[f, c], None
 
         adjoint_chain(
             L,
@@ -643,31 +683,62 @@
             lambda k: l_ref[E + k, E + c],
             co,
             emit,
-            lambda k, value: store_speed(2, k, c, opened[k], value),
+            (lambda k, value: store_speed(2, k, c, opened[k], value)) if speed_ref is not None else None,
         )
         return carry
 
-    lax.fori_loop(0, C, column_v, 0)
-
-
-def start_body(dims, n_tile, n_lev, *refs):
-    T, L, C, Y = dims
-    qe, fe, de, mc_ref, late_ref = refs[:5]
-    kept = refs[5:11]
-    tile_in = refs[11 : 11 + n_tile]
-    lev_in = refs[11 + n_tile : 11 + n_tile + n_lev]
-    out_ref, sp_out, *rest = refs[11 + n_tile + n_lev :]
-    given_ref = rest[0] if len(rest) == 4 else None
-    le, acc, sp_ref = rest[-3:]
-    tile_even, lev_even = parities()
-    zero = jnp.zeros((T, Y), jnp.float32)
+    if "v" in passes:
+        lax.fori_loop(0, len(columns), column_v, 0)
+
+
+def start_inner_body(dims, *refs):
+    _, L, C, _ = dims
+    qe, fe, de, mc_ref, yu, yd, le, acc = refs
 
     def own(k, carry):
         for c in range(C):
             le[E + k, E + c] = mc_ref[k, c]
         return carry
 
-    lax.fori_loop(0, L, own, 0)
+    lax.fori_loop(0, L, own, 0, unroll=2)
+    fields = Fields(fe, de, lax.axis_index("lev") * L)
+    adjoint(dims, fields, qe, H, le, acc, None, parts(C)[1], kept=(yu, yd, None, None), passes="yz")
+
+
+def start_levels_body(dims, n_lev, *refs):
+    T, L, C, Y = dims
+    fe, de, vu, vd, acc = refs[:5]
+    lev_in = refs[5 : 5 + n_lev]
+    le, out_ref = refs[6 + n_lev :]
+    _, lev_even = parities()
+    zero = jnp.zeros((T, Y), jnp.float32)
+
+    def place_lev(source, high):
+        def column(c, carry):
+            for j in range(E):
+                le[(E + L if high else 0) + j, E + c] = zero if source is None else source[j, c]
+            return carry
+
+        lax.fori_loop(0, C, column, 0, unroll=2)
+
+    for phase in range(2):
+        source = lev_in[phase] if phase < n_lev else None
+        by_parity(lev_even, phase, lambda high, s=source: place_lev(s, high))
+
+    def done(k, c, value):
+        out_ref[pl.ds(k * C + c, T, stride=L * C), :] = value
+
+    fields = Fields(fe, de, lax.axis_index("lev") * L)
+    adjoint(dims, fields, None, H, le, acc, done, parts(C)[1], kept=(None, None, vu, vd), passes="v")
+
+
+def speeds_body(dims, n_tile, *refs):
+    T, L, C, Y = dims
+    fe, de, late_ref, zc, yc, vc = refs[:6]
+    tile_in = refs[6 : 6 + n_tile]
+    le, *outs, sp_ref = refs[7 + n_tile :]
+    tile_even, _ = parities()
+    zero = jnp.zeros((T, Y), jnp.float32)
 
     def place_tile(source, high):
         def level(k, carry):
@@ -675,28 +746,27 @@
                 le[E + k, (E + C if high else 0) + j] = zero if source is None else source[k, j]
             return carry
 
-        lax.fori_loop(0, L, level, 0)
-
-    def place_lev(source, high):
-        def column(c, carry):
-            for j in range(E):
-                le[(E + L if high else 0) + j, E + c] = zero if source is None else source[j, c]
-            return carry
-
-        lax.fori_loop(0, C, column, 0)
+        lax.fori_loop(0, L, level, 0, unroll=2)
 
     for phase in range(2):
-        by_parity(
-            tile_even, phase, lambda high, p=phase: place_tile(tile_in[p] if p < n_tile else None, high)
-        )
-        by_parity(lev_even, phase, lambda high, p=phase: place_lev(lev_in[p] if p < n_lev else None, high))
-
-    def done(k, c, value):
-        out_ref[pl.ds(k * C + c, T, stride=L * C), :] = value
-
-    adjoint(dims, Fields(fe, de, lax.axis_index("lev") * L), qe, H, le, acc, done, sp_ref, kept)
-    if given_ref is None:
-        sp_out[...] = sp_ref[...] + late_ref[...]
+        source = tile_in[phase] if phase < n_tile else None
+        by_parity(tile_even, phase, lambda high, s=source: place_tile(s, high))
+
+    fields = Fields(fe, de, lax.axis_index("lev") * L)
+
+    def level(k, carry):
+        for c in range(C):
+            l = le[E + k, E + c]
+            befores = (le[E + k, E + c - 1], pltpu.roll(l, 1, 1), le[E + k - 1, E + c])
+            for direction, before, carried in zip(range(3), befores, (zc, yc, vc)):
+                row = jnp.sum((l - before) * carried[k, c], axis=0, keepdims=True)
+                row = jnp.where(fields.open(direction, k, c), row, 0.0)
+                sp_ref[direction, k, c : c + 1, :] = row
+        return carry
+
+    lax.fori_loop(0, L, level, 0)
+    if len(outs) == 1:
+        outs[0][...] = sp_ref[...] + late_ref[...]
         return
     half = L // 2
     low = lax.axis_index("trc") == 0
@@ -704,26 +774,42 @@
 
         @pl.when(low if keeps_low else jnp.logical_not(low))
         def _(keeps_low=keeps_low):
-            for out, first in ((sp_out, keeps_low), (given_ref, not keeps_low)):
+            for out, first in zip(outs, (keeps_low, not keeps_low)):
                 k0 = 0 if first else half
                 out[...] = sp_ref[:, k0 : k0 + half] + late_ref[:, k0 : k0 + half]
 
 
+def start_edge_body(dims, *refs):
+    T, L, C, _ = dims
+    qe, fe, de, le = refs[:4]
+    kept = refs[4:8]
+    out_hbm, out_ref, acc, sem = refs[9:]
+
+    def done(k, c, value):
+        out_ref[pl.ds(k * C + c, T, stride=L * C), :] = value
+
+    fields = Fields(fe, de, lax.axis_index("lev") * L)
+    adjoint(dims, fields, qe, H, le, acc, done, parts(C)[0], kept=kept)
+    copy = pltpu.make_async_copy(out_ref, out_hbm, sem)
+    copy.start()
+    copy.wait()
+
+
 def f32(*shape):
     return jax.ShapeDtypeStruct(shape, jnp.float32)
 
 
-def call(body, outs, scratch, args, hbm=0, aliases=None, mib=4):
-    return run(body, outs, scratch, args, hbm, aliases, mib)
-
-
-def run(body, outs, scratch, args, hbm, aliases, mib):
+def call(body, outs, scratch, args, hbm=0, aliases=None, mib=4, hbm_out=0):
+    return run(body, outs, scratch, args, hbm, aliases, mib, hbm_out)
+
+
+def run(body, outs, scratch, args, hbm, aliases, mib, hbm_out):
     vmem = pl.BlockSpec(memory_space=pltpu.VMEM)
     return pl.pallas_call(
         body,
         out_shape=outs,
         in_specs=[pl.BlockSpec(memory_space=pltpu.HBM)] * hbm + [vmem] * (len(args) - hbm),
-        out_specs=[vmem] * len(outs),
+        out_specs=[pl.BlockSpec(memory_space=pltpu.HBM)] * hbm_out + [vmem] * (len(outs) - hbm_out),
         scratch_shapes=scratch,
         input_output_aliases=aliases or {},
         compiler_params=pltpu.CompilerParams(vmem_limit_bytes=mib * 1024 * 1024),
@@ -745,18 +831,18 @@
     q = tracers.reshape(T * L * C, Y)
     l = cotangent.reshape(T * L * C, Y)
     inputs = [q, l, zonal_speed, meridional_speed, vertical_speed, lateral_mixing, vertical_mixing, column_depth]
-    landing = [
-        pltpu.VMEM((T * L * C, Y), jnp.float32),
-        pltpu.VMEM((T * L * C, Y), jnp.float32),
-        pltpu.VMEM((NF, L, C, Y), jnp.float32),
-        pltpu.VMEM((C, Y), jnp.int32),
-        pltpu.SemaphoreType.DMA((8,)),
-    ]
-
-    tile_rows = (H + E) * T + FPAD
+    inputs = [pltpu.with_memory_space_constraint(x, pltpu.HBM) for x in inputs]
+    tile_rows = H * T + FPAD
     lev_rows = max(C * T, W * NF * C)
-    to_tile = call(
-        functools.partial(edges_body, dims, n_tile), [f32(L, tile_rows, Y)] * n_tile, landing, inputs, hbm=8, mib=MIB
+    *to_tile, q, l, f, d = call(
+        functools.partial(edges_body, dims, n_tile),
+        [f32(L, tile_rows, Y)] * n_tile
+        + [f32(T * L * C, Y)] * 2
+        + [f32(NF, L, C, Y), jax.ShapeDtypeStruct((C, Y), jnp.int32)],
+        [pltpu.SemaphoreType.DMA((8,))],
+        inputs,
+        hbm=8,
+        mib=MIB,
     )
     from_tile = swap(to_tile, "tile", tile_pairs)
 
@@ -765,55 +851,80 @@
     fe_s = f32(NF, L + 2 * W, C + 2 * W, 1, Y)
     de_s = f32(3, C + 2 * W, 1, Y)
     own_s = f32(L, C, T, Y)
-    *to_lev, qe, le, fe, de = call(
-        functools.partial(own_body, dims, n_lev),
-        [f32(H + E + 1, lev_rows, Y)] * n_lev + [qe_s, ext_s, fe_s, de_s],
-        landing,
-        inputs + [to_tile[0]],
-        hbm=8,
-    )
-    from_lev = swap(to_lev, "lev", lev_pairs)
+    sent = call(
+        functools.partial(own_body, dims, n_tile, n_lev),
+        [f32(L, E, T, Y)] * n_tile + [f32(H + E + 1, lev_rows, Y)] * n_lev + [qe_s, ext_s, fe_s, de_s],
+        [],
+        [q, l, f, d],
+    )
+    qe, le, fe, de = sent[n_tile + n_lev :]
+    from_lev = swap(sent[n_tile : n_tile + n_lev], "lev", lev_pairs)
+    late_tile = swap(sent[:n_tile], "tile", tile_pairs)
+    me, yu, yd, yc = call(functools.partial(inner_y_body, dims), [ext_s] + [own_s] * 3, [], [qe, fe, de])
     n = n_lev
-    qe, le, fe, me, *kept = call(
-        functools.partial(inner_body, dims, n_lev),
-        [qe_s, ext_s, fe_s, ext_s] + [own_s] * 3 + [f32(L + 2, C, T, Y)] * 2 + [own_s],
+    qe, le, fe, me, vu, vd, vc = call(
+        functools.partial(inner_v_body, dims, n_lev),
+        [qe_s, ext_s, fe_s, ext_s] + [f32(L + 2, C, T, Y)] * 2 + [own_s],
         [],
-        [*from_lev, qe, le, fe, de],
-        aliases={n: 0, n + 1: 1, n + 2: 2},
+        [*from_lev, qe, le, fe, me, de],
+        aliases={n + i: i for i in range(4)},
     )
     to_lev = call(
         functools.partial(corner_body, dims, n_tile), [f32(n_tile, E, tile_rows, Y)] * n_lev, [], [*from_tile, me]
     )
     corners = swap(to_lev, "lev", lev_pairs)
     n = n_tile
-    qe, le, fe, de, me = call(
+    qe, fe, de, me, zc = call(
         functools.partial(beside_body, dims, n_tile),
-        [qe_s, ext_s, fe_s, de_s, ext_s],
+        [qe_s, fe_s, de_s, ext_s, own_s],
         [],
-        [*from_tile, qe, le, fe, de, me],
-        aliases={n + i: i for i in range(5)},
-    )
-    n = n_lev
-    qe, fe, me, mc, late, *mc_edges = call(
+        [*from_tile, qe, fe, de, me],
+        aliases={n + i: i for i in range(4)},
+    )
+    n = n_lev + n_tile
+    qe, le, fe, me, mc, late, *mc_edges = call(
         functools.partial(late_body, dims, n_tile, n_lev),
-        [qe_s, fe_s, ext_s, own_s, f32(3, L, C, Y)] + [f32(L, E, T, Y)] * n_tile + [f32(E, C, T, Y)] * n_lev,
+        [qe_s, ext_s, fe_s, ext_s, own_s, f32(3, L, C, Y)] + [f32(L, E, T, Y)] * n_tile,
         [],
-        [*corners, le, de, qe, fe, me],
-        aliases={n + 2: 0, n + 3: 1, n + 4: 2},
-    )
-    mc_tile = swap(mc_edges[:n_tile], "tile", tile_pairs)
-    mc_lev = swap(mc_edges[n_tile:], "lev", lev_pairs)
+        [*corners, *late_tile, de, qe, le, fe, me],
+        aliases={n + 1 + i: i for i in range(4)},
+    )
+    mc_tile = swap(mc_edges, "tile", tile_pairs)
+    mc, late, *mc_edges = call(
+        functools.partial(late_inner_body, dims),
+        [own_s, f32(3, L, C, Y)] + [f32(E, C, T, Y)] * n_lev,
+        [],
+        [le, fe, de, me, mc, late],
+        aliases={4: 0, 5: 1},
+    )
+    mc_lev = swap(mc_edges, "lev", lev_pairs)
+    le, acc = call(functools.partial(start_inner_body, dims), [ext_s, own_s], [], [qe, fe, de, mc, yu, yd])
+    le, out = call(
+        functools.partial(start_levels_body, dims, n_lev),
+        [ext_s, f32(T * L * C, Y)],
+        [],
+        [fe, de, vu, vd, acc, *mc_lev, le],
+        aliases={5 + n_lev: 0},
+    )
     pair = lax.axis_size("trc") == 2 and L % 2 == 0
-    start, speeds, *given = call(
-        functools.partial(start_body, dims, n_tile, n_lev),
-        [f32(T * L * C, Y)] + ([f32(3, L // 2, C, Y)] * 2 if pair else [f32(3, L, C, Y)]),
-        [pltpu.VMEM(x.shape, jnp.float32) for x in (ext_s, own_s, f32(3, L, C, Y))],
-        [qe, fe, de, mc, late, *kept, *mc_tile, *mc_lev],
+    le, speeds, *given = call(
+        functools.partial(speeds_body, dims, n_tile),
+        [ext_s] + ([f32(3, L // 2, C, Y)] * 2 if pair else [f32(3, L, C, Y)]),
+        [pltpu.VMEM((3, L, C, Y), jnp.float32)],
+        [fe, de, late, zc, yc, vc, *mc_tile, le],
+        aliases={6 + n_tile: 0},
     )
     if pair:
-        speeds = speeds + lax.ppermute(given[0], "trc", [(0, 1), (1, 0)])
-    else:
-        speeds = lax.psum_scatter(speeds, "trc", scatter_dimension=1, tiled=True)
+        other = swap(given, "trc", [[(0, 1), (1, 0)]])[0]
+    start, _ = call(
+        functools.partial(start_edge_body, dims),
+        [f32(T * L * C, Y)] * 2,
+        [pltpu.VMEM(own_s.shape, jnp.float32), pltpu.SemaphoreType.DMA],
+        [qe, fe, de, le, yu, yd, vu, vd, out],
+        aliases={8: 1},
+        hbm_out=1,
+    )
+    speeds = speeds + other if pair else lax.psum_scatter(speeds, "trc", scatter_dimension=1, tiled=True)
     return start.reshape(T, L, C, Y), speeds
 
 

time: 47.2 us -> 43.6 us (0.924)
  the two profiles are of different devices: /device:TPU:0 before, /device:TPU:16 now
where the time goes in v3:
time: 43.6 us; the launch traced here: 43.4 us
  Pallas kernels  19.9 us (46%)
  waiting for transfers between devices  12.2 us (28%)
  starting transfers between devices  9.85 us (23%)
  between operations  0.81 us (2%)
  other arithmetic  0.63 us (1%)
    pallas_call x12, Pallas kernels, run(): pl.pallas_call(body, out_shape=outs, in_specs=[pl.BlockSpec(memory_space=...  19.9 us
    ppermute x10, waiting for transfers between devices, swap(): received.append(lax.ppermute(x, axis, pairs))  12.2 us
    ppermute x10, starting transfers between devices, swap(): received.append(lax.ppermute(x, axis, pairs))  9.85 us
  transfers between devices with their start and end apart: 10, of which 6 were waited for; matrix products, arithmetic and copies ran while one was open for 0% of the time, Pallas kernels for 26%

profile of v3, /device:TPU:16, one launch (start us, length us, event | category | flops | bytes accessed | tf_op | source)
XLA Modules:
  0.0 43.4 jit_solution(1733286926994238225)
XLA Ops:
  0.6 1.5 %shard_map.95 = (f32[8,80,128]{2,1,0:T(8,128)S(1)}, f32[8,80,128]{2,1,0:T(8,128)S(1)}, f32[1024,128]{1,0:T(8,128)S(1)}, f32[1024,128]{1,0:T(8,128)S(1)}, f32[5,8...) custom-call(f32[1024,128]{1,0:T(8,128)} %bitcast.3, f32[1024,128]{1,0:T(8,128)} %bitcast.4, f32[8,8,128]{2,1,0:T(8,128)} %refs_2_.1, ...), custom_call_target="tpu_custom_call" | custom-call | tf_op jit(solution)/shard_map/pallas_call | solution.py:808
  2.1 1.0 %shard_map.96 = (f32[8,2,16,128]{3,2,1,0:T(8,128)S(1)}, f32[8,2,16,128]{3,2,1,0:T(8,128)S(1)}, f32[7,128,128]{2,1,0:T(8,128)S(1)}, f32[16,16,16,128]{3,2,1,0:T(8...) custom-call(f32[1024,128]{1,0:T(8,128)S(1)} %get-tuple-element.52.refs, ...), custom_call_target="tpu_custom_call" | custom-call | tf_op jit(solution)/shard_map/pallas_call | solution.py:808
  3.1 0.1 collective-permute-start.2
  3.2 1.6 %collective-permute-start = (f32[8,80,128]{2,1,0:T(8,128)S(1)}, f32[8,80,128]{2,1,0:T(8,128)S(1)}, u32[]{:S(2)}, u32[]{:S(2)}) collective-permute-start(f32[8,80,128]{2,1,0:T(8,128)S(1)} %get-tuple-element.50), channel_id=1, source_target_pairs={{0,4},{4,0},{8,12},{12,8},{1,5},{5,1},{9,13},{13,9},{2,6},{6,2},{1... | collective-permute-start | bytes 983048 | tf_op jit(solution)/shard_map/ppermute | solution.py:822
  4.8 1.9 %collective-permute-start.1 = (f32[8,80,128]{2,1,0:T(8,128)S(1)}, f32[8,80,128]{2,1,0:T(8,128)S(1)}, u32[]{:S(2)}, u32[]{:S(2)}) collective-permute-start(f32[8,80,128]{2,1,0:T(8,128)S(1)} %get-tuple-element.51), channel_id=1, source_target_pairs={{4,8},{8,4},{5,9},{9,5},{6,10},{10,6},{7,11},{11,7},{20,24},{24,20... | collective-permute-start | bytes 983048 | tf_op jit(solution)/shard_map/ppermute | solution.py:822
  6.8 2.6 %shard_map.97 = (f32[12,12,16,128]{3,2,1,0:T(8,128)S(1)}, f32[8,8,16,128]{3,2,1,0:T(8,128)S(1)}, f32[8,8,16,128]{3,2,1,0:T(8,128)S(1)}, f32[8,8,16,128]{3,2,1,0:T(8,128)S(1)}) custom-call(f32[16,16,16,128]{3,2,1,0:T(8,128)S(1)} %get-tuple-element.57.qe.refs_1_, f32[5,14,14,1,128]{4,3,2,1,0:T(1,128)S(1)} %get-tuple-element.59.fe.refs_3_, ...), custom_call_target="tpu_custom_call" | custom-call | tf_op jit(solution)/shard_map/pallas_call | solution.py:808
  9.4 1.7 %shard_map.98 = (f32[16,16,16,128]{3,2,1,0:T(8,128)S(1)}, f32[12,12,16,128]{3,2,1,0:T(8,128)S(1)}, f32[5,14,14,1,128]{4,3,2,1,0:T(1,128)S(1)}, f32[12,12,16,128]...) custom-call(f32[7,128,128]{2,1,0:T(8,128)S(1)} %collective-permute-d, ...), custom_call_target="tpu_custom_call", output_to_operand_aliasing={{0}: (1, {}), {1}: (2, {}), {2}: (3, {}), {3}: (4, {})} | custom-call | tf_op jit(solution)/shard_map/pallas_call | solution.py:808
  11.1 2.2 %collective-permute-done.refs_0_ = f32[8,80,128]{2,1,0:T(8,128)S(1)} collective-permute-done((f32[8,80,128]{2,1,0:T(8,128)S(1)}, f32[8,80,128]{2,1,0:T(8,128)S(1)}, u32[]{:S(2)}, u32[]{:S(2)}) %collective-permute-start) | collective-permute-done | bytes 327712 | tf_op jit(solution)/shard_map/ppermute | solution.py:822
  13.3 3.2 %collective-permute-done.1.refs_1_ = f32[8,80,128]{2,1,0:T(8,128)S(1)} collective-permute-done((f32[8,80,128]{2,1,0:T(8,128)S(1)}, f32[8,80,128]{2,1,0:T(8,128)S(1)}, u32[]{:S(2)}, u32[]{:S(2)}) %collective-permute-start.1) | collective-permute-done | bytes 327712 | tf_op jit(solution)/shard_map/ppermute | solution.py:822
  16.7 2.2 %collective-permute-start.5 = (f32[8,2,16,128]{3,2,1,0:T(8,128)S(1)}, f32[8,2,16,128]{3,2,1,0:T(8,128)S(1)}, u32[]{:S(2)}, u32[]{:S(2)}) collective-permute-start(f32[8,2,16,128]{3,2,1,0:T(8,128)S(1)} %get-tuple-element.64), channel_id=1, source_target_pairs={{4,8},{8,4},{5,9},{9,5},{6,10},{10,6},{7,11},{11,7},{20,24},{24,20... | collective-permute-start | bytes 393224 | tf_op jit(solution)/shard_map/ppermute | solution.py:822
  18.9 2.2 %shard_map.100 = (f32[16,16,16,128]{3,2,1,0:T(8,128)S(1)}, f32[5,14,14,1,128]{4,3,2,1,0:T(1,128)S(1)}, f32[3,14,1,128]{3,2,1,0:T(1,128)S(1)}, f32[12,12,16,128]{3,2,1,0:T(8,128)S(1)}, f32[8,8,16,128]{3,2,1,0:T(8,128)S(1)}) custom-call(f32[8,80,128]{2,1,0:T(8,128)S(1)} %collective-permute-done, ...), custom_call_target="tpu_custom_call", output_to_operand_aliasing={{0}: (2, {}), {1}: (3, {}), {2}: (4, {}), {3}: (5, {})} | custom-call | tf_op jit(solution)/shard_map/pallas_call | solution.py:808
  21.1 1.4 %collective-permute-done.4.refs_1_ = f32[8,2,16,128]{3,2,1,0:T(8,128)S(1)} collective-permute-done((f32[8,2,16,128]{3,2,1,0:T(8,128)S(1)}, f32[8,2,16,128]{3,2,1,0:T(8,128)S(1)}, u32[]{:S(2)}, u32[]{:S(2)}) %collective-permute-start.4) | collective-permute-done | bytes 131104 | tf_op jit(solution)/shard_map/ppermute | solution.py:822
  22.5 1.9 %collective-permute-done.5.refs_2_ = f32[8,2,16,128]{3,2,1,0:T(8,128)S(1)} collective-permute-done((f32[8,2,16,128]{3,2,1,0:T(8,128)S(1)}, f32[8,2,16,128]{3,2,1,0:T(8,128)S(1)}, u32[]{:S(2)}, u32[]{:S(2)}) %collective-permute-start.5) | collective-permute-done | bytes 131104 | tf_op jit(solution)/shard_map/ppermute | solution.py:822
  24.4 3.0 %shard_map.101 = (f32[16,16,16,128]{3,2,1,0:T(8,128)S(1)}, f32[12,12,16,128]{3,2,1,0:T(8,128)S(1)}, f32[5,14,14,1,128]{4,3,2,1,0:T(1,128)S(1)}, f32[12,12,16,128...) custom-call(f32[2,2,80,128]{3,2,1,0:T(8,128)S(1)} %collective-permut, ...), custom_call_target="tpu_custom_call", output_to_operand_aliasing={{0}: (4, {}), {1}: (5, {}), {2}: (6, {}), {3}: (7, {})} | custom-call | tf_op jit(solution)/shard_map/pallas_call | solution.py:808
  27.4 2.4 %shard_map.102 = (f32[8,8,16,128]{3,2,1,0:T(8,128)S(1)}, f32[3,8,8,128]{3,2,1,0:T(8,128)S(1)}, f32[2,8,16,128]{3,2,1,0:T(8,128)S(1)}) custom-call(f32[12,12,16,128]{3,2,1,0:T(8,128)S(1)} %get-tuple-element.74.refs_0_, f32[5,14,14,1,128]{4,3,2,1,0:T(1,128)S(1)} %get-tuple-element.73.refs_1_.refs_0_, ...), custom_call_target="tpu_custom_call", output_to_operand_aliasing={{0}: (4, {}), {1}: (5, {})} | custom-call | tf_op jit(solution)/shard_map/pallas_call | solution.py:808
  29.9 2.2 %collective-permute-start.7 = (f32[8,2,16,128]{3,2,1,0:T(8,128)S(1)}, f32[8,2,16,128]{3,2,1,0:T(8,128)S(1)}, u32[]{:S(2)}, u32[]{:S(2)}) collective-permute-start(f32[8,2,16,128]{3,2,1,0:T(8,128)S(1)} %get-tuple-element.83), channel_id=1, source_target_pairs={{4,8},{8,4},{5,9},{9,5},{6,10},{10,6},{7,11},{11,7},{20,24},{24,20... | collective-permute-start | bytes 393224 | tf_op jit(solution)/shard_map/ppermute | solution.py:822
  32.1 1.5 %shard_map.103 = (f32[12,12,16,128]{3,2,1,0:T(8,128)S(1)}, f32[8,8,16,128]{3,2,1,0:T(8,128)S(1)}) custom-call(f32[16,16,16,128]{3,2,1,0:T(8,128)S(1)} %get-tuple-element.72.refs_0_, f32[5,14,14,1,128]{4,3,2,1,0:T(1,128)S(1)} %get-tuple-element.73.refs_1_.refs_0_, f32[3,14,1,128]{3,2,1,0:T(1,128)S(1)} %get-tuple-element.67.refs_3_.refs_2_.refs_1_, ...), custom_call_target="tpu_custom_call" | custom-call | tf_op jit(solution)/shard_map/pallas_call | solution.py:808
  33.6 0.4 shard_map.104
  34.1 1.6 %collective-permute-done.6.refs_6_ = f32[8,2,16,128]{3,2,1,0:T(8,128)S(1)} collective-permute-done((f32[8,2,16,128]{3,2,1,0:T(8,128)S(1)}, f32[8,2,16,128]{3,2,1,0:T(8,128)S(1)}, u32[]{:S(2)}, u32[]{:S(2)}) %collective-permute-start.6) | collective-permute-done | bytes 131104 | tf_op jit(solution)/shard_map/ppermute | solution.py:822
  35.7 1.9 %collective-permute-done.7.refs_7_ = f32[8,2,16,128]{3,2,1,0:T(8,128)S(1)} collective-permute-done((f32[8,2,16,128]{3,2,1,0:T(8,128)S(1)}, f32[8,2,16,128]{3,2,1,0:T(8,128)S(1)}, u32[]{:S(2)}, u32[]{:S(2)}) %collective-permute-start.7) | collective-permute-done | bytes 131104 | tf_op jit(solution)/shard_map/ppermute | solution.py:822
  37.6 0.8 %shard_map.105 = (f32[12,12,16,128]{3,2,1,0:T(8,128)S(1)}, f32[3,4,8,128]{3,2,1,0:T(8,128)S(1)}, f32[3,4,8,128]{3,2,1,0:T(8,128)S(1)}) custom-call(f32[5,14,14,1,128]{4,3,2,1,0:T(1,128)S(1)} %get-tuple-element.73.refs_1_.refs_0_, f32[3,14,1,128]{3,2,1,0:T(1,128)S(1)} %get-tuple-element.67.refs_3_.refs_2_.refs_1_, ...), custom_call_target="tpu_custom_call", output_to_operand_aliasing={{0}: (8, {})} | custom-call | tf_op jit(solution)/shard_map/pallas_call | solution.py:808
  38.4 1.6 %collective-permute-start.9 = (f32[3,4,8,128]{3,2,1,0:T(8,128)S(1)}, f32[3,4,8,128]{3,2,1,0:T(8,128)S(1)}, u32[]{:S(2)}, u32[]{:S(2)}) collective-permute-start(f32[3,4,8,128]{3,2,1,0:T(8,128)S(1)} %get-tuple-element.97), channel_id=1, source_target_pairs={{0,2},{2,0},{1,3},{3,1},{4,6},{6,4},{5,7},{7,5},{8,10},{10,8},{9,1... | collective-permute-start | bytes 147464 | tf_op jit(solution)/shard_map/ppermute | solution.py:822
  40.0 2.8 %shard_map.106 = (f32[1024,128]{1,0:T(8,128)}, f32[1024,128]{1,0:T(8,128)S(1)}) custom-call(f32[16,16,16,128]{3,2,1,0:T(8,128)S(1)} %get-tuple-element.72.refs_0_, f32[5,14,14,1,128]{4,3,2,1,0:T(1,128)S(1)} %get-tuple-element.73.refs_1_.refs_0_, f32[3,14,1,128]{3,2,1,0:T(1,128)S(1)} %get-tuple-element.67.refs_3_.refs_2_.refs_1_, ...), custom_call_target="tpu_custom_call", output_to_operand_aliasing={{1}: (8, {})} | custom-call | tf_op jit(solution)/shard_map/pallas_call | solution.py:808
  42.8 0.6 %add.3 = f32[3,4,8,128]{3,2,1,0:T(8,128)} add(f32[3,4,8,128]{3,2,1,0:T(8,128)S(1)} %get-tuple-element.96, f32[3,4,8,128]{3,2,1,0:T(8,128)S(1)} %collective-permute-done.9) | non-fusion elementwise | flops 12288 | bytes 147456 | tf_op jit(solution)/shard_map/add | solution.py:927
  (9 shorter events, 0.3 us)
Async XLA Ops:
  3.1 6.3 %collective-permute-start.2 = (f32[7,128,128]{2,1,0:T(8,128)S(1)}, f32[7,128,128]{2,1,0:T(8,128)S(1)}, u32[]{:S(2)}, u32[]{:S(2)}) collective-permute-start(f32[7,128,128]{2,1,0:T(8,128)S(1)} %get-tuple-element.56), channel_id=1, source_target_pairs={{0,1},{1,0},{2,3},{3,2},{4,5},{5,4},{6,7},{7,6},{8,9},{9,8},{10,11... | collective-permute-start | bytes 1376264 | tf_op jit(solution)/shard_map/ppermute | solution.py:822
  3.2 10.1 %collective-permute-start = (f32[8,80,128]{2,1,0:T(8,128)S(1)}, f32[8,80,128]{2,1,0:T(8,128)S(1)}, u32[]{:S(2)}, u32[]{:S(2)}) collective-permute-start(f32[8,80,128]{2,1,0:T(8,128)S(1)} %get-tuple-element.50), channel_id=1, source_target_pairs={{0,4},{4,0},{8,12},{12,8},{1,5},{5,1},{9,13},{13,9},{2,6},{6,2},{1... | collective-permute-start | bytes 983048 | tf_op jit(solution)/shard_map/ppermute | solution.py:822
  4.8 11.6 %collective-permute-start.1 = (f32[8,80,128]{2,1,0:T(8,128)S(1)}, f32[8,80,128]{2,1,0:T(8,128)S(1)}, u32[]{:S(2)}, u32[]{:S(2)}) collective-permute-start(f32[8,80,128]{2,1,0:T(8,128)S(1)} %get-tuple-element.51), channel_id=1, source_target_pairs={{4,8},{8,4},{5,9},{9,5},{6,10},{10,6},{7,11},{11,7},{20,24},{24,20... | collective-permute-start | bytes 983048 | tf_op jit(solution)/shard_map/ppermute | solution.py:822
  16.5 7.9 %collective-permute-start.3 = (f32[2,2,80,128]{3,2,1,0:T(8,128)S(1)}, f32[2,2,80,128]{3,2,1,0:T(8,128)S(1)}, u32[]{:S(2)}, u32[]{:S(2)}) collective-permute-start(f32[2,2,80,128]{3,2,1,0:T(8,128)S(1)} %shard_map.99), channel_id=1, source_target_pairs={{0,1},{1,0},{2,3},{3,2},{4,5},{5,4},{6,7},{7,6},{8,9},{9,8},{10,11... | collective-permute-start | bytes 491528 | tf_op jit(solution)/shard_map/ppermute | solution.py:822
  16.6 5.9 %collective-permute-start.4 = (f32[8,2,16,128]{3,2,1,0:T(8,128)S(1)}, f32[8,2,16,128]{3,2,1,0:T(8,128)S(1)}, u32[]{:S(2)}, u32[]{:S(2)}) collective-permute-start(f32[8,2,16,128]{3,2,1,0:T(8,128)S(1)} %get-tuple-element.63), channel_id=1, source_target_pairs={{0,4},{4,0},{8,12},{12,8},{1,5},{5,1},{9,13},{13,9},{2,6},{6,2},{1... | collective-permute-start | bytes 393224 | tf_op jit(solution)/shard_map/ppermute | solution.py:822
  16.7 7.7 %collective-permute-start.5 = (f32[8,2,16,128]{3,2,1,0:T(8,128)S(1)}, f32[8,2,16,128]{3,2,1,0:T(8,128)S(1)}, u32[]{:S(2)}, u32[]{:S(2)}) collective-permute-start(f32[8,2,16,128]{3,2,1,0:T(8,128)S(1)} %get-tuple-element.64), channel_id=1, source_target_pairs={{4,8},{8,4},{5,9},{9,5},{6,10},{10,6},{7,11},{11,7},{20,24},{24,20... | collective-permute-start | bytes 393224 | tf_op jit(solution)/shard_map/ppermute | solution.py:822
  29.7 3.9 %collective-permute-start.8 = (f32[2,8,16,128]{3,2,1,0:T(8,128)S(1)}, f32[2,8,16,128]{3,2,1,0:T(8,128)S(1)}, u32[]{:S(2)}, u32[]{:S(2)}) collective-permute-start(f32[2,8,16,128]{3,2,1,0:T(8,128)S(1)} %get-tuple-element.90), channel_id=1, source_target_pairs={{0,1},{1,0},{2,3},{3,2},{4,5},{5,4},{6,7},{7,6},{8,9},{9,8},{10,11... | collective-permute-start | bytes 393224 | tf_op jit(solution)/shard_map/ppermute | solution.py:822
  29.8 5.9 %collective-permute-start.6 = (f32[8,2,16,128]{3,2,1,0:T(8,128)S(1)}, f32[8,2,16,128]{3,2,1,0:T(8,128)S(1)}, u32[]{:S(2)}, u32[]{:S(2)}) collective-permute-start(f32[8,2,16,128]{3,2,1,0:T(8,128)S(1)} %get-tuple-element.82), channel_id=1, source_target_pairs={{0,4},{4,0},{8,12},{12,8},{1,5},{5,1},{9,13},{13,9},{2,6},{6,2},{1... | collective-permute-start | bytes 393224 | tf_op jit(solution)/shard_map/ppermute | solution.py:822
  29.9 7.7 %collective-permute-start.7 = (f32[8,2,16,128]{3,2,1,0:T(8,128)S(1)}, f32[8,2,16,128]{3,2,1,0:T(8,128)S(1)}, u32[]{:S(2)}, u32[]{:S(2)}) collective-permute-start(f32[8,2,16,128]{3,2,1,0:T(8,128)S(1)} %get-tuple-element.83), channel_id=1, source_target_pairs={{4,8},{8,4},{5,9},{9,5},{6,10},{10,6},{7,11},{11,7},{20,24},{24,20... | collective-permute-start | bytes 393224 | tf_op jit(solution)/shard_map/ppermute | solution.py:822
  38.4 4.3 %collective-permute-start.9 = (f32[3,4,8,128]{3,2,1,0:T(8,128)S(1)}, f32[3,4,8,128]{3,2,1,0:T(8,128)S(1)}, u32[]{:S(2)}, u32[]{:S(2)}) collective-permute-start(f32[3,4,8,128]{3,2,1,0:T(8,128)S(1)} %get-tuple-element.97), channel_id=1, source_target_pairs={{0,2},{2,0},{1,3},{3,1},{4,6},{6,4},{5,7},{7,5},{8,10},{10,8},{9,1... | collective-permute-start | bytes 147464 | tf_op jit(solution)/shard_map/ppermute | solution.py:822

commit v4 on v3

--- a/solution.py
+++ b/solution.py
@@ -133,7 +133,7 @@
     Y = u.shape[-1]
     before = jnp.where(first, 0.0, pltpu.roll(u, 1, 1))
     d = u - before
-    nxt = jnp.where(last, -u, pltpu.roll(d, Y - 1, 1))
+    nxt = jnp.where(last, 0.0, pltpu.roll(u, Y - 1, 1)) - u
     xx, yy = d * d, nxt * nxt
     s, r, a = limiter(d, nxt, xx, yy)
     half = 0.5 * a
@@ -150,15 +150,15 @@
     first, last = ends
     Y = l.shape[-1]
     g = l - pltpu.roll(l, 1, 1)
-    p = jnp.maximum(v, 0.0) * g
     n = jnp.minimum(v, 0.0) * g
-    e = pltpu.roll(p, Y - 1, 1) - n
+    p_next = pltpu.roll(jnp.maximum(v, 0.0), Y - 1, 1) * (pltpu.roll(l, Y - 1, 1) - l)
+    e = p_next - n
     z = e * up - m * g
     y = e * down
     add = (
-        (n + z - y)
+        (n + z - y + p_next)
         + jnp.where(first, 0.0, pltpu.roll(y, 1, 1))
-        + jnp.where(last, 0.0, pltpu.roll(p - z, Y - 1, 1))
+        - jnp.where(last, 0.0, pltpu.roll(z, Y - 1, 1))
     )
     return add, g
 
@@ -306,7 +306,7 @@
         by_parity(lev_even, phase, blank_lev)
 
 
-def inner_y_body(dims, qe, fe, de, me, yu, yd, yc):
+def inner_y_body(dims, qe, fe, de, me, ky):
     T, L, C, Y = dims
     fields = Fields(fe, de, lax.axis_index("lev") * L)
     ends = lanes(T, Y)
@@ -316,8 +316,8 @@
             u = qe[H + k, H + c]
             v, m, _ = fields.at(1, k, c)
             d, carried, coefs = along_values(u, v, ends)
-            yu[k, c], yd[k, c] = coefs()
-            yc[k, c] = carried
+            ky[k, c, 0], ky[k, c, 1] = coefs()
+            ky[k, c, 2] = carried
             me[E + k, E + c] = u + along_forward(d, carried, v, m)
         return carry
 
@@ -328,7 +328,7 @@
     T, L, C, Y = dims
     lev_in = refs[:n_lev]
     de = refs[n_lev + 4]
-    qe, le, fe, me, vu, vd, vc = refs[n_lev + 5 :]
+    qe, le, fe, me, kv = refs[n_lev + 5 :]
     _, lev_even = parities()
     zero = jnp.zeros((T, Y), jnp.float32)
 
@@ -393,9 +393,9 @@
         def keep(k, coefs, carried):
             k = k - E
             if -1 <= k <= L:
-                vu[1 + k, c], vd[1 + k, c] = coefs()
+                kv[1 + k, c, 0], kv[1 + k, c, 1] = coefs()
             if 0 <= k < L:
-                vc[k, c] = carried
+                kv[1 + k, c, 2] = carried
 
         forward_chain(
             L + 2 * E, lambda k: qe[H - E + k, H + c], lambda k: fields.at(2, k - E, c)[:2], emit, keep
@@ -600,14 +600,22 @@
 def parts(C):
     edge = (list(range(E)) + list(range(C - E, C)), [(0, E), (C - E, E)], lambda i: jnp.where(i < E, i, C - 2 * E + i))
     inner = (list(range(E, C - E)), [(E, C - 2 * E)] if C > 2 * E else [], lambda i: E + i)
-    return edge, inner
-
-
-def adjoint(dims, fields, u_ref, uo, l_ref, acc_ref, done, part, speed_ref=None, kept=None, passes="yzv"):
+    both = (list(range(C)), [(0, C)], lambda i: i)
+    return edge, inner, both
+
+
+def adjoint(dims, fields, u_ref, uo, l_ref, acc_ref, done, part, speed_ref=None, kept=None, passes="yzv", level_done=None):
     T, L, _, Y = dims
     ends = lanes(T, Y)
-    yu, yd, vu, vd = kept or [None] * 4
+    ky, kv = kept or (None, None)
     columns, runs, column_of = part
+
+    def put(direction, k, c, value):
+        value = acc_ref[k, c] + value
+        if done is not None and direction == passes[-1]:
+            done(k, c, value)
+        else:
+            acc_ref[k, c] = value
 
     def store_speed(direction, k, c, is_open, value):
         if speed_ref is not None:
@@ -622,16 +630,13 @@
                 _, carried, coefs = along_values(u_ref[uo + k, uo + c], v, ends)
                 up, down = coefs()
             else:
-                up, down = yu[k, c], yd[k, c]
+                up, down = ky[k, c, 0], ky[k, c, 1]
             add, g = along_adjoint(l, v, m, up, down, ends)
             acc_ref[k, c] = l + add
             if speed_ref is not None:
                 store_speed(1, k, c, is_open, g * carried)
         return carry
 
-    if "y" in passes:
-        lax.fori_loop(0, L, along, 0, unroll=2)
-
     def level_z(k, carry):
         for c0, n in runs:
             opened = {}
@@ -641,7 +646,7 @@
                 return v, m
 
             def emit(c, value, c0=c0):
-                acc_ref[k, c0 + c] = acc_ref[k, c0 + c] + value
+                put("z", k, c0 + c, value)
 
             def speed(c, value, c0=c0, opened=opened):
                 store_speed(0, k, c0 + c, opened[c], value)
@@ -654,10 +659,9 @@
                 emit,
                 speed if speed_ref is not None else None,
             )
-        return carry
-
-    if "z" in passes:
-        lax.fori_loop(0, L, level_z, 0)
+        if level_done is not None:
+            level_done(k)
+        return carry
 
     def column_v(i, carry):
         c = column_of(i)
@@ -668,14 +672,14 @@
             return v, m
 
         def emit(k, value):
-            done(k, c, acc_ref[k, c] + value)
-
-        if kept is None:
+            put("v", k, c, value)
+
+        if kept is None or kv is None:
             limits = fresh_limits(lambda k: u_ref[uo + k, uo + c])
         else:
 
             def limits(f, v):
-                return vu[f, c], vd[f, c], None
+                return kv[f, c, 0], kv[f, c, 1], None
 
         adjoint_chain(
             L,
@@ -687,13 +691,18 @@
         )
         return carry
 
-    if "v" in passes:
-        lax.fori_loop(0, len(columns), column_v, 0)
+    for direction in passes:
+        if direction == "y":
+            lax.fori_loop(0, L, along, 0, unroll=2 if len(columns) <= 4 else 1)
+        elif direction == "z":
+            lax.fori_loop(0, L, level_z, 0)
+        else:
+            lax.fori_loop(0, len(columns), column_v, 0)
 
 
 def start_inner_body(dims, *refs):
     _, L, C, _ = dims
-    qe, fe, de, mc_ref, yu, yd, le, acc = refs
+    qe, fe, de, mc_ref, ky, le, acc = refs
 
     def own(k, carry):
         for c in range(C):
@@ -702,14 +711,14 @@
 
     lax.fori_loop(0, L, own, 0, unroll=2)
     fields = Fields(fe, de, lax.axis_index("lev") * L)
-    adjoint(dims, fields, qe, H, le, acc, None, parts(C)[1], kept=(yu, yd, None, None), passes="yz")
+    adjoint(dims, fields, qe, H, le, acc, None, parts(C)[1], kept=(ky, None), passes="yz")
 
 
 def start_levels_body(dims, n_lev, *refs):
     T, L, C, Y = dims
-    fe, de, vu, vd, acc = refs[:5]
-    lev_in = refs[5 : 5 + n_lev]
-    le, out_ref = refs[6 + n_lev :]
+    fe, de, kv, ky, zc, late_ref = refs[:6]
+    lev_in = refs[6 : 6 + n_lev]
+    le, sp_ref = refs[7 + n_lev :]
     _, lev_even = parities()
     zero = jnp.zeros((T, Y), jnp.float32)
 
@@ -725,18 +734,33 @@
         source = lev_in[phase] if phase < n_lev else None
         by_parity(lev_even, phase, lambda high, s=source: place_lev(s, high))
 
-    def done(k, c, value):
-        out_ref[pl.ds(k * C + c, T, stride=L * C), :] = value
-
     fields = Fields(fe, de, lax.axis_index("lev") * L)
-    adjoint(dims, fields, None, H, le, acc, done, parts(C)[1], kept=(None, None, vu, vd), passes="v")
+
+    def level(k, carry):
+        for c in range(C):
+            l = le[E + k, E + c]
+            befores = (le[E + k, E + c - 1] if c > 0 else None, pltpu.roll(l, 1, 1), le[E + k - 1, E + c])
+            values = (zc[k, c], ky[k, c, 2], kv[k + 1, c, 2])
+            for direction, before, carried in zip(range(3), befores, values):
+                row = late_ref[direction, k, c : c + 1, :]
+                if before is not None:
+                    row = row + face_row(fields, direction, k, c, l - before, carried)
+                sp_ref[direction, k, c : c + 1, :] = row
+        return carry
+
+    lax.fori_loop(0, L, level, 0)
+
+
+def face_row(fields, direction, k, c, difference, carried):
+    row = jnp.sum(difference * carried, axis=0, keepdims=True)
+    return jnp.where(fields.open(direction, k, c), row, 0.0)
 
 
 def speeds_body(dims, n_tile, *refs):
     T, L, C, Y = dims
-    fe, de, late_ref, zc, yc, vc = refs[:6]
-    tile_in = refs[6 : 6 + n_tile]
-    le, *outs, sp_ref = refs[7 + n_tile :]
+    fe, de, part_ref, zc = refs[:4]
+    tile_in = refs[4 : 4 + n_tile]
+    le, *outs, row_ref = refs[5 + n_tile :]
     tile_even, _ = parities()
     zero = jnp.zeros((T, Y), jnp.float32)
 
@@ -754,19 +778,16 @@
 
     fields = Fields(fe, de, lax.axis_index("lev") * L)
 
-    def level(k, carry):
-        for c in range(C):
-            l = le[E + k, E + c]
-            befores = (le[E + k, E + c - 1], pltpu.roll(l, 1, 1), le[E + k - 1, E + c])
-            for direction, before, carried in zip(range(3), befores, (zc, yc, vc)):
-                row = jnp.sum((l - before) * carried[k, c], axis=0, keepdims=True)
-                row = jnp.where(fields.open(direction, k, c), row, 0.0)
-                sp_ref[direction, k, c : c + 1, :] = row
-        return carry
-
-    lax.fori_loop(0, L, level, 0)
+    for k in range(L):
+        row_ref[k : k + 1, :] = face_row(fields, 0, k, 0, le[E + k, E] - le[E + k, E - 1], zc[k, 0])
+
+    def put(out, k0, n):
+        out[...] = part_ref[:, k0 : k0 + n]
+        for k in range(n):
+            out[0, k, 0:1, :] = out[0, k, 0:1, :] + row_ref[k0 + k : k0 + k + 1, :]
+
     if len(outs) == 1:
-        outs[0][...] = sp_ref[...] + late_ref[...]
+        put(outs[0], 0, L)
         return
     half = L // 2
     low = lax.axis_index("trc") == 0
@@ -775,24 +796,31 @@
         @pl.when(low if keeps_low else jnp.logical_not(low))
         def _(keeps_low=keeps_low):
             for out, first in zip(outs, (keeps_low, not keeps_low)):
-                k0 = 0 if first else half
-                out[...] = sp_ref[:, k0 : k0 + half] + late_ref[:, k0 : k0 + half]
+                put(out, 0 if first else half, half)
 
 
 def start_edge_body(dims, *refs):
-    T, L, C, _ = dims
-    qe, fe, de, le = refs[:4]
-    kept = refs[4:8]
-    out_hbm, out_ref, acc, sem = refs[9:]
+    T, L, C, Y = dims
+    qe, fe, de, le, ky, kv = refs[:6]
+    out_hbm, acc, out_ref, sem = refs[7:]
+    flat = out_ref.reshape(T * L * C, Y)
 
     def done(k, c, value):
-        out_ref[pl.ds(k * C + c, T, stride=L * C), :] = value
+        flat[pl.ds(k * C + c, T, stride=L * C), :] = value
+
+    def leaving(k):
+        return pltpu.make_async_copy(out_ref.at[:, k], out_hbm.at[:, k], sem.at[k])
 
     fields = Fields(fe, de, lax.axis_index("lev") * L)
-    adjoint(dims, fields, qe, H, le, acc, done, parts(C)[0], kept=kept)
-    copy = pltpu.make_async_copy(out_ref, out_hbm, sem)
-    copy.start()
-    copy.wait()
+    kept = (ky, kv)
+    edge, inner = parts(C)[:2]
+    adjoint(dims, fields, qe, H, le, acc, None, edge, kept=kept, passes="y")
+    adjoint(dims, fields, qe, H, le, acc, done, inner, kept=kept, passes="v")
+    adjoint(
+        dims, fields, qe, H, le, acc, done, edge, kept=kept, passes="vz", level_done=lambda k: leaving(k).start()
+    )
+    for k in range(L):
+        leaving(k).wait()
 
 
 def f32(*shape):
@@ -860,11 +888,11 @@
     qe, le, fe, de = sent[n_tile + n_lev :]
     from_lev = swap(sent[n_tile : n_tile + n_lev], "lev", lev_pairs)
     late_tile = swap(sent[:n_tile], "tile", tile_pairs)
-    me, yu, yd, yc = call(functools.partial(inner_y_body, dims), [ext_s] + [own_s] * 3, [], [qe, fe, de])
+    me, ky = call(functools.partial(inner_y_body, dims), [ext_s, f32(L, C, 3, T, Y)], [], [qe, fe, de])
     n = n_lev
-    qe, le, fe, me, vu, vd, vc = call(
+    qe, le, fe, me, kv = call(
         functools.partial(inner_v_body, dims, n_lev),
-        [qe_s, ext_s, fe_s, ext_s] + [f32(L + 2, C, T, Y)] * 2 + [own_s],
+        [qe_s, ext_s, fe_s, ext_s, f32(L + 2, C, 3, T, Y)],
         [],
         [*from_lev, qe, le, fe, me, de],
         aliases={n + i: i for i in range(4)},
@@ -898,34 +926,34 @@
         aliases={4: 0, 5: 1},
     )
     mc_lev = swap(mc_edges, "lev", lev_pairs)
-    le, acc = call(functools.partial(start_inner_body, dims), [ext_s, own_s], [], [qe, fe, de, mc, yu, yd])
-    le, out = call(
+    le, acc = call(functools.partial(start_inner_body, dims), [ext_s, own_s], [], [qe, fe, de, mc, ky])
+    le, speeds = call(
         functools.partial(start_levels_body, dims, n_lev),
-        [ext_s, f32(T * L * C, Y)],
+        [ext_s, f32(3, L, C, Y)],
         [],
-        [fe, de, vu, vd, acc, *mc_lev, le],
-        aliases={5 + n_lev: 0},
+        [fe, de, kv, ky, zc, late, *mc_lev, le],
+        aliases={6 + n_lev: 0},
     )
     pair = lax.axis_size("trc") == 2 and L % 2 == 0
     le, speeds, *given = call(
         functools.partial(speeds_body, dims, n_tile),
         [ext_s] + ([f32(3, L // 2, C, Y)] * 2 if pair else [f32(3, L, C, Y)]),
-        [pltpu.VMEM((3, L, C, Y), jnp.float32)],
-        [fe, de, late, zc, yc, vc, *mc_tile, le],
-        aliases={6 + n_tile: 0},
+        [pltpu.VMEM((L, Y), jnp.float32)],
+        [fe, de, speeds, zc, *mc_tile, le],
+        aliases={4 + n_tile: 0},
     )
     if pair:
         other = swap(given, "trc", [[(0, 1), (1, 0)]])[0]
     start, _ = call(
         functools.partial(start_edge_body, dims),
-        [f32(T * L * C, Y)] * 2,
-        [pltpu.VMEM(own_s.shape, jnp.float32), pltpu.SemaphoreType.DMA],
-        [qe, fe, de, le, yu, yd, vu, vd, out],
-        aliases={8: 1},
+        [f32(T, L, C, Y), own_s],
+        [pltpu.VMEM((T, L, C, Y), jnp.float32), pltpu.SemaphoreType.DMA((L,))],
+        [qe, fe, de, le, ky, kv, acc],
+        aliases={6: 1},
         hbm_out=1,
     )
     speeds = speeds + other if pair else lax.psum_scatter(speeds, "trc", scatter_dimension=1, tiled=True)
-    return start.reshape(T, L, C, Y), speeds
+    return start, speeds
 
 
 def solution(mesh):

time: 43.6 us -> 42.3 us (0.970)
  Pallas kernels: 19.9 us -> 18.1 us
  waiting for transfers between devices: 12.2 us -> 12.8 us
    pallas_call x12, Pallas kernels: 19.9 us -> 18.1 us  [run(): pl.pallas_call(body, out_shape=outs, in_specs=[pl.BlockSpec(memory_space=...]
    ppermute x10, waiting for transfers between devices: 12.2 us -> 12.8 us  [swap(): received.append(lax.ppermute(x, axis, pairs))]
  transfers between devices with their start and end apart: 10 -> 10, of which waited for: 6 -> 6; matrix products, arithmetic and copies ran while one was open for 0% -> 0% of each run, Pallas kernels for 26% -> 25%
where the time goes in v4:
time: 42.3 us; the launch traced here: 42.2 us
  Pallas kernels  18.1 us (43%)
  waiting for transfers between devices  12.8 us (30%)
  starting transfers between devices  9.85 us (23%)
  between operations  0.8 us (2%)
  other arithmetic  0.63 us (1%)
    pallas_call x12, Pallas kernels, run(): pl.pallas_call(body, out_shape=outs, in_specs=[pl.BlockSpec(memory_space=...  18.1 us
    ppermute x10, waiting for transfers between devices, swap(): received.append(lax.ppermute(x, axis, pairs))  12.8 us
    ppermute x10, starting transfers between devices, swap(): received.append(lax.ppermute(x, axis, pairs))  9.85 us
  transfers between devices with their start and end apart: 10, of which 6 were waited for; matrix products, arithmetic and copies ran while one was open for 0% of the time, Pallas kernels for 25%

profile of v4, /device:TPU:16, one launch (start us, length us, event | category | flops | bytes accessed | tf_op | source)
XLA Modules:
  0.0 42.2 jit_solution(12106088178032505649)
XLA Ops:
  0.6 1.5 %shard_map.95 = (f32[8,80,128]{2,1,0:T(8,128)S(1)}, f32[8,80,128]{2,1,0:T(8,128)S(1)}, f32[1024,128]{1,0:T(8,128)S(1)}, f32[1024,128]{1,0:T(8,128)S(1)}, f32[5,8...) custom-call(f32[1024,128]{1,0:T(8,128)} %bitcast.2, f32[1024,128]{1,0:T(8,128)} %bitcast.3, f32[8,8,128]{2,1,0:T(8,128)} %refs_2_.1, ...), custom_call_target="tpu_custom_call" | custom-call | tf_op jit(solution)/shard_map/pallas_call | solution.py:836
  2.1 1.0 %shard_map.96 = (f32[8,2,16,128]{3,2,1,0:T(8,128)S(1)}, f32[8,2,16,128]{3,2,1,0:T(8,128)S(1)}, f32[7,128,128]{2,1,0:T(8,128)S(1)}, f32[16,16,16,128]{3,2,1,0:T(8...) custom-call(f32[1024,128]{1,0:T(8,128)S(1)} %get-tuple-element.48.refs, ...), custom_call_target="tpu_custom_call" | custom-call | tf_op jit(solution)/shard_map/pallas_call | solution.py:836
  3.2 1.6 %collective-permute-start = (f32[8,80,128]{2,1,0:T(8,128)S(1)}, f32[8,80,128]{2,1,0:T(8,128)S(1)}, u32[]{:S(2)}, u32[]{:S(2)}) collective-permute-start(f32[8,80,128]{2,1,0:T(8,128)S(1)} %get-tuple-element.46), channel_id=1, source_target_pairs={{0,4},{4,0},{8,12},{12,8},{1,5},{5,1},{9,13},{13,9},{2,6},{6,2},{1... | collective-permute-start | bytes 983048 | tf_op jit(solution)/shard_map/ppermute | solution.py:850
  4.8 1.9 %collective-permute-start.1 = (f32[8,80,128]{2,1,0:T(8,128)S(1)}, f32[8,80,128]{2,1,0:T(8,128)S(1)}, u32[]{:S(2)}, u32[]{:S(2)}) collective-permute-start(f32[8,80,128]{2,1,0:T(8,128)S(1)} %get-tuple-element.47), channel_id=1, source_target_pairs={{4,8},{8,4},{5,9},{9,5},{6,10},{10,6},{7,11},{11,7},{20,24},{24,20... | collective-permute-start | bytes 983048 | tf_op jit(solution)/shard_map/ppermute | solution.py:850
  6.8 2.1 %shard_map.97 = (f32[12,12,16,128]{3,2,1,0:T(8,128)S(1)}, f32[8,8,3,16,128]{4,3,2,1,0:T(8,128)S(1)}) custom-call(f32[16,16,16,128]{3,2,1,0:T(8,128)S(1)} %get-tuple-element.53.qe.refs_1_, f32[5,14,14,1,128]{4,3,2,1,0:T(1,128)S(1)} %get-tuple-element.55.fe.refs_3_, f32[3,14,1,128]{3,2,1,0:T(1,128)S(1)} %get-tuple-element.56.de.refs_5_.refs_4_), custom_call_target="tpu_custom_call" | custom-call | tf_op jit(solution)/shard_map/pallas_call | solution.py:836
  8.9 1.6 %shard_map.98 = (f32[16,16,16,128]{3,2,1,0:T(8,128)S(1)}, f32[12,12,16,128]{3,2,1,0:T(8,128)S(1)}, f32[5,14,14,1,128]{4,3,2,1,0:T(1,128)S(1)}, f32[12,12,16,128]{3,2,1,0:T(8,128)S(1)}, f32[10,8,3,16,128]{4,3,2,1,0:T(8,128)S(1)}) custom-call(f32[7,128,128]{2,1,0:T(8,128)S(1)} %collective-permute-d, ...), custom_call_target="tpu_custom_call", output_to_operand_aliasing={{0}: (1, {}), {1}: (2, {}), {2}: (3, {}), {3}: (4, {})} | custom-call | tf_op jit(solution)/shard_map/pallas_call | solution.py:836
  10.5 2.9 %collective-permute-done.refs_0_ = f32[8,80,128]{2,1,0:T(8,128)S(1)} collective-permute-done((f32[8,80,128]{2,1,0:T(8,128)S(1)}, f32[8,80,128]{2,1,0:T(8,128)S(1)}, u32[]{:S(2)}, u32[]{:S(2)}) %collective-permute-start) | collective-permute-done | bytes 327712 | tf_op jit(solution)/shard_map/ppermute | solution.py:850
  13.3 3.2 %collective-permute-done.1.refs_1_ = f32[8,80,128]{2,1,0:T(8,128)S(1)} collective-permute-done((f32[8,80,128]{2,1,0:T(8,128)S(1)}, f32[8,80,128]{2,1,0:T(8,128)S(1)}, u32[]{:S(2)}, u32[]{:S(2)}) %collective-permute-start.1) | collective-permute-done | bytes 327712 | tf_op jit(solution)/shard_map/ppermute | solution.py:850
  16.5 0.1 collective-permute-start.3
  16.7 2.2 %collective-permute-start.5 = (f32[8,2,16,128]{3,2,1,0:T(8,128)S(1)}, f32[8,2,16,128]{3,2,1,0:T(8,128)S(1)}, u32[]{:S(2)}, u32[]{:S(2)}) collective-permute-start(f32[8,2,16,128]{3,2,1,0:T(8,128)S(1)} %get-tuple-element.60), channel_id=1, source_target_pairs={{4,8},{8,4},{5,9},{9,5},{6,10},{10,6},{7,11},{11,7},{20,24},{24,20... | collective-permute-start | bytes 393224 | tf_op jit(solution)/shard_map/ppermute | solution.py:850
  18.9 1.9 %shard_map.100 = (f32[16,16,16,128]{3,2,1,0:T(8,128)S(1)}, f32[5,14,14,1,128]{4,3,2,1,0:T(1,128)S(1)}, f32[3,14,1,128]{3,2,1,0:T(1,128)S(1)}, f32[12,12,16,128]{3,2,1,0:T(8,128)S(1)}, f32[8,8,16,128]{3,2,1,0:T(8,128)S(1)}) custom-call(f32[8,80,128]{2,1,0:T(8,128)S(1)} %collective-permute-done, ...), custom_call_target="tpu_custom_call", output_to_operand_aliasing={{0}: (2, {}), {1}: (3, {}), {2}: (4, {}), {3}: (5, {})} | custom-call | tf_op jit(solution)/shard_map/pallas_call | solution.py:836
  20.8 1.7 %collective-permute-done.4.refs_1_ = f32[8,2,16,128]{3,2,1,0:T(8,128)S(1)} collective-permute-done((f32[8,2,16,128]{3,2,1,0:T(8,128)S(1)}, f32[8,2,16,128]{3,2,1,0:T(8,128)S(1)}, u32[]{:S(2)}, u32[]{:S(2)}) %collective-permute-start.4) | collective-permute-done | bytes 131104 | tf_op jit(solution)/shard_map/ppermute | solution.py:850
  22.5 1.9 %collective-permute-done.5.refs_2_ = f32[8,2,16,128]{3,2,1,0:T(8,128)S(1)} collective-permute-done((f32[8,2,16,128]{3,2,1,0:T(8,128)S(1)}, f32[8,2,16,128]{3,2,1,0:T(8,128)S(1)}, u32[]{:S(2)}, u32[]{:S(2)}) %collective-permute-start.5) | collective-permute-done | bytes 131104 | tf_op jit(solution)/shard_map/ppermute | solution.py:850
  24.4 2.8 %shard_map.101 = (f32[16,16,16,128]{3,2,1,0:T(8,128)S(1)}, f32[12,12,16,128]{3,2,1,0:T(8,128)S(1)}, f32[5,14,14,1,128]{4,3,2,1,0:T(1,128)S(1)}, f32[12,12,16,128...) custom-call(f32[2,2,80,128]{3,2,1,0:T(8,128)S(1)} %collective-permut, ...), custom_call_target="tpu_custom_call", output_to_operand_aliasing={{0}: (4, {}), {1}: (5, {}), {2}: (6, {}), {3}: (7, {})} | custom-call | tf_op jit(solution)/shard_map/pallas_call | solution.py:836
  27.1 2.1 %shard_map.102 = (f32[8,8,16,128]{3,2,1,0:T(8,128)S(1)}, f32[3,8,8,128]{3,2,1,0:T(8,128)S(1)}, f32[2,8,16,128]{3,2,1,0:T(8,128)S(1)}) custom-call(f32[12,12,16,128]{3,2,1,0:T(8,128)S(1)} %get-tuple-element.73.refs_0_, f32[5,14,14,1,128]{4,3,2,1,0:T(1,128)S(1)} %get-tuple-element.69.refs_1_.refs_0_, ...), custom_call_target="tpu_custom_call", output_to_operand_aliasing={{0}: (4, {}), {1}: (5, {})} | custom-call | tf_op jit(solution)/shard_map/pallas_call | solution.py:836
  29.4 2.2 %collective-permute-start.8 = (f32[8,2,16,128]{3,2,1,0:T(8,128)S(1)}, f32[8,2,16,128]{3,2,1,0:T(8,128)S(1)}, u32[]{:S(2)}, u32[]{:S(2)}) collective-permute-start(f32[8,2,16,128]{3,2,1,0:T(8,128)S(1)} %get-tuple-element.83), channel_id=1, source_target_pairs={{4,8},{8,4},{5,9},{9,5},{6,10},{10,6},{7,11},{11,7},{20,24},{24,20... | collective-permute-start | bytes 393224 | tf_op jit(solution)/shard_map/ppermute | solution.py:850
  31.6 1.4 %shard_map.103 = (f32[12,12,16,128]{3,2,1,0:T(8,128)S(1)}, f32[8,8,16,128]{3,2,1,0:T(8,128)S(1)}) custom-call(f32[16,16,16,128]{3,2,1,0:T(8,128)S(1)} %get-tuple-element.68.refs_0_, f32[5,14,14,1,128]{4,3,2,1,0:T(1,128)S(1)} %get-tuple-element.69.refs_1_.refs_0_, f32[3,14,1,128]{3,2,1,0:T(1,128)S(1)} %get-tuple-element.63.refs_3_.refs_2_.refs_1_, ...), custom_call_target="tpu_custom_call" | custom-call | tf_op jit(solution)/shard_map/pallas_call | solution.py:836
  33.0 0.9 %shard_map.104 = (f32[12,12,16,128]{3,2,1,0:T(8,128)S(1)}, f32[3,8,8,128]{3,2,1,0:T(8,128)S(1)}) custom-call(f32[5,14,14,1,128]{4,3,2,1,0:T(1,128)S(1)} %get-tuple-element.69.refs_1_.refs_0_, f32[3,14,1,128]{3,2,1,0:T(1,128)S(1)} %get-tuple-element.63.refs_3_.refs_2_.refs_1_, ...), custom_call_target="tpu_custom_call", output_to_operand_aliasing={{0}: (7, {})} | custom-call | tf_op jit(solution)/shard_map/pallas_call | solution.py:836
  33.9 1.4 %collective-permute-done.7.refs_4_ = f32[8,2,16,128]{3,2,1,0:T(8,128)S(1)} collective-permute-done((f32[8,2,16,128]{3,2,1,0:T(8,128)S(1)}, f32[8,2,16,128]{3,2,1,0:T(8,128)S(1)}, u32[]{:S(2)}, u32[]{:S(2)}) %collective-permute-start.7) | collective-permute-done | bytes 131104 | tf_op jit(solution)/shard_map/ppermute | solution.py:850
  35.2 1.9 %collective-permute-done.8.refs_5_ = f32[8,2,16,128]{3,2,1,0:T(8,128)S(1)} collective-permute-done((f32[8,2,16,128]{3,2,1,0:T(8,128)S(1)}, f32[8,2,16,128]{3,2,1,0:T(8,128)S(1)}, u32[]{:S(2)}, u32[]{:S(2)}) %collective-permute-start.8) | collective-permute-done | bytes 131104 | tf_op jit(solution)/shard_map/ppermute | solution.py:850
  37.1 0.1 shard_map.105
  37.2 1.6 %collective-permute-start.9 = (f32[3,4,8,128]{3,2,1,0:T(8,128)S(1)}, f32[3,4,8,128]{3,2,1,0:T(8,128)S(1)}, u32[]{:S(2)}, u32[]{:S(2)}) collective-permute-start(f32[3,4,8,128]{3,2,1,0:T(8,128)S(1)} %get-tuple-element.89), channel_id=1, source_target_pairs={{0,2},{2,0},{1,3},{3,1},{4,6},{6,4},{5,7},{7,5},{8,10},{10,8},{9,1... | collective-permute-start | bytes 147464 | tf_op jit(solution)/shard_map/ppermute | solution.py:850
  38.8 2.7 %shard_map.106 = (f32[16,8,8,128]{3,2,1,0:T(8,128)}, f32[8,8,16,128]{3,2,1,0:T(8,128)S(1)}) custom-call(f32[16,16,16,128]{3,2,1,0:T(8,128)S(1)} %get-tuple-element.68.refs_0_, f32[5,14,14,1,128]{4,3,2,1,0:T(1,128)S(1)} %get-tuple-element.69.refs_1_.refs_0_, ...), custom_call_target="tpu_custom_call", output_to_operand_aliasing={{1}: (6, {})} | custom-call | tf_op jit(solution)/shard_map/pallas_call | solution.py:836
  41.5 0.6 %add.3 = f32[3,4,8,128]{3,2,1,0:T(8,128)} add(f32[3,4,8,128]{3,2,1,0:T(8,128)S(1)} %get-tuple-element.88, f32[3,4,8,128]{3,2,1,0:T(8,128)S(1)} %collective-permute-done.9) | non-fusion elementwise | flops 12288 | bytes 147456 | tf_op jit(solution)/shard_map/add | solution.py:955
  (9 shorter events, 0.3 us)
Async XLA Ops:
  3.1 5.7 %collective-permute-start.2 = (f32[7,128,128]{2,1,0:T(8,128)S(1)}, f32[7,128,128]{2,1,0:T(8,128)S(1)}, u32[]{:S(2)}, u32[]{:S(2)}) collective-permute-start(f32[7,128,128]{2,1,0:T(8,128)S(1)} %get-tuple-element.52), channel_id=1, source_target_pairs={{0,1},{1,0},{2,3},{3,2},{4,5},{5,4},{6,7},{7,6},{8,9},{9,8},{10,11... | collective-permute-start | bytes 1376264 | tf_op jit(solution)/shard_map/ppermute | solution.py:850
  3.2 10.1 %collective-permute-start = (f32[8,80,128]{2,1,0:T(8,128)S(1)}, f32[8,80,128]{2,1,0:T(8,128)S(1)}, u32[]{:S(2)}, u32[]{:S(2)}) collective-permute-start(f32[8,80,128]{2,1,0:T(8,128)S(1)} %get-tuple-element.46), channel_id=1, source_target_pairs={{0,4},{4,0},{8,12},{12,8},{1,5},{5,1},{9,13},{13,9},{2,6},{6,2},{1... | collective-permute-start | bytes 983048 | tf_op jit(solution)/shard_map/ppermute | solution.py:850
  4.8 11.6 %collective-permute-start.1 = (f32[8,80,128]{2,1,0:T(8,128)S(1)}, f32[8,80,128]{2,1,0:T(8,128)S(1)}, u32[]{:S(2)}, u32[]{:S(2)}) collective-permute-start(f32[8,80,128]{2,1,0:T(8,128)S(1)} %get-tuple-element.47), channel_id=1, source_target_pairs={{4,8},{8,4},{5,9},{9,5},{6,10},{10,6},{7,11},{11,7},{20,24},{24,20... | collective-permute-start | bytes 983048 | tf_op jit(solution)/shard_map/ppermute | solution.py:850
  16.5 7.9 %collective-permute-start.3 = (f32[2,2,80,128]{3,2,1,0:T(8,128)S(1)}, f32[2,2,80,128]{3,2,1,0:T(8,128)S(1)}, u32[]{:S(2)}, u32[]{:S(2)}) collective-permute-start(f32[2,2,80,128]{3,2,1,0:T(8,128)S(1)} %shard_map.99), channel_id=1, source_target_pairs={{0,1},{1,0},{2,3},{3,2},{4,5},{5,4},{6,7},{7,6},{8,9},{9,8},{10,11... | collective-permute-start | bytes 491528 | tf_op jit(solution)/shard_map/ppermute | solution.py:850
  16.6 5.9 %collective-permute-start.4 = (f32[8,2,16,128]{3,2,1,0:T(8,128)S(1)}, f32[8,2,16,128]{3,2,1,0:T(8,128)S(1)}, u32[]{:S(2)}, u32[]{:S(2)}) collective-permute-start(f32[8,2,16,128]{3,2,1,0:T(8,128)S(1)} %get-tuple-element.59), channel_id=1, source_target_pairs={{0,4},{4,0},{8,12},{12,8},{1,5},{5,1},{9,13},{13,9},{2,6},{6,2},{1... | collective-permute-start | bytes 393224 | tf_op jit(solution)/shard_map/ppermute | solution.py:850
  16.7 7.7 %collective-permute-start.5 = (f32[8,2,16,128]{3,2,1,0:T(8,128)S(1)}, f32[8,2,16,128]{3,2,1,0:T(8,128)S(1)}, u32[]{:S(2)}, u32[]{:S(2)}) collective-permute-start(f32[8,2,16,128]{3,2,1,0:T(8,128)S(1)} %get-tuple-element.60), channel_id=1, source_target_pairs={{4,8},{8,4},{5,9},{9,5},{6,10},{10,6},{7,11},{11,7},{20,24},{24,20... | collective-permute-start | bytes 393224 | tf_op jit(solution)/shard_map/ppermute | solution.py:850
  29.3 3.7 %collective-permute-start.6 = (f32[2,8,16,128]{3,2,1,0:T(8,128)S(1)}, f32[2,8,16,128]{3,2,1,0:T(8,128)S(1)}, u32[]{:S(2)}, u32[]{:S(2)}) collective-permute-start(f32[2,8,16,128]{3,2,1,0:T(8,128)S(1)} %get-tuple-element.78), channel_id=1, source_target_pairs={{0,1},{1,0},{2,3},{3,2},{4,5},{5,4},{6,7},{7,6},{8,9},{9,8},{10,11... | collective-permute-start | bytes 393224 | tf_op jit(solution)/shard_map/ppermute | solution.py:850
  29.3 5.9 %collective-permute-start.7 = (f32[8,2,16,128]{3,2,1,0:T(8,128)S(1)}, f32[8,2,16,128]{3,2,1,0:T(8,128)S(1)}, u32[]{:S(2)}, u32[]{:S(2)}) collective-permute-start(f32[8,2,16,128]{3,2,1,0:T(8,128)S(1)} %get-tuple-element.82), channel_id=1, source_target_pairs={{0,4},{4,0},{8,12},{12,8},{1,5},{5,1},{9,13},{13,9},{2,6},{6,2},{1... | collective-permute-start | bytes 393224 | tf_op jit(solution)/shard_map/ppermute | solution.py:850
  29.4 7.7 %collective-permute-start.8 = (f32[8,2,16,128]{3,2,1,0:T(8,128)S(1)}, f32[8,2,16,128]{3,2,1,0:T(8,128)S(1)}, u32[]{:S(2)}, u32[]{:S(2)}) collective-permute-start(f32[8,2,16,128]{3,2,1,0:T(8,128)S(1)} %get-tuple-element.83), channel_id=1, source_target_pairs={{4,8},{8,4},{5,9},{9,5},{6,10},{10,6},{7,11},{11,7},{20,24},{24,20... | collective-permute-start | bytes 393224 | tf_op jit(solution)/shard_map/ppermute | solution.py:850
  37.2 4.3 %collective-permute-start.9 = (f32[3,4,8,128]{3,2,1,0:T(8,128)S(1)}, f32[3,4,8,128]{3,2,1,0:T(8,128)S(1)}, u32[]{:S(2)}, u32[]{:S(2)}) collective-permute-start(f32[3,4,8,128]{3,2,1,0:T(8,128)S(1)} %get-tuple-element.89), channel_id=1, source_target_pairs={{0,2},{2,0},{1,3},{3,1},{4,6},{6,4},{5,7},{7,5},{8,10},{10,8},{9,1... | collective-permute-start | bytes 147464 | tf_op jit(solution)/shard_map/ppermute | solution.py:850
